TPU v7x, 512 devices: a whole 4x8x8 slice. The times are simulated.
512 devices in a mesh: row: 32 (over z, x), col: 16 (over y, core).
Axes of the slice: x: 4, y: 8, z: 8, core: 2. Of those that a mesh axis runs over, the one named last changes fastest.
Arguments:
- incoming_hidden: bfloat16 [16384, 2048], P('row', 'col'), may hold values from -6 to 6
- input_norm_weight: bfloat16 [1, 2048], P(None, 'col'), may hold values from 0.5 to 1.5
- query_key_value_weight: bfloat16 [3, 2048, 2048], P(None, 'row', 'col'), may hold values from -0.125 to 0.125
- query_key_value_bias: bfloat16 [3, 2048], P(None, 'col'), may hold values from -27 to 27
- output_weight: bfloat16 [2048, 2048], P('col', 'row'), may hold values from -0.125 to 0.125
- adapter_down_weight: bfloat16 [16, 2, 16, 2048], P('col'), may hold values from -0.125 to 0.125
- adapter_up_weight: bfloat16 [16, 2, 16, 2048], P(None, None, None, 'col'), may hold values from -1.5 to 1.5
- slot_of_adapter: int32 [16], replicated, may hold values from 0 to 15, each once
- adapter_of_prompt: int32 [32, 4], P('row'), may hold values from 0 to 15
- prompt_length_list: int32 [32, 4], P('row'), may hold values from 1 to 256, 512 in all within a row
- cache_page_index: int32 [32, 32], P('row'), may hold values from 0 to 31, each once within a row
Outputs:
- attn_out: bfloat16 [16384, 2048], P(('row', 'col'))
- kv_pages: bfloat16 [1024, 2, 16, 2048], P('row', None, None, 'col')
All inputs are finite; a program needn't handle non-finite values.
Results may differ from a plain program's by a relative error of at most 0.023.
Values may be sent and summed in bfloat16 or wider, within the bound.
No kernel may reach another device: no remote copies, remote signals or barrier semaphores. Data moves between devices by JAX's collectives and lax.ppermute only.
A program may use at most 64 MiB of HBM per device.

v0:
```python
import jax
import jax.numpy as jnp
from jax import lax
from jax.sharding import PartitionSpec as P

HEAD_DIM = 128
PAGE = 16


rope_base = 1000000.0
norm_eps = 1e-06
adapter_scale = 2.0


def layout(lengths, total_rows):
    places = jnp.arange(total_rows, dtype=jnp.int32)
    prompt_end = jnp.cumsum(lengths)
    prompt_start = prompt_end - lengths
    inside = (places[:, None] >= prompt_start[None, :]) & (places[:, None] < prompt_end[None, :])
    numbers = jnp.arange(lengths.shape[0], dtype=jnp.int32)
    segment = jnp.sum(jnp.where(inside, numbers[None, :], 0), axis=1)
    position = places - jnp.sum(jnp.where(inside, prompt_start[None, :], 0), axis=1)
    return (segment, position, inside)


def rotary(vectors, position):
    half_dim = vectors.shape[-1] // 2
    inverse_freq = rope_base ** (
        -(jnp.arange(half_dim, dtype=jnp.float32) * 2.0 / vectors.shape[-1])
    )
    angles = position.astype(jnp.float32)[:, None] * inverse_freq[None, :]
    cosine = jnp.cos(angles)[:, None, :]
    sine_part = jnp.sin(angles)[:, None, :]
    first_half = vectors[..., :half_dim]
    second_half = vectors[..., half_dim:]
    return jnp.concatenate(
        [
            first_half * cosine - second_half * sine_part,
            second_half * cosine + first_half * sine_part,
        ],
        axis=-1,
    )


def attend(queries_rot, keys_rot, values_rot, segment):
    total_rows = queries_rot.shape[0]
    block_rows = min(512, total_rows)
    blocks = total_rows // block_rows
    factor = queries_rot.shape[-1] ** (-0.5)
    key_index = jnp.arange(total_rows, dtype=jnp.int32)

    def one_block(index):
        start = index * block_rows
        query_index = start + jnp.arange(block_rows, dtype=jnp.int32)
        scores = (
            jnp.einsum("qhd,khd->hqk", queries_rot, keys_rot, preferred_element_type=jnp.float32)
            * factor
        )
        allowed = (segment[:, None] == segment[None, :]) & (
            key_index[None, :] <= query_index[:, None]
        )
        scores = jnp.where(allowed[None], scores, -1e30)
        highest = jnp.max(scores, axis=-1, keepdims=True)
        exps = jnp.exp(scores - highest)
        probs = (exps / jnp.sum(exps, axis=-1, keepdims=True)).astype(jnp.bfloat16)
        return jnp.einsum(
            "hqk,khd->qhd", probs, values_rot, preferred_element_type=jnp.float32
        ).astype(jnp.bfloat16)

    outputs = lax.map(one_block, jnp.arange(blocks, dtype=jnp.int32))
    return outputs.reshape(total_rows, -1)


def body(
    incoming_hidden,
    input_norm_weight,
    query_key_value_weight,
    query_key_value_bias,
    output_weight,
    adapter_down_weight,
    adapter_up_weight,
    slot_of_adapter,
    adapter_of_prompt,
    prompt_length_list,
    cache_page_index,
):
    gathered, gain_full = (
        lax.all_gather(incoming_hidden, "col", axis=1, tiled=True),
        lax.all_gather(input_norm_weight, "col", axis=1, tiled=True),
    )
    widened = gathered.astype(jnp.float32)
    power = jnp.mean(widened * widened, axis=1, keepdims=True)
    normed = (widened * lax.rsqrt(power + norm_eps) * gain_full.astype(jnp.float32)).astype(
        jnp.bfloat16
    )
    total_rows = normed.shape[0]
    head_column_count = query_key_value_weight.shape[2]
    heads_here = head_column_count // HEAD_DIM
    segment, position, inside = layout(prompt_length_list[0], total_rows)
    slot_prompt = slot_of_adapter[adapter_of_prompt[0]]
    slot_token = jnp.sum(jnp.where(inside, slot_prompt[None, :], 0), axis=1)
    projected_rows = jnp.einsum(
        "td,kdh->kth",
        normed,
        lax.all_gather(query_key_value_weight, "row", axis=1, tiled=True),
        preferred_element_type=jnp.float32,
    )
    projected_rows = projected_rows + query_key_value_bias.astype(jnp.float32)[:, None, :]
    every_slot = adapter_up_weight.shape[0]
    adapter_rank_size = adapter_up_weight.shape[2]
    adapter_factors = lax.all_gather(adapter_down_weight, "col", axis=0, tiled=True)
    flat_all = adapter_factors.reshape(-1, adapter_factors.shape[3])
    lowrank = lax.dot_general(
        normed, flat_all, (((1,), (1,)), ((), ())), preferred_element_type=jnp.float32
    ).astype(jnp.bfloat16)
    lowrank = lowrank.reshape(total_rows, every_slot, 2, adapter_rank_size)
    chosen = slot_token[:, None] == jnp.arange(every_slot, dtype=jnp.int32)[None, :]
    picked = jnp.where(chosen[:, :, None, None], lowrank, jnp.zeros_like(lowrank))
    query_update = jnp.dot(
        picked[:, :, 0, :].reshape(total_rows, -1),
        adapter_up_weight[:, 0].reshape(-1, head_column_count),
        preferred_element_type=jnp.float32,
    )
    value_update = jnp.dot(
        picked[:, :, 1, :].reshape(total_rows, -1),
        adapter_up_weight[:, 1].reshape(-1, head_column_count),
        preferred_element_type=jnp.float32,
    )
    query_rows = projected_rows[0] + adapter_scale * query_update
    value_rows = projected_rows[2] + adapter_scale * value_update
    queries_rot = rotary(query_rows.reshape(total_rows, heads_here, HEAD_DIM), position).astype(
        jnp.bfloat16
    )
    keys_rot = rotary(projected_rows[1].reshape(total_rows, heads_here, HEAD_DIM), position).astype(
        jnp.bfloat16
    )
    values_rot = value_rows.astype(jnp.bfloat16).reshape(total_rows, heads_here, HEAD_DIM)
    pages_here = total_rows // PAGE
    stacked = jnp.stack(
        [
            keys_rot.reshape(pages_here, PAGE, head_column_count),
            values_rot.reshape(pages_here, PAGE, head_column_count),
        ],
        axis=1,
    )
    cache = jnp.zeros_like(stacked).at[cache_page_index[0]].set(stacked)
    attended = attend(queries_rot, keys_rot, values_rot, segment)
    wo_rows = lax.all_gather(output_weight, "row", axis=1, tiled=True)
    summed = lax.psum_scatter(
        jnp.dot(attended, wo_rows, preferred_element_type=jnp.float32).astype(jnp.bfloat16),
        "col",
        scatter_dimension=0,
        tiled=True,
    )
    return (summed, cache)


def solution(mesh):
    in_specs = (
        P("row", "col"),
        P(None, "col"),
        P(None, "row", "col"),
        P(None, "col"),
        P("col", "row"),
        P("col", None, None, None),
        P(None, None, None, "col"),
        P(),
        P("row", None),
        P("row", None),
        P("row", None),
    )
    out_specs = (P(("row", "col"), None), P("row", None, None, "col"))
    return jax.shard_map(body, mesh=mesh, in_specs=in_specs, out_specs=out_specs, check_vma=False)
```

profile of v0, /device:TPU:1, one launch (start us, length us, event | category | flops | bytes accessed | tf_op | source)
XLA Modules:
  0.0 258.3 jit_solution(8952180835351165998)
XLA Ops:
  7.2 0.7 all-gather.4.cloned.1.call-update
  8.0 0.7 all-gather.6.cloned.1.call-update
  8.7 0.7 all-gather.8.cloned.1.call-update
  9.4 20.9 %all_gather.16 = bf16[1,2048]{1,0:T(2,128)(2,1)S(1)} all-gather(bf16[1,128]{1,0:T(2,128)(2,1)} %param.12), channel_id=1, replica_groups=mesh['row'=32,'col'=16] {'col'}, dimensions={1}, use_global_device_ids=true | all-gather | bytes 4352 | tf_op jit(solution)/shard_map/all_gather | solution.py:89
  30.4 0.7 convert_element_type.59
  31.1 0.8 reduce-window.4
  31.9 0.7 fusion.56
  32.6 0.6 gather_fusion
  33.2 0.7 fusion.58
  34.0 47.5 %all_gather.19 = bf16[128,2048]{0,1:T(8,128)(2,1)} all-gather(bf16[128,64]{0,1:T(8,128)(2,1)} %param.15), channel_id=1, replica_groups=mesh['row'=32,'col'=16] {'row'}, dimensions={1}, use_global_device_ids=true | all-gather | bytes 540672 | tf_op jit(solution)/shard_map/all_gather | solution.py:148
  81.6 2.2 fusion
  83.8 57.4 %all-gather.6.cloned.1.call-done = bf16[3,2048,128]{2,1,0:T(8,128)(2,1)} async-done(((bf16[3,64,128]{2,1,0:T(8,128)(2,1)}), bf16[3,2048,128]{2,1,0:T(8,128)(2,1)}) %all-gather.6.cloned.1.call-update) | async-done | bytes 1572880 | tf_op jit(solution)/shard_map/all_gather | solution.py:105
  141.1 2.6 fusion.9
  143.7 42.5 %all-gather.8.cloned.1.call-done = bf16[16,2,16,2048]{3,2,1,0:T(8,128)(2,1)} async-done(((bf16[1,2,16,2048]{3,2,1,0:T(8,128)(2,1)}), bf16[16,2,16,2048]{3,2,1,0:T(8,128)(2,1)}) %all-gather.8.cloned.1.call-update) | async-done | bytes 2097168 | tf_op jit(solution)/shard_map/all_gather | solution.py:111
  186.3 3.0 %convolution_convert_fusion.1 = bf16[512,512]{0,1:T(8,128)(2,1)S(1)} fusion(bf16[512,2048]{1,0:T(8,128)(2,1)} %bitcast.103, bf16[512,2048]{1,0:T(8,128)(2,1)S(1)} %copy-done.1, f32[2048]{0:T(1024)S(1)} %bitcast.101, f32[512]{0:T(512)S(1)} %add_rsqrt_fusion), kind=kOutput, calls=%fused_computation.12 | convolution fusion | flops 1078198272 | bytes 4728832 | tf_op jit(solution)/shard_map/dot_general | solution.py:113
  189.4 0.2 fusion.16
  189.6 0.2 fusion.17
  189.8 0.6 fusion.40
  190.4 0.4 fusion.60
  190.9 0.2 fusion.20
  191.1 2.4 convolution_convert_fusion
  193.5 0.6 copy-done.5
  194.7 1.5 scatter_fusion
  196.2 55.5 %reduce-scatter.2.cloned.1.call-done = bf16[32,2048]{1,0:T(8,128)(2,1)} async-done(((bf16[512,2048]{1,0:T(8,128)(2,1)}), bf16[32,2048]{1,0:T(8,128)(2,1)}) %reduce-scatter.2.cloned.1.call-update) | async-done | bytes 131088 | tf_op jit(solution)/shard_map/reduce_scatter | solution.py:149
  (33 shorter events, 1.0 us)
Async XLA Ops:
  7.2 25.4 %copy-start = (s32[16]{0:T(128)S(1)}, s32[16]{0:T(128)}, u32[]{:S(2)}) copy-start(s32[16]{0:T(128)} %param.18) | copy-start | bytes 196
  7.2 74.4 %all-gather.4.cloned.1.call-start = ((), (), s32[]{:S(2)}) async-start(), calls=%async_computation.1 | async-start | bytes 2228224 | tf_op jit(solution)/shard_map/all_gather | solution.py:88
  7.9 133.2 %all-gather.6.cloned.1.call-start = ((), (), s32[]{:S(2)}) async-start(), calls=%async_computation.2 | async-start | bytes 1622016 | tf_op jit(solution)/shard_map/all_gather | solution.py:105
  8.7 177.6 %all-gather.8.cloned.1.call-start = ((), (), s32[]{:S(2)}) async-start(), calls=%async_computation.3 | async-start | bytes 2228224 | tf_op jit(solution)/shard_map/all_gather | solution.py:111
  9.4 242.4 %reduce-scatter.2.cloned.1.call-start = ((), (), s32[]{:S(2)}) async-start(), calls=%async_computation.4 | async-start | bytes 2228224 | tf_op jit(solution)/shard_map/reduce_scatter | solution.py:149
  81.5 59.6 %copy-start.1 = (bf16[512,2048]{1,0:T(8,128)(2,1)S(1)}, bf16[512,2048]{1,0:T(8,128)(2,1)}, u32[]{:S(2)}) copy-start(bf16[512,2048]{1,0:T(8,128)(2,1)} %all-gather.4.cloned.1.call-done) | copy-start | bytes 6291460
  186.3 3.1 %copy-start.4 = (bf16[16,2,16,128]{3,2,1,0:T(8,128)(2,1)S(1)}, bf16[16,2,16,128]{3,2,1,0:T(8,128)(2,1)}, u32[]{:S(2)}) copy-start(bf16[16,2,16,128]{3,2,1,0:T(8,128)(2,1)} %param.17) | copy-start | bytes 393220
  189.8 1.2 copy-start.3
  193.4 0.7 copy-start.5
  196.2 55.6 %copy-start.2 = (bf16[32,2,16,128]{3,2,1,0:T(8,128)(2,1)}, bf16[32,2,16,128]{3,2,1,0:T(8,128)(2,1)S(1)}, u32[]{:S(2)}) copy-start(bf16[32,2,16,128]{3,2,1,0:T(8,128)(2,1)S(1)} %scatter_fusion) | copy-start | bytes 786436
Sparse Core Ops, SparseCore 0:
  10.1 49.2 all-gather.3
  62.5 78.5 all-gather.5
  143.3 42.9 all-gather.7
  193.6 58.1 reduce-scatter.1
where the time goes:
time: 260 us; the launch traced here: 258 us
  waiting for transfers between devices  158 us (61%)
  blocking collectives  68.4 us (26%)
  between operations  13.9 us (5%)
  matrix products  8.79 us (3%)
  other arithmetic  6.18 us (2%)
  local copies, waits for them, and re-layouts  3.27 us (1%)
    all_gather x1, waiting for transfers between devices, body(): lax.all_gather(query_key_value_weight, 'row', axis=1, tiled=True)  57.4 us
    reduce_scatter x1, waiting for transfers between devices, body(): lax.psum_scatter(jnp.dot(attended, wo_rows, preferred_element_type=jnp.fl...  55.5 us
    all_gather x1, blocking collectives, body(): wo_rows = lax.all_gather(output_weight, 'row', axis=1, tiled=True)  47.5 us
    all_gather x1, waiting for transfers between devices, body(): lax.all_gather(adapter_down_weight, 'col', axis=0, tiled=True)  42.5 us
    all_gather x1, blocking collectives, body(): lax.all_gather(input_norm_weight, 'col', axis=1, tiled=True)  20.9 us
  transfers between devices with their start and end apart: 4, of which 3 were waited for; matrix products, arithmetic and copies ran while one was open for 4% of the time, Pallas kernels for 0%

commit v1 on v0

v1 whole, which is shorter than its diff:
```python
import jax
import jax.numpy as jnp
from jax import lax
from jax.sharding import PartitionSpec as P

HEAD_DIM = 128
PAGE = 16
GAIN_ROWS = 16
X_SIZE = 4

rope_base = 1000000.0
norm_eps = 1e-06
adapter_scale = 2.0


def layout(lengths, total_rows):
    places = jnp.arange(total_rows, dtype=jnp.int32)
    prompt_end = jnp.cumsum(lengths)
    prompt_start = prompt_end - lengths
    inside = (places[:, None] >= prompt_start[None, :]) & (places[:, None] < prompt_end[None, :])
    numbers = jnp.arange(lengths.shape[0], dtype=jnp.int32)
    segment = jnp.sum(jnp.where(inside, numbers[None, :], 0), axis=1)
    position = places - jnp.sum(jnp.where(inside, prompt_start[None, :], 0), axis=1)
    return (segment, position, inside)


def rotary(vectors, position):
    half_dim = vectors.shape[-1] // 2
    inverse_freq = rope_base ** (
        -(jnp.arange(half_dim, dtype=jnp.float32) * 2.0 / vectors.shape[-1])
    )
    angles = position.astype(jnp.float32)[:, None] * inverse_freq[None, :]
    cosine = jnp.cos(angles)
    sine_part = jnp.sin(angles)
    first_half = vectors[..., :half_dim]
    second_half = vectors[..., half_dim:]
    return jnp.concatenate(
        [
            first_half * cosine - second_half * sine_part,
            second_half * cosine + first_half * sine_part,
        ],
        axis=-1,
    )


def attend(queries_rot, keys_rot, values_rot, segment):
    total_rows = queries_rot.shape[0]
    factor = queries_rot.shape[-1] ** (-0.5)
    index = jnp.arange(total_rows, dtype=jnp.int32)
    scores = jnp.einsum("qd,kd->qk", queries_rot, keys_rot, preferred_element_type=jnp.float32)
    scores = scores * factor
    allowed = (segment[:, None] == segment[None, :]) & (index[None, :] <= index[:, None])
    scores = jnp.where(allowed, scores, -1e30)
    highest = jnp.max(scores, axis=-1, keepdims=True)
    exps = jnp.exp(scores - highest)
    probs = (exps / jnp.sum(exps, axis=-1, keepdims=True)).astype(jnp.bfloat16)
    return jnp.dot(probs, values_rot, preferred_element_type=jnp.float32).astype(jnp.bfloat16)


def copies(block, count):
    return jnp.broadcast_to(block[None], (count,) + block.shape)


def make_body(n_row, n_col):
    n_z = n_row // X_SIZE
    x_groups = [[z * X_SIZE + x for x in range(X_SIZE)] for z in range(n_z)]
    z_groups = [[z * X_SIZE + x for z in range(n_z)] for x in range(X_SIZE)]
    pair_groups = [[i, i + 1] for i in range(0, n_col, 2)]
    y_groups = [list(range(core, n_col, 2)) for core in range(2)]

    def body(
        incoming_hidden,
        input_norm_weight,
        query_key_value_weight,
        query_key_value_bias,
        output_weight,
        adapter_down_weight,
        adapter_up_weight,
        slot_of_adapter,
        adapter_of_prompt,
        prompt_length_list,
        cache_page_index,
    ):
        total_rows, feature_part = incoming_hidden.shape
        rank2 = adapter_down_weight.shape[1] * adapter_down_weight.shape[2]
        width = adapter_down_weight.shape[3]
        row_part = query_key_value_weight.shape[1]
        head_cols = query_key_value_weight.shape[2]
        rank = adapter_down_weight.shape[2]
        down_block = (
            adapter_down_weight.reshape(rank2, n_col, feature_part)
            .transpose(1, 0, 2)
            .reshape(n_col * rank2, feature_part)
        )
        payload = jnp.concatenate(
            [
                incoming_hidden,
                down_block,
                jnp.broadcast_to(input_norm_weight, (GAIN_ROWS, feature_part)),
            ],
            axis=0,
        )
        gathered = lax.all_gather(payload, "col", axis=0, tiled=False)
        weight_block = jnp.concatenate(
            [query_key_value_weight[i] for i in range(3)] + [output_weight.T], axis=1
        )
        over_z = lax.all_to_all(
            copies(weight_block, n_z), "row", 0, 0, tiled=False, axis_index_groups=z_groups
        )
        over_x = lax.all_to_all(
            copies(over_z, X_SIZE), "row", 0, 0, tiled=False, axis_index_groups=x_groups
        )
        weights = over_x.transpose(1, 0, 2, 3).reshape(n_row * row_part, 4 * head_cols)

        gathered_hidden = (
            gathered[:, :total_rows].transpose(1, 0, 2).reshape(total_rows, width)
        )
        down_full = (
            gathered[:, total_rows : total_rows + n_col * rank2]
            .reshape(n_col, n_col, rank2, feature_part)
            .transpose(0, 2, 1, 3)
            .reshape(n_col * rank2, width)
        )
        gain_full = gathered[:, total_rows + n_col * rank2].reshape(1, width)

        widened = gathered_hidden.astype(jnp.float32)
        power = jnp.mean(widened * widened, axis=1, keepdims=True)
        normed = (widened * lax.rsqrt(power + norm_eps) * gain_full.astype(jnp.float32)).astype(
            jnp.bfloat16
        )
        segment, position, inside = layout(prompt_length_list[0], total_rows)
        slot_prompt = slot_of_adapter[adapter_of_prompt[0]]
        slot_token = jnp.sum(jnp.where(inside, slot_prompt[None, :], 0), axis=1)
        projected = jnp.dot(
            normed, weights[:, : 3 * head_cols], preferred_element_type=jnp.float32
        )
        projected = projected + query_key_value_bias.astype(jnp.float32).reshape(1, 3 * head_cols)
        lowrank = lax.dot_general(
            normed, down_full, (((1,), (1,)), ((), ())), preferred_element_type=jnp.float32
        ).astype(jnp.bfloat16)
        every_slot = adapter_up_weight.shape[0]
        lowrank = lowrank.reshape(total_rows, every_slot, 2, rank)
        chosen = slot_token[:, None] == jnp.arange(every_slot, dtype=jnp.int32)[None, :]
        picked = jnp.where(chosen[:, :, None, None], lowrank, jnp.zeros_like(lowrank))
        query_update = jnp.dot(
            picked[:, :, 0, :].reshape(total_rows, -1),
            adapter_up_weight[:, 0].reshape(-1, head_cols),
            preferred_element_type=jnp.float32,
        )
        value_update = jnp.dot(
            picked[:, :, 1, :].reshape(total_rows, -1),
            adapter_up_weight[:, 1].reshape(-1, head_cols),
            preferred_element_type=jnp.float32,
        )
        query_rows = projected[:, :head_cols] + adapter_scale * query_update
        key_rows = projected[:, head_cols : 2 * head_cols]
        value_rows = projected[:, 2 * head_cols :] + adapter_scale * value_update
        queries_rot = rotary(query_rows, position).astype(jnp.bfloat16)
        keys_rot = rotary(key_rows, position).astype(jnp.bfloat16)
        values_rot = value_rows.astype(jnp.bfloat16)
        pages_here = total_rows // PAGE
        stacked = jnp.stack(
            [
                keys_rot.reshape(pages_here, PAGE, head_cols),
                values_rot.reshape(pages_here, PAGE, head_cols),
            ],
            axis=1,
        )
        cache = jnp.zeros_like(stacked).at[cache_page_index[0]].set(stacked)
        attended = attend(queries_rot, keys_rot, values_rot, segment)
        partial = lax.dot_general(
            attended,
            weights[:, 3 * head_cols :],
            (((1,), (1,)), ((), ())),
            preferred_element_type=jnp.float32,
        ).astype(jnp.bfloat16)
        out_rows = total_rows // n_col
        by_core = partial.reshape(n_col // 2, 2, out_rows, width).transpose(1, 0, 2, 3)
        pair = lax.all_to_all(by_core, "col", 0, 0, tiled=False, axis_index_groups=pair_groups)
        pair_sum = (pair[0].astype(jnp.float32) + pair[1].astype(jnp.float32)).astype(jnp.bfloat16)
        terms = lax.all_to_all(pair_sum, "col", 0, 0, tiled=False, axis_index_groups=y_groups)
        summed = jnp.sum(terms.astype(jnp.float32), axis=0).astype(jnp.bfloat16)
        return (summed, cache)

    return body


def solution(mesh):
    in_specs = (
        P("row", "col"),
        P(None, "col"),
        P(None, "row", "col"),
        P(None, "col"),
        P("col", "row"),
        P("col", None, None, None),
        P(None, None, None, "col"),
        P(),
        P("row", None),
        P("row", None),
        P("row", None),
    )
    out_specs = (P(("row", "col"), None), P("row", None, None, "col"))
    body = make_body(mesh.shape["row"], mesh.shape["col"])
    return jax.shard_map(body, mesh=mesh, in_specs=in_specs, out_specs=out_specs, check_vma=False)
```

time: 260 us -> 160 us (0.62)
  waiting for transfers between devices: 158 us -> 50.2 us
  blocking collectives: 68.4 us -> 35.4 us
  local copies, waits for them, and re-layouts: 3.27 us -> 20.8 us
  other arithmetic: 6.18 us -> 18 us
  starting transfers between devices: 0.15 us -> 11 us
  Pallas kernels: 0 us -> 2.63 us
    all_gather x3 -> x1, waiting for transfers between devices: 99.9 us -> 0.01 us  [body(): gathered = lax.all_gather(payload, 'col', axis=0, tiled=False)]
    all_gather x2 -> x0, blocking collectives: 68.4 us -> none  [the longest x1 47.5 us: body(): wo_rows = lax.all_gather(output_weight, 'row', axis=1, tiled=True)]
    reduce_scatter x1 -> x0, waiting for transfers between devices: 55.5 us -> none  [body(): lax.psum_scatter(jnp.dot(attended, wo_rows, preferred_element_type=jnp.fl...]
    all_to_all x0 -> x2, waiting for transfers between devices: none -> 50.1 us  [the longest x1 27.5 us: body(): lax.all_to_all(pair_sum, 'col', 0, 0, tiled=False, axis_index_groups=y_gr...]
    all_to_all x0 -> x2, blocking collectives: none -> 35.4 us  [the longest x1 26.7 us: body(): lax.all_to_all(copies(weight_block, n_z), 'row', 0, 0, tiled=False, axis_...]
    all_to_all x0 -> x2, starting transfers between devices: none -> 11 us  [the longest x1 6.82 us: body(): lax.all_to_all(pair_sum, 'col', 0, 0, tiled=False, axis_index_groups=y_gr...]
    convert_element_type x1 -> x4, other arithmetic: 0.68 us -> 7.28 us  [the longest x1 4.7 us: body(): widened = gathered_hidden.astype(jnp.float32)]
    convert_element_type x1, local copies, waits for them, and re-layouts: 0.13 us -> 5.39 us  [body(): widened = gathered_hidden.astype(jnp.float32)]
  transfers between devices with their start and end apart: 4 -> 3, of which waited for: 3 -> 2; matrix products, arithmetic and copies ran while one was open for 4% -> 5% of each run, Pallas kernels for 0% -> 0%
where the time goes in v1:
time: 160 us; the launch traced here: 159 us
  waiting for transfers between devices  50.2 us (31%)
  blocking collectives  35.4 us (22%)
  local copies, waits for them, and re-layouts  20.8 us (13%)
  other arithmetic  18 us (11%)
  between operations  14.2 us (9%)
  starting transfers between devices  11 us (7%)
  matrix products  6.86 us (4%)
  Pallas kernels  2.63 us (2%)
    all_to_all x1, waiting for transfers between devices, body(): lax.all_to_all(pair_sum, 'col', 0, 0, tiled=False, axis_index_groups=y_gr...  27.5 us
    all_to_all x1, blocking collectives, body(): lax.all_to_all(copies(weight_block, n_z), 'row', 0, 0, tiled=False, axis_...  26.7 us
    all_to_all x1, waiting for transfers between devices, body(): lax.all_to_all(copies(over_z, X_SIZE), 'row', 0, 0, tiled=False, axis_ind...  22.6 us
    all_to_all x1, blocking collectives, body(): lax.all_to_all(by_core, 'col', 0, 0, tiled=False, axis_index_groups=pair_...  8.7 us
    all_to_all x1, starting transfers between devices, body(): lax.all_to_all(pair_sum, 'col', 0, 0, tiled=False, axis_index_groups=y_gr...  6.82 us
    convert_element_type x1, local copies, waits for them, and re-layouts, body(): widened = gathered_hidden.astype(jnp.float32)  5.39 us
    convert_element_type x1, other arithmetic, body(): widened = gathered_hidden.astype(jnp.float32)  4.7 us
    all_to_all x1, starting transfers between devices, body(): lax.all_to_all(copies(over_z, X_SIZE), 'row', 0, 0, tiled=False, axis_ind...  4.14 us
  transfers between devices with their start and end apart: 3, of which 2 were waited for; matrix products, arithmetic and copies ran while one was open for 5% of the time, Pallas kernels for 0%

profile of v1, /device:TPU:1, one launch (start us, length us, event | category | flops | bytes accessed | tf_op | source)
XLA Modules:
  0.0 159.0 jit_solution(15838546708570023677)
XLA Ops:
  8.9 1.6 %pad_maximum_fusion = bf16[1040,128]{1,0:T(8,128)(2,1)} fusion(bf16[16,128]{1,0:T(8,128)(2,1)S(1)} %broadcast_in_dim.48, bf16[512,128]{1,0:T(8,128)(2,1)S(1)} %bitcast.126, bf16[512,128]{1,0:T(8,128)(2,1)} %param.11), kind=kLoop, calls=%fused_computation.45 | loop fusion | flops 798720 | bytes 532480 | tf_op jit(solution)/shard_map/concatenate | solution.py:95
  12.0 26.7 %all_to_all.20 = bf16[8,64,512]{2,1,0:T(8,128)(2,1)S(1)} all-to-all(bf16[8,64,512]{2,1,0:T(8,128)(2,1)S(1)} %broadcast_in_dim.50), channel_id=1, replica_groups={{0,64,128,192,256,320,384,448},{16,80,144,208,272,336,400,464},{32,96,1..., dimensions={0} | all-to-all | bytes 1048576 | tf_op jit(solution)/shard_map/all_to_all | solution.py:107
  38.7 1.6 broadcast_in_dim.51
  40.2 4.1 %all-to-all-start.1 = ((bf16[4,8,64,512]{3,2,1,0:T(8,128)(2,1)}), bf16[4,8,64,512]{3,2,1,0:T(8,128)(2,1)S(1)}, u32[]{:S(2)}, u32[]{:S(2)}) async-start(bf16[4,8,64,512]{3,2,1,0:T(8,128)(2,1)} %broadcast_in_dim.51), calls=%async_computation.1 | async-start | bytes 4194304 | tf_op jit(solution)/shard_map/all_to_all | solution.py:110
  45.4 22.6 %all-to-all-done.1 = bf16[4,8,64,512]{3,2,1,0:T(8,128)(2,1)S(1)} async-done(((bf16[4,8,64,512]{3,2,1,0:T(8,128)(2,1)}), bf16[4,8,64,512]{3,2,1,0:T(8,128)(2,1)S(1)}, u32[]{:S(2)}, u32[]{:S(2)}) %all-to-all-start.1) | async-done | bytes 2097184 | tf_op jit(solution)/shard_map/all_to_all | solution.py:110
  68.0 1.5 copy.60
  69.5 4.7 %convert_bitcast_fusion = (f32[512,16,128]{2,0,1:T(8,128)}, bf16[16,512,128]{2,1,0:T(8,128)(2,1)S(1)}) fusion(bf16[16,1040,128]{2,1,0:T(8,128)(2,1)} %bitcast.111), kind=kLoop, calls=%fused_computation.4 | loop fusion | flops 1048576 | bytes 10485760 | tf_op jit(solution)/shard_map/convert_element_type | solution.py:126
  75.0 2.1 %fusion = f32[512]{0:T(512)S(1)} fusion(bf16[16,1040,128]{2,1,0:T(8,128)(2,1)} %bitcast.113), kind=kLoop, calls=%fused_computation.5 | loop fusion | flops 3145216 | bytes 2099200 | tf_op jit(solution)/shard_map/reduce_sum | solution.py:127
  77.1 5.4 %copy.59 = f32[512,16,128]{0,2,1:T(8,128)} copy(f32[512,16,128]{2,0,1:T(8,128)} %get-tuple-element.5) | data formatting | bytes 8388608 | tf_op jit(solution)/shard_map/convert_element_type | solution.py:126
  82.5 3.7 %fusion.5 = bf16[512,16,128]{2,0,1:T(8,128)(2,1)} fusion(f32[16,128]{1,0:T(8,128)S(1)} %bitcast.129, f32[512]{0:T(512)S(1)} %add_rsqrt_fusion, bf16[16,1040,128]{2,1,0:T(8,128)(2,1)} %bitcast.114), kind=kLoop, calls=%fused_computation.12 | loop fusion | flops 4194304 | bytes 4204544 | tf_op jit(solution)/shard_map/mul | solution.py:128
  86.1 3.9 %copy.62 = bf16[512,16,128]{0,2,1:T(8,128)(2,1)} copy(bf16[512,16,128]{2,0,1:T(8,128)(2,1)} %fusion.5) | data formatting | bytes 4194304 | tf_op jit(solution)/shard_map/mul | solution.py:128
  91.0 1.3 copy-done.1
  92.7 1.1 copy-done.3
  93.9 1.3 fusion.12
  95.4 1.3 fusion.15
  98.0 1.3 fusion.38
  99.3 1.4 fusion.11
  100.7 2.6 %online-softmax = f32[512,128]{1,0:T(8,128)} custom-call(f32[512,512]{1,0:T(8,128)} %fusion.11, f32[512,128]{1,0:T(8,128)} %get-tuple-element.17), custom_call_target="tpu_custom_call" | custom-call | tf_op online-softmax
  103.3 1.7 %convolution_convert_fusion = bf16[512,2048]{1,0:T(8,128)(2,1)S(1)} fusion(bf16[2048,512]{1,0:T(8,128)(2,1)S(1)} %bitcast.119, f32[512,128]{1,0:T(8,128)} %online-softmax), kind=kOutput, calls=%fused_computation.11 | convolution fusion | flops 269549568 | bytes 2883584 | tf_op jit(solution)/shard_map/dot_general | solution.py:171
  105.2 8.7 %all_to_all.21 = bf16[2,8,32,2048]{3,2,1,0:T(8,128)(2,1)S(1)} all-to-all(bf16[2,8,32,2048]{3,2,1,0:T(8,128)(2,1)S(1)} %bitcast.117), channel_id=1, replica_groups={{0,1},{2,3},{4,5},{6,7},{8,9},{10,11},{12,13},{14,15},{16,17},{18,19},{..., dimensions={0} | all-to-all | bytes 4194304 | tf_op jit(solution)/shard_map/all_to_all | solution.py:179
  113.9 1.4 fusion.22
  115.3 6.8 %all-to-all-start.3 = ((bf16[8,32,2048]{2,1,0:T(8,128)(2,1)}), bf16[8,32,2048]{2,1,0:T(8,128)(2,1)S(1)}, u32[]{:S(2)}, u32[]{:S(2)}) async-start(bf16[8,32,2048]{2,1,0:T(8,128)(2,1)} %fusion.22), calls=%async_computation.3 | async-start | bytes 2097152 | tf_op jit(solution)/shard_map/all_to_all | solution.py:181
  122.3 1.5 scatter_fusion
  123.8 27.5 %all-to-all-done.3 = bf16[8,32,2048]{2,1,0:T(8,128)(2,1)S(1)} async-done(((bf16[8,32,2048]{2,1,0:T(8,128)(2,1)}), bf16[8,32,2048]{2,1,0:T(8,128)(2,1)S(1)}, u32[]{:S(2)}, u32[]{:S(2)}) %all-to-all-start.3) | async-done | bytes 1048608 | tf_op jit(solution)/shard_map/all_to_all | solution.py:181
  (49 shorter events, 9.1 us)
Async XLA Ops:
  7.2 37.4 %copy-start = (s32[16]{0:T(128)S(1)}, s32[16]{0:T(128)}, u32[]{:S(2)}) copy-start(s32[16]{0:T(128)} %param.18) | copy-start | bytes 196
  7.2 62.3 %all-gather.3.cloned.1.call-start = ((), (), s32[]{:S(2)}) async-start(), calls=%async_computation.4 | async-start | bytes 4526080 | tf_op jit(solution)/shard_map/all_gather | solution.py:103
  40.2 4.2 %copy-start.8 = (s32[1,4]{1,0:T(1,128)S(1)}, s32[1,4]{1,0:T(1,128)}, u32[]{:S(2)}) copy-start(s32[1,4]{1,0:T(1,128)} %param.20) | copy-start | bytes 52
  40.2 4.3 %copy-start.7 = (s32[1,4]{1,0:T(1,128)S(1)}, s32[1,4]{1,0:T(1,128)}, u32[]{:S(2)}) copy-start(s32[1,4]{1,0:T(1,128)} %param.19) | copy-start | bytes 52
  40.2 5.1 %copy-start.5 = (bf16[3,128]{1,0:T(4,128)(2,1)S(1)}, bf16[3,128]{1,0:T(4,128)(2,1)}, u32[]{:S(2)}) copy-start(bf16[3,128]{1,0:T(4,128)(2,1)} %param.14) | copy-start | bytes 2308
  40.2 27.8 %all-to-all-start.1 = ((bf16[4,8,64,512]{3,2,1,0:T(8,128)(2,1)}), bf16[4,8,64,512]{3,2,1,0:T(8,128)(2,1)S(1)}, u32[]{:S(2)}, u32[]{:S(2)}) async-start(bf16[4,8,64,512]{3,2,1,0:T(8,128)(2,1)} %broadcast_in_dim.51), calls=%async_computation.1 | async-start | bytes 4194304 | tf_op jit(solution)/shard_map/all_to_all | solution.py:110
  90.1 2.2 %copy-start.1 = (f32[512,16,128]{0,2,1:T(8,128)S(1)}, f32[512,16,128]{0,2,1:T(8,128)}, u32[]{:S(2)}) copy-start(f32[512,16,128]{0,2,1:T(8,128)} %copy.59) | copy-start | bytes 12582916
  92.3 1.6 %copy-start.3 = (bf16[512,16,128]{0,2,1:T(8,128)(2,1)S(1)}, bf16[512,16,128]{0,2,1:T(8,128)(2,1)}, u32[]{:S(2)}) copy-start(bf16[512,16,128]{0,2,1:T(8,128)(2,1)} %copy.62) | copy-start | bytes 6291460
  93.9 1.6 %copy-start.2 = (bf16[4,8,64,512]{3,2,0,1:T(8,128)(2,1)S(1)}, bf16[4,8,64,512]{3,2,0,1:T(8,128)(2,1)}, u32[]{:S(2)}) copy-start(bf16[4,8,64,512]{3,2,0,1:T(8,128)(2,1)} %copy.60) | copy-start | bytes 6291460
  95.4 1.3 copy-start.6
  113.9 8.2 %copy-start.9 = (s32[1,32]{1,0:T(1,128)S(1)}, s32[1,32]{1,0:T(1,128)}, u32[]{:S(2)}) copy-start(s32[1,32]{1,0:T(1,128)} %param.21) | copy-start | bytes 388
  115.3 36.1 %all-to-all-start.3 = ((bf16[8,32,2048]{2,1,0:T(8,128)(2,1)}), bf16[8,32,2048]{2,1,0:T(8,128)(2,1)S(1)}, u32[]{:S(2)}, u32[]{:S(2)}) async-start(bf16[8,32,2048]{2,1,0:T(8,128)(2,1)} %fusion.22), calls=%async_computation.3 | async-start | bytes 2097152 | tf_op jit(solution)/shard_map/all_to_all | solution.py:181
  123.8 28.4 %copy-start.4 = (bf16[32,2,16,128]{3,2,1,0:T(8,128)(2,1)}, bf16[32,2,16,128]{3,2,1,0:T(8,128)(2,1)S(1)}, u32[]{:S(2)}) copy-start(bf16[32,2,16,128]{3,2,1,0:T(8,128)(2,1)S(1)} %scatter_fusion) | copy-start | bytes 786436
Sparse Core Ops, SparseCore 0:
  10.6 50.8 all-gather.2

commit v2 on v1

v2 whole, which is shorter than its diff:
```python
import jax
import jax.numpy as jnp
from jax import lax
from jax.experimental import pallas as pl
from jax.experimental.pallas import tpu as pltpu
from jax.sharding import PartitionSpec as P

HEAD_DIM = 128
PAGE = 16
GAIN_ROWS = 16
X_SIZE = 4
LONGEST = 256
BLOCK = 128

rope_base = 1000000.0
norm_eps = 1e-06
adapter_scale = 2.0

VMEM = pltpu.MemorySpace.VMEM
SMEM = pltpu.MemorySpace.SMEM


def payload_kernel(hidden, gain, down, out):
    rows, part = hidden.shape
    rank2 = down.shape[0]
    out[0:rows, :] = hidden[...]
    for block in range(down.shape[1] // part):
        out[rows + block * rank2 : rows + (block + 1) * rank2, :] = down[
            :, block * part : (block + 1) * part
        ]
    wide = jnp.broadcast_to(gain[...].astype(jnp.float32), (GAIN_ROWS, part))
    out[out.shape[0] - GAIN_ROWS :, :] = wide.astype(jnp.bfloat16)


def weight_copies_kernel(qkv, out_weight_t, out):
    cols = qkv.shape[2]
    for copy in range(out.shape[0]):
        for i in range(3):
            out[copy, :, i * cols : (i + 1) * cols] = qkv[i]
        out[copy, :, 3 * cols :] = out_weight_t[...]


def block_kernel(
    slots,
    adapters,
    lengths,
    pages,
    x_place,
    gathered,
    piece_0,
    piece_1,
    piece_2,
    piece_3,
    bias,
    up,
    cosine,
    sine_part,
    out,
    cache,
    hidden,
    gain,
    down_raw,
    weights,
    normed,
    down,
    up_wide,
    keys,
    values,
    attended,
    sem_hidden,
    sem_gain,
    sem_down,
    sem_weight,
):
    n_col, total_rows, part = hidden.shape
    width = n_col * part
    n_prompts = down_raw.shape[0]
    rank2 = down_raw.shape[1] // n_col
    rank = rank2 // 2
    blocks = total_rows // BLOCK
    me = x_place[0]

    gain_copy = pltpu.make_async_copy(
        gathered.at[:, pl.ds(gathered.shape[1] - GAIN_ROWS, GAIN_ROWS)], gain, sem_gain.at[0]
    )
    gain_copy.start()
    hidden_copies = []
    for i in range(blocks):
        rows = pl.ds(i * BLOCK, BLOCK)
        hidden_copies.append(
            pltpu.make_async_copy(gathered.at[:, rows], hidden.at[:, rows], sem_hidden.at[i])
        )
        hidden_copies[i].start()
    prompt_slots = [slots[adapters[0, p]] for p in range(n_prompts)]
    down_copies = []
    for p in range(n_prompts):
        down_copies.append(
            pltpu.make_async_copy(
                gathered.at[prompt_slots[p], pl.ds(total_rows, n_col * rank2)],
                down_raw.at[p],
                sem_down.at[p],
            )
        )
        down_copies[p].start()
    weight_copies = []
    for k, piece in enumerate((piece_0, piece_1, piece_2, piece_3)):
        source = lax.rem(me + (X_SIZE - k), X_SIZE)
        weight_copies.append(
            pltpu.make_async_copy(piece, weights.at[:, source], sem_weight.at[k])
        )
        weight_copies[k].start()

    up_wide[...] = jnp.zeros_like(up_wide)
    for p in range(n_prompts):
        first = p * rank2
        up_wide[first : first + rank, 0:HEAD_DIM] = up[prompt_slots[p], 0]
        up_wide[first + rank : first + rank2, HEAD_DIM:] = up[prompt_slots[p], 1]

    gain_copy.wait()
    for i in range(blocks):
        hidden_copies[i].wait()
        rows = slice(i * BLOCK, (i + 1) * BLOCK)
        squares = jnp.zeros((BLOCK, part), jnp.float32)
        for c in range(n_col):
            piece = hidden[c, rows, :].astype(jnp.float32)
            squares = squares + piece * piece
        power = jnp.sum(squares, axis=1, keepdims=True) * (1.0 / width)
        scale = lax.rsqrt(power + norm_eps)
        for c in range(n_col):
            piece = hidden[c, rows, :].astype(jnp.float32)
            gain_row = gain[c, 0:1, :].astype(jnp.float32)
            normed[rows, c * part : (c + 1) * part] = (piece * scale * gain_row).astype(
                jnp.bfloat16
            )
    for p in range(n_prompts):
        down_copies[p].wait()
        for c in range(n_col):
            down[p * rank2 : (p + 1) * rank2, c * part : (c + 1) * part] = down_raw[
                p, c * rank2 : (c + 1) * rank2, :
            ]
    for k in range(X_SIZE):
        weight_copies[k].wait()

    tokens = normed[...]
    weight_qkv = weights[:, :, :, 0 : 3 * HEAD_DIM].reshape(width, 3 * HEAD_DIM)
    projected = jnp.dot(tokens, weight_qkv, preferred_element_type=jnp.float32)
    lowrank = lax.dot_general(
        tokens, down[...], (((1,), (1,)), ((), ())), preferred_element_type=jnp.float32
    ).astype(jnp.bfloat16)

    end_0 = lengths[0, 0]
    end_1 = end_0 + lengths[0, 1]
    end_2 = end_1 + lengths[0, 2]
    place = lax.broadcasted_iota(jnp.int32, (total_rows, n_prompts * rank2), 0)
    segment = (
        (place >= end_0).astype(jnp.int32)
        + (place >= end_1).astype(jnp.int32)
        + (place >= end_2).astype(jnp.int32)
    )
    lane = lax.broadcasted_iota(jnp.int32, (total_rows, n_prompts * rank2), 1)
    in_prompt = (lane >= segment * rank2) & (lane < segment * rank2 + rank2)
    picked = jnp.where(in_prompt, lowrank.astype(jnp.float32), 0.0).astype(jnp.bfloat16)
    update = jnp.dot(picked, up_wide[...], preferred_element_type=jnp.float32)

    bias_wide = bias[...].astype(jnp.float32)
    query_rows = projected[:, 0:HEAD_DIM] + bias_wide[0:1] + adapter_scale * update[:, 0:HEAD_DIM]
    key_rows = projected[:, HEAD_DIM : 2 * HEAD_DIM] + bias_wide[1:2]
    value_rows = (
        projected[:, 2 * HEAD_DIM :] + bias_wide[2:3] + adapter_scale * update[:, HEAD_DIM:]
    )
    cos_all = cosine[...]
    sin_all = sine_part[...]
    half = HEAD_DIM // 2
    queries = (query_rows * cos_all + pltpu.roll(query_rows, half, 1) * sin_all).astype(
        jnp.bfloat16
    )
    keys[...] = (key_rows * cos_all + pltpu.roll(key_rows, half, 1) * sin_all).astype(jnp.bfloat16)
    values[...] = value_rows.astype(jnp.bfloat16)
    for page in range(total_rows // PAGE):
        to = pages[0, page]
        cache[to, 0] = keys[page * PAGE : (page + 1) * PAGE, :]
        cache[to, 1] = values[page * PAGE : (page + 1) * PAGE, :]

    factor = HEAD_DIM ** (-0.5)
    reach = LONGEST // BLOCK
    for i in range(blocks):
        low = max(0, i - reach) * BLOCK
        high = (i + 1) * BLOCK
        query = queries[i * BLOCK : high, :]
        scores = lax.dot_general(
            query, keys[low:high, :], (((1,), (1,)), ((), ())), preferred_element_type=jnp.float32
        )
        query_place = i * BLOCK + lax.broadcasted_iota(jnp.int32, scores.shape, 0)
        key_place = low + lax.broadcasted_iota(jnp.int32, scores.shape, 1)
        start = jnp.where(
            query_place >= end_2,
            end_2,
            jnp.where(query_place >= end_1, end_1, jnp.where(query_place >= end_0, end_0, 0)),
        )
        allowed = (key_place <= query_place) & (key_place >= start)
        scores = jnp.where(allowed, scores * factor, -1e30)
        highest = jnp.max(scores, axis=1, keepdims=True)
        exps = jnp.exp(scores - highest)
        probs = (exps * (1.0 / jnp.sum(exps, axis=1, keepdims=True))).astype(jnp.bfloat16)
        attended[i * BLOCK : high, :] = jnp.dot(
            probs, values[low:high, :], preferred_element_type=jnp.float32
        ).astype(jnp.bfloat16)

    weight_out = weights[:, :, :, 3 * HEAD_DIM :].reshape(width, HEAD_DIM)
    partial = lax.dot_general(
        attended[...], weight_out, (((1,), (1,)), ((), ())), preferred_element_type=jnp.float32
    ).astype(jnp.bfloat16)
    out_rows = out.shape[2]
    for b in range(n_col):
        out[b % 2, b // 2] = partial[b * out_rows : (b + 1) * out_rows, :]


def make_body(n_row, n_col):
    n_z = n_row // X_SIZE
    z_groups = [[z * X_SIZE + x for z in range(n_z)] for x in range(X_SIZE)]
    pair_groups = [[i, i + 1] for i in range(0, n_col, 2)]
    y_groups = [list(range(core, n_col, 2)) for core in range(2)]

    def x_shift(step):
        return [
            (z * X_SIZE + x, z * X_SIZE + (x + step) % X_SIZE)
            for z in range(n_z)
            for x in range(X_SIZE)
        ]

    def body(
        incoming_hidden,
        input_norm_weight,
        query_key_value_weight,
        query_key_value_bias,
        output_weight,
        adapter_down_weight,
        adapter_up_weight,
        slot_of_adapter,
        adapter_of_prompt,
        prompt_length_list,
        cache_page_index,
    ):
        total_rows, part = incoming_hidden.shape
        rank2 = adapter_down_weight.shape[1] * adapter_down_weight.shape[2]
        width = adapter_down_weight.shape[3]
        row_part = query_key_value_weight.shape[1]
        head_cols = query_key_value_weight.shape[2]
        n_prompts = prompt_length_list.shape[1]
        out_rows = total_rows // n_col
        payload_rows = total_rows + n_col * rank2 + GAIN_ROWS
        payload = pl.pallas_call(
            payload_kernel,
            out_shape=jax.ShapeDtypeStruct((payload_rows, part), jnp.bfloat16),
            name="payload",
        )(incoming_hidden, input_norm_weight, adapter_down_weight.reshape(rank2, width))
        gathered = lax.all_gather(payload, "col", axis=0, tiled=False)
        copies = pl.pallas_call(
            weight_copies_kernel,
            out_shape=jax.ShapeDtypeStruct((n_z, row_part, 4 * head_cols), jnp.bfloat16),
            name="weight_copies",
        )(query_key_value_weight, output_weight.T)
        over_z = lax.all_to_all(copies, "row", 0, 0, tiled=False, axis_index_groups=z_groups)
        pieces = [over_z] + [lax.ppermute(over_z, "row", x_shift(k)) for k in range(1, X_SIZE)]

        lengths = prompt_length_list[0]
        places = jnp.arange(total_rows, dtype=jnp.int32)
        ends = jnp.cumsum(lengths)
        start = jnp.zeros_like(places)
        for p in range(n_prompts - 1):
            start = jnp.where(places >= ends[p], ends[p], start)
        position = (places - start).astype(jnp.float32)
        half = HEAD_DIM // 2
        inverse_freq = rope_base ** (-(jnp.arange(half, dtype=jnp.float32) * 2.0 / HEAD_DIM))
        angles = position[:, None] * inverse_freq[None, :]
        cos_half = jnp.cos(angles)
        sin_half = jnp.sin(angles)
        cosine = jnp.concatenate([cos_half, cos_half], axis=1)
        sine_part = jnp.concatenate([-sin_half, sin_half], axis=1)
        x_place = lax.rem(lax.axis_index("row"), X_SIZE).astype(jnp.int32).reshape(1)

        whole = pl.BlockSpec(memory_space=VMEM)
        scalar = pl.BlockSpec(memory_space=SMEM)
        raw = pl.BlockSpec(memory_space=pl.ANY)
        partial, cache = pl.pallas_call(
            block_kernel,
            out_shape=(
                jax.ShapeDtypeStruct((2, n_col // 2, out_rows, width), jnp.bfloat16),
                jax.ShapeDtypeStruct((total_rows // PAGE, 2, PAGE, head_cols), jnp.bfloat16),
            ),
            in_specs=[scalar] * 5 + [raw] * 5 + [whole] * 4,
            out_specs=(whole, whole),
            scratch_shapes=[
                pltpu.VMEM((n_col, total_rows, part), jnp.bfloat16),
                pltpu.VMEM((n_col, GAIN_ROWS, part), jnp.bfloat16),
                pltpu.VMEM((n_prompts, n_col * rank2, part), jnp.bfloat16),
                pltpu.VMEM((n_z, X_SIZE, row_part, 4 * head_cols), jnp.bfloat16),
                pltpu.VMEM((total_rows, width), jnp.bfloat16),
                pltpu.VMEM((n_prompts * rank2, width), jnp.bfloat16),
                pltpu.VMEM((n_prompts * rank2, 2 * head_cols), jnp.bfloat16),
                pltpu.VMEM((total_rows, head_cols), jnp.bfloat16),
                pltpu.VMEM((total_rows, head_cols), jnp.bfloat16),
                pltpu.VMEM((total_rows, head_cols), jnp.bfloat16),
                pltpu.SemaphoreType.DMA((total_rows // BLOCK,)),
                pltpu.SemaphoreType.DMA((1,)),
                pltpu.SemaphoreType.DMA((n_prompts,)),
                pltpu.SemaphoreType.DMA((X_SIZE,)),
            ],
            compiler_params=pltpu.CompilerParams(vmem_limit_bytes=48 * 1024 * 1024),
            name="attention_block",
        )(
            slot_of_adapter,
            adapter_of_prompt,
            prompt_length_list,
            cache_page_index,
            x_place,
            gathered,
            *pieces,
            query_key_value_bias,
            adapter_up_weight,
            cosine,
            sine_part,
        )
        pair = lax.all_to_all(partial, "col", 0, 0, tiled=False, axis_index_groups=pair_groups)
        pair_sum = (pair[0].astype(jnp.float32) + pair[1].astype(jnp.float32)).astype(jnp.bfloat16)
        terms = lax.all_to_all(pair_sum, "col", 0, 0, tiled=False, axis_index_groups=y_groups)
        summed = jnp.sum(terms.astype(jnp.float32), axis=0).astype(jnp.bfloat16)
        return (summed, cache)

    return body


def solution(mesh):
    in_specs = (
        P("row", "col"),
        P(None, "col"),
        P(None, "row", "col"),
        P(None, "col"),
        P("col", "row"),
        P("col", None, None, None),
        P(None, None, None, "col"),
        P(),
        P("row", None),
        P("row", None),
        P("row", None),
    )
    out_specs = (P(("row", "col"), None), P("row", None, None, "col"))
    body = make_body(mesh.shape["row"], mesh.shape["col"])
    return jax.shard_map(body, mesh=mesh, in_specs=in_specs, out_specs=out_specs, check_vma=False)
```

time: 160 us -> 129 us (0.81)
  local copies, waits for them, and re-layouts: 20.8 us -> 0.62 us
  other arithmetic: 18 us -> 4.5 us
  waiting for transfers between devices: 50.2 us -> 37.6 us
  starting transfers between devices: 11 us -> 20.2 us
  Pallas kernels: 2.63 us -> 11.5 us
  matrix products: 6.86 us -> 0 us
  blocking collectives: 35.4 us -> 40.1 us
    all_to_all x2 -> x1, waiting for transfers between devices: 50.1 us -> 17.2 us  [body(): lax.all_to_all(copies, 'row', 0, 0, tiled=False, axis_index_groups=z_groups)]
    ppermute x0 -> x3, waiting for transfers between devices: none -> 20.4 us  [body(): lax.ppermute(over_z, 'row', x_shift(k))]
    pallas_call x0 -> x3, Pallas kernels: none -> 11.5 us  [the longest x1 8 us: body(): pl.pallas_call(block_kernel, out_shape=(jax.ShapeDtypeStruct((2, n_col //...]
    ppermute x0 -> x3, starting transfers between devices: none -> 9.32 us  [body(): lax.ppermute(over_z, 'row', x_shift(k))]
    dot_general x6 -> x0, matrix products: 6.86 us -> none  [the longest x1 1.66 us: body(): lax.dot_general(attended, weights[:, 3 * head_cols:], (((1,), (1,)), ((),...]
    convert_element_type x1 -> x0, local copies, waits for them, and re-layouts: 5.39 us -> none  [body(): widened = gathered_hidden.astype(jnp.float32)]
    all_to_all x2, blocking collectives: 35.4 us -> 40.1 us  [the longest x1 34.6 us: body(): lax.all_to_all(pair_sum, 'col', 0, 0, tiled=False, axis_index_groups=y_gr...]
    convert_element_type x4 -> x1, other arithmetic: 5.92 us -> 1.91 us  [body(): position = (places - start).astype(jnp.float32)]
  transfers between devices with their start and end apart: 3 -> 5, of which waited for: 2 -> 4; matrix products, arithmetic and copies ran while one was open for 5% -> 3% of each run, Pallas kernels for 0% -> 1%
where the time goes in v2:
time: 129 us
  blocking collectives  40.1 us (31%)
  waiting for transfers between devices  37.6 us (29%)
  starting transfers between devices  20.2 us (16%)
  between operations  14.1 us (11%)
  Pallas kernels  11.5 us (9%)
  other arithmetic  4.5 us (3%)
    all_to_all x1, blocking collectives, body(): lax.all_to_all(pair_sum, 'col', 0, 0, tiled=False, axis_index_groups=y_gr...  34.6 us
    ppermute x3, waiting for transfers between devices, body(): lax.ppermute(over_z, 'row', x_shift(k))  20.4 us
    all_to_all x1, waiting for transfers between devices, body(): lax.all_to_all(copies, 'row', 0, 0, tiled=False, axis_index_groups=z_groups)  17.2 us
    all_to_all x1, starting transfers between devices, body(): lax.all_to_all(copies, 'row', 0, 0, tiled=False, axis_index_groups=z_groups)  10.9 us
    ppermute x3, starting transfers between devices, body(): lax.ppermute(over_z, 'row', x_shift(k))  9.32 us
    pallas_call x1, Pallas kernels, body(): pl.pallas_call(block_kernel, out_shape=(jax.ShapeDtypeStruct((2, n_col //...  8 us
    all_to_all x1, blocking collectives, body(): lax.all_to_all(partial, 'col', 0, 0, tiled=False, axis_index_groups=pair_...  5.54 us
  transfers between devices with their start and end apart: 5, of which 4 were waited for; matrix products, arithmetic and copies ran while one was open for 3% of the time, Pallas kernels for 1%

profile of v2, /device:TPU:1, one launch (start us, length us, event | category | flops | bytes accessed | tf_op | source)
XLA Modules:
  0.0 128.6 jit_solution(14230483351554808714)
XLA Ops:
  7.2 0.0 all-gather.3.cloned.1.call-start
  7.2 1.7 %payload.1 = bf16[1040,128]{1,0:T(8,128)(2,1)} custom-call(bf16[512,128]{1,0:T(8,128)(2,1)} %hidden.1, bf16[1,128]{1,0:T(2,128)(2,1)} %gain.1, bf16[32,2048]{1,0:T(8,128)(2,1)} %bitcast.12), custom_call_target="tpu_custom_call" | custom-call | tf_op jit(solution)/shard_map/payload/pallas_call | solution.py:252
  9.0 0.0 copy-start.5
  9.0 0.0 all-gather.3.cloned.1.call-update
  9.0 1.8 %weight_copies.1 = bf16[8,64,512]{2,1,0:T(8,128)(2,1)} custom-call(bf16[3,64,128]{2,1,0:T(8,128)(2,1)} %qkv.1, bf16[64,128]{1,0:T(8,128)(2,1)} %bitcast.13), custom_call_target="tpu_custom_call" | custom-call | tf_op jit(solution)/shard_map/weight_copies/pallas_call | solution.py:258
  10.8 10.9 %all-to-all-start = ((bf16[8,64,512]{2,1,0:T(8,128)(2,1)}), bf16[8,64,512]{2,1,0:T(8,128)(2,1)S(1)}, u32[]{:S(2)}, u32[]{:S(2)}) async-start(bf16[8,64,512]{2,1,0:T(8,128)(2,1)} %weight_copies.1), calls=%async_computation | async-start | bytes 1048576 | tf_op jit(solution)/shard_map/all_to_all | solution.py:263
  21.6 0.0 copy-done.4
  21.6 0.2 reduce-window.4
  21.8 0.6 fusion.2
  22.4 17.2 %all-to-all-done.piece_0 = bf16[8,64,512]{2,1,0:T(8,128)(2,1)S(1)} async-done(((bf16[8,64,512]{2,1,0:T(8,128)(2,1)}), bf16[8,64,512]{2,1,0:T(8,128)(2,1)S(1)}, u32[]{:S(2)}, u32[]{:S(2)}) %all-to-all-start) | async-done | bytes 524320 | tf_op jit(solution)/shard_map/all_to_all | solution.py:263
  39.6 4.4 %collective-permute-start.2 = (bf16[8,64,512]{2,1,0:T(8,128)(2,1)S(1)}, bf16[8,64,512]{2,1,0:T(8,128)(2,1)S(1)}, u32[]{:S(2)}, u32[]{:S(2)}) collective-permute-start(bf16[8,64,512]{2,1,0:T(8,128)(2,1)S(1)} %all-to-all-done.piece_0), channel_id=1, source_target_pairs={{0,48},{16,0},{32,16},{48,32},{64,112},{80,64},{96,80},{112,96},{1... | collective-permute-start | bytes 1572872 | tf_op jit(solution)/shard_map/ppermute | solution.py:264
  44.0 2.4 %collective-permute-start.1 = (bf16[8,64,512]{2,1,0:T(8,128)(2,1)S(1)}, bf16[8,64,512]{2,1,0:T(8,128)(2,1)S(1)}, u32[]{:S(2)}, u32[]{:S(2)}) collective-permute-start(bf16[8,64,512]{2,1,0:T(8,128)(2,1)S(1)} %all-to-all-done.piece_0), channel_id=1, source_target_pairs={{0,32},{16,48},{32,0},{48,16},{64,96},{80,112},{96,64},{112,80},{1... | collective-permute-start | bytes 1572872 | tf_op jit(solution)/shard_map/ppermute | solution.py:264
  46.4 2.5 %collective-permute-start = (bf16[8,64,512]{2,1,0:T(8,128)(2,1)S(1)}, bf16[8,64,512]{2,1,0:T(8,128)(2,1)S(1)}, u32[]{:S(2)}, u32[]{:S(2)}) collective-permute-start(bf16[8,64,512]{2,1,0:T(8,128)(2,1)S(1)} %all-to-all-done.piece_0), channel_id=1, source_target_pairs={{0,16},{16,32},{32,48},{48,0},{64,80},{80,96},{96,112},{112,64},{1... | collective-permute-start | bytes 1572872 | tf_op jit(solution)/shard_map/ppermute | solution.py:264
  48.9 1.9 %subtract_convert_fusion = f32[512]{0:T(512)S(1)} fusion(s32[]{:T(128)} %bitcast.7, s32[]{:T(128)} %bitcast.6, s32[]{:T(128)} %bitcast.5), kind=kLoop, calls=%fused_computation.7 | loop fusion | flops 4096 | bytes 2060 | tf_op jit(solution)/shard_map/convert_element_type | solution.py:272
  50.9 1.0 fusion.1
  51.9 0.2 pad_maximum_fusion
  52.1 3.5 %collective-permute-done.2.piece_3 = bf16[8,64,512]{2,1,0:T(8,128)(2,1)S(1)} collective-permute-done((bf16[8,64,512]{2,1,0:T(8,128)(2,1)S(1)}, bf16[8,64,512]{2,1,0:T(8,128)(2,1)S(1)}, u32[]{:S(2)}, u32[]{:S(2)}) %collective-permute-start.2) | collective-permute-done | bytes 524320 | tf_op jit(solution)/shard_map/ppermute | solution.py:264
  55.5 4.5 %collective-permute-done.1.piece_2 = bf16[8,64,512]{2,1,0:T(8,128)(2,1)S(1)} collective-permute-done((bf16[8,64,512]{2,1,0:T(8,128)(2,1)S(1)}, bf16[8,64,512]{2,1,0:T(8,128)(2,1)S(1)}, u32[]{:S(2)}, u32[]{:S(2)}) %collective-permute-start.1) | collective-permute-done | bytes 524320 | tf_op jit(solution)/shard_map/ppermute | solution.py:264
  60.1 12.4 %collective-permute-done.piece_1 = bf16[8,64,512]{2,1,0:T(8,128)(2,1)S(1)} collective-permute-done((bf16[8,64,512]{2,1,0:T(8,128)(2,1)S(1)}, bf16[8,64,512]{2,1,0:T(8,128)(2,1)S(1)}, u32[]{:S(2)}, u32[]{:S(2)}) %collective-permute-start) | collective-permute-done | bytes 524320 | tf_op jit(solution)/shard_map/ppermute | solution.py:264
  72.5 8.0 %attention_block.1 = (bf16[2,8,32,2048]{3,2,1,0:T(8,128)(2,1)S(1)}, bf16[32,2,16,128]{3,2,1,0:T(8,128)(2,1)}) custom-call(s32[16]{0:T(128)S(1)} %copy-done.2, s32[1,4]{1,0:T(1,128)S(1)} %copy-done.3, s32[1,4]{1,0:T(1,128)S(1)} %copy-done.4, s32[1,32]{1,0:T(1,128)S(1)} %copy-done.5, s32[1]{0:T(128)} %bitcast.x_place, bf16[16,1040,128]{2,1,0:T(8,128)(2,1)} %bitcast.11, ...), custom_call_target="tpu_custom_call" | custom-call | tf_op jit(solution)/shard_map/attention_block/pallas_call | solution.py:285
  80.5 5.5 %all_to_all.15 = bf16[2,8,32,2048]{3,2,1,0:T(8,128)(2,1)S(1)} all-to-all(bf16[2,8,32,2048]{3,2,1,0:T(8,128)(2,1)S(1)} %get-tuple-element.4), channel_id=1, replica_groups={{0,1},{2,3},{4,5},{6,7},{8,9},{10,11},{12,13},{14,15},{16,17},{18,19},{..., dimensions={0} | all-to-all | bytes 4194304 | tf_op jit(solution)/shard_map/all_to_all | solution.py:324
  86.0 0.4 fusion
  86.4 34.6 %all_to_all.16 = bf16[8,32,2048]{2,1,0:T(8,128)(2,1)S(1)} all-to-all(bf16[8,32,2048]{2,1,0:T(8,128)(2,1)S(1)} %fusion), channel_id=1, replica_groups={{0,2,4,6,8,10,12,14},{1,3,5,7,9,11,13,15},{16,18,20,22,24,26,28,30},{17..., dimensions={0} | all-to-all | bytes 2097152 | tf_op jit(solution)/shard_map/all_to_all | solution.py:326
  121.0 0.8 reduce_sum.12
  (12 shorter events, 0.0 us)
Async XLA Ops:
  7.2 14.5 %copy-start.4 = (s32[1,4]{1,0:T(1,128)S(1)}, s32[1,4]{1,0:T(1,128)}, u32[]{:S(2)}) copy-start(s32[1,4]{1,0:T(1,128)} %lengths.1) | copy-start | bytes 52
  7.2 65.3 %all-gather.3.cloned.1.call-start = ((), (), s32[]{:S(2)}) async-start(), calls=%async_computation.3 | async-start | bytes 4526080 | tf_op jit(solution)/shard_map/all_gather | solution.py:257
  8.9 63.5 %copy-start = (bf16[16,2,16,128]{3,2,1,0:T(8,128)(2,1)S(1)}, bf16[16,2,16,128]{3,2,1,0:T(8,128)(2,1)}, u32[]{:S(2)}) copy-start(bf16[16,2,16,128]{3,2,1,0:T(8,128)(2,1)} %up.1) | copy-start | bytes 393220
  9.0 63.5 %copy-start.1 = (bf16[3,128]{1,0:T(4,128)(2,1)S(1)}, bf16[3,128]{1,0:T(4,128)(2,1)}, u32[]{:S(2)}) copy-start(bf16[3,128]{1,0:T(4,128)(2,1)} %bias.1) | copy-start | bytes 2308
  9.0 63.5 %copy-start.2 = (s32[16]{0:T(128)S(1)}, s32[16]{0:T(128)}, u32[]{:S(2)}) copy-start(s32[16]{0:T(128)} %slots.1) | copy-start | bytes 196
  9.0 63.5 %copy-start.3 = (s32[1,4]{1,0:T(1,128)S(1)}, s32[1,4]{1,0:T(1,128)}, u32[]{:S(2)}) copy-start(s32[1,4]{1,0:T(1,128)} %adapters.1) | copy-start | bytes 52
  9.0 63.5 %copy-start.5 = (s32[1,32]{1,0:T(1,128)S(1)}, s32[1,32]{1,0:T(1,128)}, u32[]{:S(2)}) copy-start(s32[1,32]{1,0:T(1,128)} %pages.1) | copy-start | bytes 388
  10.8 28.8 %all-to-all-start = ((bf16[8,64,512]{2,1,0:T(8,128)(2,1)}), bf16[8,64,512]{2,1,0:T(8,128)(2,1)S(1)}, u32[]{:S(2)}, u32[]{:S(2)}) async-start(bf16[8,64,512]{2,1,0:T(8,128)(2,1)} %weight_copies.1), calls=%async_computation | async-start | bytes 1048576 | tf_op jit(solution)/shard_map/all_to_all | solution.py:263
  39.6 16.0 %collective-permute-start.2 = (bf16[8,64,512]{2,1,0:T(8,128)(2,1)S(1)}, bf16[8,64,512]{2,1,0:T(8,128)(2,1)S(1)}, u32[]{:S(2)}, u32[]{:S(2)}) collective-permute-start(bf16[8,64,512]{2,1,0:T(8,128)(2,1)S(1)} %all-to-all-done.piece_0), channel_id=1, source_target_pairs={{0,48},{16,0},{32,16},{48,32},{64,112},{80,64},{96,80},{112,96},{1... | collective-permute-start | bytes 1572872 | tf_op jit(solution)/shard_map/ppermute | solution.py:264
  44.0 16.1 %collective-permute-start.1 = (bf16[8,64,512]{2,1,0:T(8,128)(2,1)S(1)}, bf16[8,64,512]{2,1,0:T(8,128)(2,1)S(1)}, u32[]{:S(2)}, u32[]{:S(2)}) collective-permute-start(bf16[8,64,512]{2,1,0:T(8,128)(2,1)S(1)} %all-to-all-done.piece_0), channel_id=1, source_target_pairs={{0,32},{16,48},{32,0},{48,16},{64,96},{80,112},{96,64},{112,80},{1... | collective-permute-start | bytes 1572872 | tf_op jit(solution)/shard_map/ppermute | solution.py:264
  46.4 26.0 %collective-permute-start = (bf16[8,64,512]{2,1,0:T(8,128)(2,1)S(1)}, bf16[8,64,512]{2,1,0:T(8,128)(2,1)S(1)}, u32[]{:S(2)}, u32[]{:S(2)}) collective-permute-start(bf16[8,64,512]{2,1,0:T(8,128)(2,1)S(1)} %all-to-all-done.piece_0), channel_id=1, source_target_pairs={{0,16},{16,32},{32,48},{48,0},{64,80},{80,96},{96,112},{112,64},{1... | collective-permute-start | bytes 1572872 | tf_op jit(solution)/shard_map/ppermute | solution.py:264
Sparse Core Ops, SparseCore 0:
  10.1 50.8 all-gather.2

commit v3 on v2

--- a/solution.py
+++ b/solution.py
@@ -1,5 +1,6 @@
 import jax
 import jax.numpy as jnp
+import numpy as np
 from jax import lax
 from jax.experimental import pallas as pl
 from jax.experimental.pallas import tpu as pltpu
@@ -18,6 +19,7 @@
 
 VMEM = pltpu.MemorySpace.VMEM
 SMEM = pltpu.MemorySpace.SMEM
+HBM = pltpu.MemorySpace.HBM
 
 
 def payload_kernel(hidden, gain, down, out):
@@ -40,37 +42,28 @@
         out[copy, :, 3 * cols :] = out_weight_t[...]
 
 
-def block_kernel(
+def norm_kernel(
     slots,
     adapters,
     lengths,
-    pages,
-    x_place,
     gathered,
-    piece_0,
-    piece_1,
-    piece_2,
-    piece_3,
     bias,
     up,
     cosine,
     sine_part,
-    out,
-    cache,
+    gained_x,
+    row_scale,
+    offset,
+    cos_all,
+    sin_all,
     hidden,
     gain,
     down_raw,
-    weights,
-    normed,
-    down,
+    down_x,
     up_wide,
-    keys,
-    values,
-    attended,
     sem_hidden,
     sem_gain,
     sem_down,
-    sem_weight,
 ):
     n_col, total_rows, part = hidden.shape
     width = n_col * part
@@ -78,7 +71,6 @@
     rank2 = down_raw.shape[1] // n_col
     rank = rank2 // 2
     blocks = total_rows // BLOCK
-    me = x_place[0]
 
     gain_copy = pltpu.make_async_copy(
         gathered.at[:, pl.ds(gathered.shape[1] - GAIN_ROWS, GAIN_ROWS)], gain, sem_gain.at[0]
@@ -102,13 +94,6 @@
             )
         )
         down_copies[p].start()
-    weight_copies = []
-    for k, piece in enumerate((piece_0, piece_1, piece_2, piece_3)):
-        source = lax.rem(me + (X_SIZE - k), X_SIZE)
-        weight_copies.append(
-            pltpu.make_async_copy(piece, weights.at[:, source], sem_weight.at[k])
-        )
-        weight_copies[k].start()
 
     up_wide[...] = jnp.zeros_like(up_wide)
     for p in range(n_prompts):
@@ -116,41 +101,71 @@
         up_wide[first : first + rank, 0:HEAD_DIM] = up[prompt_slots[p], 0]
         up_wide[first + rank : first + rank2, HEAD_DIM:] = up[prompt_slots[p], 1]
 
+    end_0 = lengths[0, 0]
+    end_1 = end_0 + lengths[0, 1]
+    end_2 = end_1 + lengths[0, 2]
+    place_wide = lax.broadcasted_iota(jnp.int32, (total_rows, HEAD_DIM), 0)
+    lane_sign = jnp.where(
+        lax.broadcasted_iota(jnp.int32, (1, HEAD_DIM), 1) < HEAD_DIM // 2, -1.0, 1.0
+    )
+    start_cos = jnp.ones((total_rows, HEAD_DIM), jnp.float32)
+    start_sin = jnp.zeros((total_rows, HEAD_DIM), jnp.float32)
+    for end in (end_0, end_1, end_2):
+        after = place_wide >= end
+        start_cos = jnp.where(after, cosine[pl.ds(end, 1), :], start_cos)
+        start_sin = jnp.where(after, sine_part[pl.ds(end, 1), :], start_sin)
+    cos_all[...] = cosine[...] * start_cos + sine_part[...] * start_sin
+    sin_all[...] = (sine_part[...] * start_cos - cosine[...] * start_sin) * lane_sign
+
+    def by_x(one, two):
+        low_half = lax.broadcasted_iota(jnp.int32, one.shape, 1) < part // 2
+        one_turned = pltpu.roll(one, part // 2, 1)
+        two_turned = pltpu.roll(two, part // 2, 1)
+        return (
+            jnp.where(low_half, one, two_turned).astype(jnp.bfloat16),
+            jnp.where(low_half, one_turned, two).astype(jnp.bfloat16),
+        )
+
+    for p in range(n_prompts):
+        down_copies[p].wait()
+        rows = slice(p * rank2, (p + 1) * rank2)
+        for quad in range(n_col // 4):
+            lanes = slice(quad * part, (quad + 1) * part)
+            for pair in range(2):
+                c = quad * 4 + pair
+                one = down_raw[p, c * rank2 : (c + 1) * rank2, :].astype(jnp.float32)
+                two = down_raw[p, (c + 2) * rank2 : (c + 3) * rank2, :].astype(jnp.float32)
+                even, odd = by_x(one, two)
+                down_x[2 * pair, rows, lanes] = even
+                down_x[2 * pair + 1, rows, lanes] = odd
+
     gain_copy.wait()
     for i in range(blocks):
         hidden_copies[i].wait()
         rows = slice(i * BLOCK, (i + 1) * BLOCK)
         squares = jnp.zeros((BLOCK, part), jnp.float32)
-        for c in range(n_col):
-            piece = hidden[c, rows, :].astype(jnp.float32)
-            squares = squares + piece * piece
+        for quad in range(n_col // 4):
+            lanes = slice(quad * part, (quad + 1) * part)
+            for pair in range(2):
+                c = quad * 4 + pair
+                one = hidden[c, rows, :].astype(jnp.float32)
+                two = hidden[c + 2, rows, :].astype(jnp.float32)
+                squares = squares + one * one + two * two
+                even, odd = by_x(
+                    one * gain[c, 0:1, :].astype(jnp.float32),
+                    two * gain[c + 2, 0:1, :].astype(jnp.float32),
+                )
+                gained_x[2 * pair, rows, lanes] = even
+                gained_x[2 * pair + 1, rows, lanes] = odd
         power = jnp.sum(squares, axis=1, keepdims=True) * (1.0 / width)
-        scale = lax.rsqrt(power + norm_eps)
-        for c in range(n_col):
-            piece = hidden[c, rows, :].astype(jnp.float32)
-            gain_row = gain[c, 0:1, :].astype(jnp.float32)
-            normed[rows, c * part : (c + 1) * part] = (piece * scale * gain_row).astype(
-                jnp.bfloat16
-            )
-    for p in range(n_prompts):
-        down_copies[p].wait()
-        for c in range(n_col):
-            down[p * rank2 : (p + 1) * rank2, c * part : (c + 1) * part] = down_raw[
-                p, c * rank2 : (c + 1) * rank2, :
-            ]
-    for k in range(X_SIZE):
-        weight_copies[k].wait()
-
-    tokens = normed[...]
-    weight_qkv = weights[:, :, :, 0 : 3 * HEAD_DIM].reshape(width, 3 * HEAD_DIM)
-    projected = jnp.dot(tokens, weight_qkv, preferred_element_type=jnp.float32)
-    lowrank = lax.dot_general(
-        tokens, down[...], (((1,), (1,)), ((), ())), preferred_element_type=jnp.float32
-    ).astype(jnp.bfloat16)
-
-    end_0 = lengths[0, 0]
-    end_1 = end_0 + lengths[0, 1]
-    end_2 = end_1 + lengths[0, 2]
+        row_scale[rows, :] = jnp.broadcast_to(lax.rsqrt(power + norm_eps), (BLOCK, HEAD_DIM))
+
+    unscaled = jnp.zeros((total_rows, n_prompts * rank2), jnp.float32)
+    for x in range(X_SIZE):
+        unscaled = unscaled + lax.dot_general(
+            gained_x[x], down_x[x], (((1,), (1,)), ((), ())), preferred_element_type=jnp.float32
+        )
+    lowrank = (unscaled * row_scale[...]).astype(jnp.bfloat16)
     place = lax.broadcasted_iota(jnp.int32, (total_rows, n_prompts * rank2), 0)
     segment = (
         (place >= end_0).astype(jnp.int32)
@@ -161,16 +176,49 @@
     in_prompt = (lane >= segment * rank2) & (lane < segment * rank2 + rank2)
     picked = jnp.where(in_prompt, lowrank.astype(jnp.float32), 0.0).astype(jnp.bfloat16)
     update = jnp.dot(picked, up_wide[...], preferred_element_type=jnp.float32)
-
     bias_wide = bias[...].astype(jnp.float32)
-    query_rows = projected[:, 0:HEAD_DIM] + bias_wide[0:1] + adapter_scale * update[:, 0:HEAD_DIM]
-    key_rows = projected[:, HEAD_DIM : 2 * HEAD_DIM] + bias_wide[1:2]
-    value_rows = (
-        projected[:, 2 * HEAD_DIM :] + bias_wide[2:3] + adapter_scale * update[:, HEAD_DIM:]
-    )
+    offset[:, 0:HEAD_DIM] = bias_wide[0:1] + adapter_scale * update[:, 0:HEAD_DIM]
+    offset[:, HEAD_DIM : 2 * HEAD_DIM] = jnp.broadcast_to(bias_wide[1:2], (total_rows, HEAD_DIM))
+    offset[:, 2 * HEAD_DIM :] = bias_wide[2:3] + adapter_scale * update[:, HEAD_DIM:]
+
+
+def block_kernel(
+    lengths,
+    pages,
+    x_place,
+    piece_0,
+    piece_1,
+    piece_2,
+    piece_3,
+    gained_x,
+    row_scale,
+    offset,
+    cosine,
+    sine_part,
+    attended,
+    cache,
+    keys,
+    values,
+):
+    total_rows = gained_x.shape[1]
+    inner = gained_x.shape[2]
+    blocks = total_rows // BLOCK
+    me = x_place[0]
+    unscaled = jnp.zeros(offset.shape, jnp.float32)
+    for k, piece in enumerate((piece_0, piece_1, piece_2, piece_3)):
+        source = lax.rem(me + (X_SIZE - k), X_SIZE)
+        unscaled = unscaled + jnp.dot(
+            gained_x[source],
+            piece[:, :, 0 : 3 * HEAD_DIM].reshape(inner, 3 * HEAD_DIM),
+            preferred_element_type=jnp.float32,
+        )
+    scale = row_scale[...]
+    query_rows = unscaled[:, 0:HEAD_DIM] * scale + offset[:, 0:HEAD_DIM]
+    key_rows = unscaled[:, HEAD_DIM : 2 * HEAD_DIM] * scale + offset[:, HEAD_DIM : 2 * HEAD_DIM]
+    value_rows = unscaled[:, 2 * HEAD_DIM :] * scale + offset[:, 2 * HEAD_DIM :]
+    half = HEAD_DIM // 2
     cos_all = cosine[...]
     sin_all = sine_part[...]
-    half = HEAD_DIM // 2
     queries = (query_rows * cos_all + pltpu.roll(query_rows, half, 1) * sin_all).astype(
         jnp.bfloat16
     )
@@ -181,6 +229,9 @@
         cache[to, 0] = keys[page * PAGE : (page + 1) * PAGE, :]
         cache[to, 1] = values[page * PAGE : (page + 1) * PAGE, :]
 
+    end_0 = lengths[0, 0]
+    end_1 = end_0 + lengths[0, 1]
+    end_2 = end_1 + lengths[0, 2]
     factor = HEAD_DIM ** (-0.5)
     reach = LONGEST // BLOCK
     for i in range(blocks):
@@ -206,13 +257,40 @@
             probs, values[low:high, :], preferred_element_type=jnp.float32
         ).astype(jnp.bfloat16)
 
-    weight_out = weights[:, :, :, 3 * HEAD_DIM :].reshape(width, HEAD_DIM)
+
+def output_kernel(
+    x_place, piece_0, piece_1, piece_2, piece_3, attended, out, out_weights, sem
+):
+    me = x_place[0]
+    copies = []
+    for k, piece in enumerate((piece_0, piece_1, piece_2, piece_3)):
+        source = lax.rem(me + (X_SIZE - k), X_SIZE)
+        piece = piece.at[:, :, pl.ds(piece.shape[2] - HEAD_DIM, HEAD_DIM)]
+        copies.append(pltpu.make_async_copy(piece, out_weights.at[:, source], sem.at[k]))
+        copies[k].start()
+    for k in range(X_SIZE):
+        copies[k].wait()
+    width = out.shape[3]
+    weight_out = out_weights[...].reshape(width, HEAD_DIM)
     partial = lax.dot_general(
         attended[...], weight_out, (((1,), (1,)), ((), ())), preferred_element_type=jnp.float32
     ).astype(jnp.bfloat16)
     out_rows = out.shape[2]
-    for b in range(n_col):
+    for b in range(2 * out.shape[1]):
         out[b % 2, b // 2] = partial[b * out_rows : (b + 1) * out_rows, :]
+
+
+def rotary_tables(rows):
+    half = HEAD_DIM // 2
+    inverse_freq = np.float32(rope_base) ** (
+        -(np.arange(half, dtype=np.float32) * np.float32(2.0) / np.float32(HEAD_DIM))
+    )
+    angles = (
+        np.arange(rows, dtype=np.float32)[:, None] * inverse_freq.astype(np.float32)[None, :]
+    ).astype(np.float64)
+    cosine = np.concatenate([np.cos(angles)] * 2, axis=1).astype(np.float32)
+    sine_part = np.concatenate([np.sin(angles)] * 2, axis=1).astype(np.float32)
+    return jnp.asarray(cosine), jnp.asarray(sine_part)
 
 
 def make_body(n_row, n_col):
@@ -255,72 +333,98 @@
             name="payload",
         )(incoming_hidden, input_norm_weight, adapter_down_weight.reshape(rank2, width))
         gathered = lax.all_gather(payload, "col", axis=0, tiled=False)
-        copies = pl.pallas_call(
+        weight_copies = pl.pallas_call(
             weight_copies_kernel,
             out_shape=jax.ShapeDtypeStruct((n_z, row_part, 4 * head_cols), jnp.bfloat16),
             name="weight_copies",
         )(query_key_value_weight, output_weight.T)
-        over_z = lax.all_to_all(copies, "row", 0, 0, tiled=False, axis_index_groups=z_groups)
-        pieces = [over_z] + [lax.ppermute(over_z, "row", x_shift(k)) for k in range(1, X_SIZE)]
-
-        lengths = prompt_length_list[0]
-        places = jnp.arange(total_rows, dtype=jnp.int32)
-        ends = jnp.cumsum(lengths)
-        start = jnp.zeros_like(places)
-        for p in range(n_prompts - 1):
-            start = jnp.where(places >= ends[p], ends[p], start)
-        position = (places - start).astype(jnp.float32)
-        half = HEAD_DIM // 2
-        inverse_freq = rope_base ** (-(jnp.arange(half, dtype=jnp.float32) * 2.0 / HEAD_DIM))
-        angles = position[:, None] * inverse_freq[None, :]
-        cos_half = jnp.cos(angles)
-        sin_half = jnp.sin(angles)
-        cosine = jnp.concatenate([cos_half, cos_half], axis=1)
-        sine_part = jnp.concatenate([-sin_half, sin_half], axis=1)
+        over_z = lax.all_to_all(weight_copies, "row", 0, 0, tiled=False, axis_index_groups=z_groups)
+        own_qkv = over_z[:, :, : 3 * head_cols]
+        own_out = over_z[:, :, 3 * head_cols :]
+        pieces, out_pieces = [over_z] * X_SIZE, [over_z] * X_SIZE
+        for k in (1, 3, 2):
+            if k == 1:
+                pieces[k] = out_pieces[k] = lax.ppermute(over_z, "row", x_shift(k))
+            else:
+                pieces[k] = lax.ppermute(own_qkv, "row", x_shift(k))
+                out_pieces[k] = lax.ppermute(own_out, "row", x_shift(k))
+
+        cosine, sine_part = rotary_tables(total_rows)
         x_place = lax.rem(lax.axis_index("row"), X_SIZE).astype(jnp.int32).reshape(1)
 
         whole = pl.BlockSpec(memory_space=VMEM)
         scalar = pl.BlockSpec(memory_space=SMEM)
         raw = pl.BlockSpec(memory_space=pl.ANY)
-        partial, cache = pl.pallas_call(
-            block_kernel,
+        gained_x, row_scale, offset, cos_all, sin_all = pl.pallas_call(
+            norm_kernel,
             out_shape=(
-                jax.ShapeDtypeStruct((2, n_col // 2, out_rows, width), jnp.bfloat16),
-                jax.ShapeDtypeStruct((total_rows // PAGE, 2, PAGE, head_cols), jnp.bfloat16),
+                jax.ShapeDtypeStruct((X_SIZE, total_rows, width // X_SIZE), jnp.bfloat16),
+                jax.ShapeDtypeStruct((total_rows, head_cols), jnp.float32),
+                jax.ShapeDtypeStruct((total_rows, 3 * head_cols), jnp.float32),
+                jax.ShapeDtypeStruct((total_rows, head_cols), jnp.float32),
+                jax.ShapeDtypeStruct((total_rows, head_cols), jnp.float32),
             ),
-            in_specs=[scalar] * 5 + [raw] * 5 + [whole] * 4,
-            out_specs=(whole, whole),
+            in_specs=[scalar] * 3 + [pl.BlockSpec(memory_space=HBM)] + [whole] * 4,
+            out_specs=(whole,) * 5,
             scratch_shapes=[
                 pltpu.VMEM((n_col, total_rows, part), jnp.bfloat16),
                 pltpu.VMEM((n_col, GAIN_ROWS, part), jnp.bfloat16),
                 pltpu.VMEM((n_prompts, n_col * rank2, part), jnp.bfloat16),
-                pltpu.VMEM((n_z, X_SIZE, row_part, 4 * head_cols), jnp.bfloat16),
-                pltpu.VMEM((total_rows, width), jnp.bfloat16),
-                pltpu.VMEM((n_prompts * rank2, width), jnp.bfloat16),
+                pltpu.VMEM((X_SIZE, n_prompts * rank2, width // X_SIZE), jnp.bfloat16),
                 pltpu.VMEM((n_prompts * rank2, 2 * head_cols), jnp.bfloat16),
-                pltpu.VMEM((total_rows, head_cols), jnp.bfloat16),
-                pltpu.VMEM((total_rows, head_cols), jnp.bfloat16),
-                pltpu.VMEM((total_rows, head_cols), jnp.bfloat16),
                 pltpu.SemaphoreType.DMA((total_rows // BLOCK,)),
                 pltpu.SemaphoreType.DMA((1,)),
                 pltpu.SemaphoreType.DMA((n_prompts,)),
-                pltpu.SemaphoreType.DMA((X_SIZE,)),
             ],
-            compiler_params=pltpu.CompilerParams(vmem_limit_bytes=48 * 1024 * 1024),
-            name="attention_block",
+            compiler_params=pltpu.CompilerParams(vmem_limit_bytes=32 * 1024 * 1024),
+            name="norm_and_adapters",
         )(
             slot_of_adapter,
             adapter_of_prompt,
             prompt_length_list,
-            cache_page_index,
-            x_place,
-            gathered,
-            *pieces,
+            pltpu.with_memory_space_constraint(gathered, HBM),
             query_key_value_bias,
             adapter_up_weight,
             cosine,
             sine_part,
         )
+        attended, cache = pl.pallas_call(
+            block_kernel,
+            out_shape=(
+                jax.ShapeDtypeStruct((total_rows, head_cols), jnp.bfloat16),
+                jax.ShapeDtypeStruct((total_rows // PAGE, 2, PAGE, head_cols), jnp.bfloat16),
+            ),
+            in_specs=[scalar] * 3 + [whole] * 9,
+            out_specs=(whole, whole),
+            scratch_shapes=[
+                pltpu.VMEM((total_rows, head_cols), jnp.bfloat16),
+                pltpu.VMEM((total_rows, head_cols), jnp.bfloat16),
+            ],
+            compiler_params=pltpu.CompilerParams(vmem_limit_bytes=32 * 1024 * 1024),
+            name="attention_block",
+        )(
+            prompt_length_list,
+            cache_page_index,
+            x_place,
+            *pieces,
+            gained_x,
+            row_scale,
+            offset,
+            cos_all,
+            sin_all,
+        )
+        partial = pl.pallas_call(
+            output_kernel,
+            out_shape=jax.ShapeDtypeStruct((2, n_col // 2, out_rows, width), jnp.bfloat16),
+            in_specs=[scalar] + [raw] * X_SIZE + [whole],
+            out_specs=whole,
+            scratch_shapes=[
+                pltpu.VMEM((n_z, X_SIZE, row_part, head_cols), jnp.bfloat16),
+                pltpu.SemaphoreType.DMA((X_SIZE,)),
+            ],
+            compiler_params=pltpu.CompilerParams(vmem_limit_bytes=32 * 1024 * 1024),
+            name="output_projection",
+        )(x_place, *out_pieces, attended)
         pair = lax.all_to_all(partial, "col", 0, 0, tiled=False, axis_index_groups=pair_groups)
         pair_sum = (pair[0].astype(jnp.float32) + pair[1].astype(jnp.float32)).astype(jnp.bfloat16)
         terms = lax.all_to_all(pair_sum, "col", 0, 0, tiled=False, axis_index_groups=y_groups)

time: 129 us -> 119 us (0.922)
  waiting for transfers between devices: 37.6 us -> 7.44 us
  blocking collectives: 40.1 us -> 67 us
  starting transfers between devices: 20.2 us -> 15.9 us
  other arithmetic: 4.5 us -> 1.21 us
    all_to_all x0 -> x1, blocking collectives: none -> 26.9 us  [body(): lax.all_to_all(weight_copies, 'row', 0, 0, tiled=False, axis_index_groups...]
    ppermute x3 -> x5, waiting for transfers between devices: 20.4 us -> 0.01 us  [the longest x2 0.01 us: body(): pieces[k] = lax.ppermute(own_qkv, 'row', x_shift(k))]
    all_to_all x1 -> x0, waiting for transfers between devices: 17.2 us -> none  [body(): lax.all_to_all(copies, 'row', 0, 0, tiled=False, axis_index_groups=z_groups)]
    all_to_all x1 -> x0, starting transfers between devices: 10.9 us -> none  [body(): lax.all_to_all(copies, 'row', 0, 0, tiled=False, axis_index_groups=z_groups)]
    all_gather x1, waiting for transfers between devices: 0.01 us -> 7.41 us  [body(): gathered = lax.all_gather(payload, 'col', axis=0, tiled=False)]
    ppermute x3 -> x5, starting transfers between devices: 9.32 us -> 15.8 us  [the longest x2 6.82 us: body(): pieces[k] = lax.ppermute(own_qkv, 'row', x_shift(k))]
    convert_element_type x1 -> x0, other arithmetic: 1.91 us -> none  [body(): position = (places - start).astype(jnp.float32)]
    pallas_call x1 -> x3, Pallas kernels: 8 us -> 8.25 us  [the longest x1 4.23 us: body(): pl.pallas_call(norm_kernel, out_shape=(jax.ShapeDtypeStruct((X_SIZE, tota...]
  transfers between devices with their start and end apart: 5 -> 6, of which waited for: 4 -> 1; matrix products, arithmetic and copies ran while one was open for 3% -> 0% of each run, Pallas kernels for 1% -> 8%
where the time goes in v3:
time: 119 us; the launch traced here: 118 us
  blocking collectives  67 us (56%)
  starting transfers between devices  15.9 us (13%)
  between operations  14.2 us (12%)
  Pallas kernels  11.8 us (10%)
  waiting for transfers between devices  7.44 us (6%)
  other arithmetic  1.21 us (1%)
    all_to_all x1, blocking collectives, body(): lax.all_to_all(pair_sum, 'col', 0, 0, tiled=False, axis_index_groups=y_gr...  34.6 us
    all_to_all x1, blocking collectives, body(): lax.all_to_all(weight_copies, 'row', 0, 0, tiled=False, axis_index_groups...  26.9 us
    all_gather x1, waiting for transfers between devices, body(): gathered = lax.all_gather(payload, 'col', axis=0, tiled=False)  7.41 us
    ppermute x2, starting transfers between devices, body(): pieces[k] = lax.ppermute(own_qkv, 'row', x_shift(k))  6.82 us
    ppermute x2, starting transfers between devices, body(): out_pieces[k] = lax.ppermute(own_out, 'row', x_shift(k))  5.92 us
    all_to_all x1, blocking collectives, body(): lax.all_to_all(partial, 'col', 0, 0, tiled=False, axis_index_groups=pair_...  5.58 us
    pallas_call x1, Pallas kernels, body(): pl.pallas_call(norm_kernel, out_shape=(jax.ShapeDtypeStruct((X_SIZE, tota...  4.23 us
    pallas_call x1, Pallas kernels, body(): pl.pallas_call(block_kernel, out_shape=(jax.ShapeDtypeStruct((total_rows,...  3.16 us
  transfers between devices with their start and end apart: 6, of which 1 were waited for; matrix products, arithmetic and copies ran while one was open for 0% of the time, Pallas kernels for 8%

profile of v3, /device:TPU:1, one launch (start us, length us, event | category | flops | bytes accessed | tf_op | source)
XLA Modules:
  0.0 117.6 jit_solution(9235693899424746343)
XLA Ops:
  7.2 0.0 copy-start
  7.2 0.0 copy-start.1
  7.2 0.0 all-gather.3.cloned.1.call-start
  7.3 1.8 %payload.1 = bf16[1040,128]{1,0:T(8,128)(2,1)} custom-call(bf16[512,128]{1,0:T(8,128)(2,1)} %hidden.1, bf16[1,128]{1,0:T(2,128)(2,1)} %gain.1, bf16[32,2048]{1,0:T(8,128)(2,1)} %bitcast.7), custom_call_target="tpu_custom_call" | custom-call | tf_op jit(solution)/shard_map/payload/pallas_call | solution.py:330
  9.1 0.0 all-gather.3.cloned.1.call-update
  9.1 1.7 %weight_copies.1 = bf16[8,64,512]{2,1,0:T(8,128)(2,1)} custom-call(bf16[3,64,128]{2,1,0:T(8,128)(2,1)} %qkv.1, bf16[64,128]{1,0:T(8,128)(2,1)} %bitcast.8), custom_call_target="tpu_custom_call" | custom-call | tf_op jit(solution)/shard_map/weight_copies/pallas_call | solution.py:336
  10.8 26.9 %all_to_all.15.piece_0 = bf16[8,64,512]{2,1,0:T(8,128)(2,1)S(1)} all-to-all(bf16[8,64,512]{2,1,0:T(8,128)(2,1)} %weight_copies.1), channel_id=1, replica_groups={{0,64,128,192,256,320,384,448},{16,80,144,208,272,336,400,464},{32,96,1..., dimensions={0} | all-to-all | bytes 1048576 | tf_op jit(solution)/shard_map/all_to_all | solution.py:341
  37.7 3.1 %collective-permute-start = (bf16[8,64,512]{2,1,0:T(8,128)(2,1)S(1)}, bf16[8,64,512]{2,1,0:T(8,128)(2,1)S(1)}, u32[]{:S(2)}, u32[]{:S(2)}) collective-permute-start(bf16[8,64,512]{2,1,0:T(8,128)(2,1)S(1)} %all_to_all.15.piece_0), channel_id=1, source_target_pairs={{0,16},{16,32},{32,48},{48,0},{64,80},{80,96},{96,112},{112,64},{1... | collective-permute-start | bytes 1572872 | tf_op jit(solution)/shard_map/ppermute | solution.py:347
  40.8 3.4 %collective-permute-start.4 = (bf16[8,64,384]{2,1,0:T(8,128)(2,1)S(1)}, bf16[8,64,384]{2,1,0:T(8,128)(2,1)S(1)}, u32[]{:S(2)}, u32[]{:S(2)}) collective-permute-start(bf16[8,64,384]{2,1,0:T(8,128)(2,1)S(1)} %slice.17), channel_id=1, source_target_pairs={{0,48},{16,0},{32,16},{48,32},{64,112},{80,64},{96,80},{112,96},{1... | collective-permute-start | bytes 1179656 | tf_op jit(solution)/shard_map/ppermute | solution.py:349
  44.2 3.4 %collective-permute-start.3 = (bf16[8,64,384]{2,1,0:T(8,128)(2,1)S(1)}, bf16[8,64,384]{2,1,0:T(8,128)(2,1)S(1)}, u32[]{:S(2)}, u32[]{:S(2)}) collective-permute-start(bf16[8,64,384]{2,1,0:T(8,128)(2,1)S(1)} %slice.17), channel_id=1, source_target_pairs={{0,32},{16,48},{32,0},{48,16},{64,96},{80,112},{96,64},{112,80},{1... | collective-permute-start | bytes 1179656 | tf_op jit(solution)/shard_map/ppermute | solution.py:349
  47.7 2.8 %collective-permute-start.2 = (bf16[8,64,128]{2,1,0:T(8,128)(2,1)S(1)}, bf16[8,64,128]{2,1,0:T(8,128)(2,1)S(1)}, u32[]{:S(2)}, u32[]{:S(2)}) collective-permute-start(bf16[8,64,128]{2,1,0:T(8,128)(2,1)S(1)} %slice.16), channel_id=1, source_target_pairs={{0,48},{16,0},{32,16},{48,32},{64,112},{80,64},{96,80},{112,96},{1... | collective-permute-start | bytes 393224 | tf_op jit(solution)/shard_map/ppermute | solution.py:350
  50.5 3.1 %collective-permute-start.1 = (bf16[8,64,128]{2,1,0:T(8,128)(2,1)S(1)}, bf16[8,64,128]{2,1,0:T(8,128)(2,1)S(1)}, u32[]{:S(2)}, u32[]{:S(2)}) collective-permute-start(bf16[8,64,128]{2,1,0:T(8,128)(2,1)S(1)} %slice.16), channel_id=1, source_target_pairs={{0,32},{16,48},{32,0},{48,16},{64,96},{80,112},{96,64},{112,80},{1... | collective-permute-start | bytes 393224 | tf_op jit(solution)/shard_map/ppermute | solution.py:350
  53.6 7.4 %all-gather.3.cloned.1.call-done = bf16[16640,128]{1,0:T(8,128)(2,1)} async-done(((bf16[1040,128]{1,0:T(8,128)(2,1)}), bf16[16640,128]{1,0:T(8,128)(2,1)}) %all-gather.3.cloned.1.call-update) | async-done | bytes 4259856 | tf_op jit(solution)/shard_map/all_gather | solution.py:335
  61.1 0.0 copy-start.7
  61.1 4.2 %norm_and_adapters.1 = (bf16[4,512,512]{2,1,0:T(8,128)(2,1)S(1)}, f32[512,128]{1,0:T(8,128)S(1)}, f32[512,384]{1,0:T(8,128)S(1)}, f32[512,128]{1,0:T(8,128)S(1)}, f32[512,128]{1,0:T(8,128)S(1)}) custom-call(s32[16]{0:T(128)S(1)} %copy-done.5, s32[1,4]{1,0:T(1,128)S(1)} %copy-done.6, s32[1,4]{1,0:T(1,128)S(1)} %copy-done.3, bf16[16,1040,128]{2,1,0:T(8,128)(2,1)} %bitcast.6, ...), custom_call_target="tpu_custom_call" | custom-call | tf_op jit(solution)/shard_map/norm_and_adapters/pallas_call | solution.py:358
  65.3 0.0 collective-permute-done.4.piece_3
  65.4 0.0 collective-permute-done.3.piece_2
  65.4 0.0 collective-permute-done.piece_1
  65.4 3.2 %attention_block.1 = (bf16[512,128]{1,0:T(8,128)(2,1)S(1)}, bf16[32,2,16,128]{3,2,1,0:T(8,128)(2,1)}) custom-call(s32[1,4]{1,0:T(1,128)S(1)} %copy-done.3, s32[1,32]{1,0:T(1,128)S(1)} %copy-done.7, s32[1]{0:T(128)} %bitcast.x_place, bf16[8,64,512]{2,1,0:T(8,128)(2,1)S(1)} %all_to_all.15.piece_0, bf16[8,64,512]{2,1,0:T(8,128)(2,1)S(1)} %collective-permute-done.piece_1, ...), custom_call_target="tpu_custom_call" | custom-call | tf_op jit(solution)/shard_map/attention_block/pallas_call | solution.py:391
  68.6 0.9 output_projection.1
  69.4 5.6 %all_to_all.16 = bf16[2,8,32,2048]{3,2,1,0:T(8,128)(2,1)S(1)} all-to-all(bf16[2,8,32,2048]{3,2,1,0:T(8,128)(2,1)S(1)} %output_projection.1), channel_id=1, replica_groups={{0,1},{2,3},{4,5},{6,7},{8,9},{10,11},{12,13},{14,15},{16,17},{18,19},{..., dimensions={0} | all-to-all | bytes 4194304 | tf_op jit(solution)/shard_map/all_to_all | solution.py:428
  75.0 0.4 fusion
  75.4 34.6 %all_to_all.17 = bf16[8,32,2048]{2,1,0:T(8,128)(2,1)S(1)} all-to-all(bf16[8,32,2048]{2,1,0:T(8,128)(2,1)S(1)} %fusion), channel_id=1, replica_groups={{0,2,4,6,8,10,12,14},{1,3,5,7,9,11,13,15},{16,18,20,22,24,26,28,30},{17..., dimensions={0} | all-to-all | bytes 2097152 | tf_op jit(solution)/shard_map/all_to_all | solution.py:430
  110.0 0.8 reduce_sum.12
  (17 shorter events, 0.1 us)
Async XLA Ops:
  7.2 53.9 %copy-start = (f32[512,128]{1,0:T(8,128)S(1)}, f32[512,128]{1,0:T(8,128)}, u32[]{:S(2)}) copy-start(f32[512,128]{1,0:T(8,128)} %constant.19.clone.sine_part) | copy-start | bytes 786436
  7.2 53.9 %copy-start.1 = (f32[512,128]{1,0:T(8,128)S(1)}, f32[512,128]{1,0:T(8,128)}, u32[]{:S(2)}) copy-start(f32[512,128]{1,0:T(8,128)} %constant.18.clone.cosine) | copy-start | bytes 786436
  7.2 53.9 %copy-start.3 = (s32[1,4]{1,0:T(1,128)S(1)}, s32[1,4]{1,0:T(1,128)}, u32[]{:S(2)}) copy-start(s32[1,4]{1,0:T(1,128)} %lengths.3) | copy-start | bytes 52
  7.2 53.9 %copy-start.6 = (s32[1,4]{1,0:T(1,128)S(1)}, s32[1,4]{1,0:T(1,128)}, u32[]{:S(2)}) copy-start(s32[1,4]{1,0:T(1,128)} %adapters.1) | copy-start | bytes 52
  7.2 53.9 %copy-start.5 = (s32[16]{0:T(128)S(1)}, s32[16]{0:T(128)}, u32[]{:S(2)}) copy-start(s32[16]{0:T(128)} %slots.1) | copy-start | bytes 196
  7.2 53.9 %copy-start.2 = (bf16[16,2,16,128]{3,2,1,0:T(8,128)(2,1)S(1)}, bf16[16,2,16,128]{3,2,1,0:T(8,128)(2,1)}, u32[]{:S(2)}) copy-start(bf16[16,2,16,128]{3,2,1,0:T(8,128)(2,1)} %up.1) | copy-start | bytes 393220
  7.2 53.9 %copy-start.4 = (bf16[3,128]{1,0:T(4,128)(2,1)S(1)}, bf16[3,128]{1,0:T(4,128)(2,1)}, u32[]{:S(2)}) copy-start(bf16[3,128]{1,0:T(4,128)(2,1)} %bias.1) | copy-start | bytes 2308
  7.2 53.8 %all-gather.3.cloned.1.call-start = ((), (), s32[]{:S(2)}) async-start(), calls=%async_computation.3 | async-start | bytes 4526080 | tf_op jit(solution)/shard_map/all_gather | solution.py:335
  37.7 27.7 %collective-permute-start = (bf16[8,64,512]{2,1,0:T(8,128)(2,1)S(1)}, bf16[8,64,512]{2,1,0:T(8,128)(2,1)S(1)}, u32[]{:S(2)}, u32[]{:S(2)}) collective-permute-start(bf16[8,64,512]{2,1,0:T(8,128)(2,1)S(1)} %all_to_all.15.piece_0), channel_id=1, source_target_pairs={{0,16},{16,32},{32,48},{48,0},{64,80},{80,96},{96,112},{112,64},{1... | collective-permute-start | bytes 1572872 | tf_op jit(solution)/shard_map/ppermute | solution.py:347
  40.8 24.5 %collective-permute-start.4 = (bf16[8,64,384]{2,1,0:T(8,128)(2,1)S(1)}, bf16[8,64,384]{2,1,0:T(8,128)(2,1)S(1)}, u32[]{:S(2)}, u32[]{:S(2)}) collective-permute-start(bf16[8,64,384]{2,1,0:T(8,128)(2,1)S(1)} %slice.17), channel_id=1, source_target_pairs={{0,48},{16,0},{32,16},{48,32},{64,112},{80,64},{96,80},{112,96},{1... | collective-permute-start | bytes 1179656 | tf_op jit(solution)/shard_map/ppermute | solution.py:349
  44.2 21.1 %collective-permute-start.3 = (bf16[8,64,384]{2,1,0:T(8,128)(2,1)S(1)}, bf16[8,64,384]{2,1,0:T(8,128)(2,1)S(1)}, u32[]{:S(2)}, u32[]{:S(2)}) collective-permute-start(bf16[8,64,384]{2,1,0:T(8,128)(2,1)S(1)} %slice.17), channel_id=1, source_target_pairs={{0,32},{16,48},{32,0},{48,16},{64,96},{80,112},{96,64},{112,80},{1... | collective-permute-start | bytes 1179656 | tf_op jit(solution)/shard_map/ppermute | solution.py:349
  47.7 20.8 %collective-permute-start.2 = (bf16[8,64,128]{2,1,0:T(8,128)(2,1)S(1)}, bf16[8,64,128]{2,1,0:T(8,128)(2,1)S(1)}, u32[]{:S(2)}, u32[]{:S(2)}) collective-permute-start(bf16[8,64,128]{2,1,0:T(8,128)(2,1)S(1)} %slice.16), channel_id=1, source_target_pairs={{0,48},{16,0},{32,16},{48,32},{64,112},{80,64},{96,80},{112,96},{1... | collective-permute-start | bytes 393224 | tf_op jit(solution)/shard_map/ppermute | solution.py:350
  50.5 18.1 %collective-permute-start.1 = (bf16[8,64,128]{2,1,0:T(8,128)(2,1)S(1)}, bf16[8,64,128]{2,1,0:T(8,128)(2,1)S(1)}, u32[]{:S(2)}, u32[]{:S(2)}) collective-permute-start(bf16[8,64,128]{2,1,0:T(8,128)(2,1)S(1)} %slice.16), channel_id=1, source_target_pairs={{0,32},{16,48},{32,0},{48,16},{64,96},{80,112},{96,64},{112,80},{1... | collective-permute-start | bytes 393224 | tf_op jit(solution)/shard_map/ppermute | solution.py:350
  61.1 4.3 %copy-start.7 = (s32[1,32]{1,0:T(1,128)S(1)}, s32[1,32]{1,0:T(1,128)}, u32[]{:S(2)}) copy-start(s32[1,32]{1,0:T(1,128)} %pages.1) | copy-start | bytes 388
Sparse Core Ops, SparseCore 0:
  10.2 50.8 all-gather.2

commit v4 on v3

--- a/solution.py
+++ b/solution.py
@@ -22,24 +22,21 @@
 HBM = pltpu.MemorySpace.HBM
 
 
-def payload_kernel(hidden, gain, down, out):
+def outgoing_kernel(hidden, gain, down, qkv, out_weight_t, payload, copies):
     rows, part = hidden.shape
     rank2 = down.shape[0]
-    out[0:rows, :] = hidden[...]
+    payload[0:rows, :] = hidden[...]
     for block in range(down.shape[1] // part):
-        out[rows + block * rank2 : rows + (block + 1) * rank2, :] = down[
+        payload[rows + block * rank2 : rows + (block + 1) * rank2, :] = down[
             :, block * part : (block + 1) * part
         ]
     wide = jnp.broadcast_to(gain[...].astype(jnp.float32), (GAIN_ROWS, part))
-    out[out.shape[0] - GAIN_ROWS :, :] = wide.astype(jnp.bfloat16)
-
-
-def weight_copies_kernel(qkv, out_weight_t, out):
+    payload[payload.shape[0] - GAIN_ROWS :, :] = wide.astype(jnp.bfloat16)
     cols = qkv.shape[2]
-    for copy in range(out.shape[0]):
+    for copy in range(copies.shape[0]):
         for i in range(3):
-            out[copy, :, i * cols : (i + 1) * cols] = qkv[i]
-        out[copy, :, 3 * cols :] = out_weight_t[...]
+            copies[copy, :, i * cols : (i + 1) * cols] = qkv[i]
+        copies[copy, :, 3 * cols :] = out_weight_t[...]
 
 
 def norm_kernel(
@@ -56,66 +53,58 @@
     offset,
     cos_all,
     sin_all,
-    hidden,
-    gain,
-    down_raw,
+    received,
     down_x,
     up_wide,
-    sem_hidden,
-    sem_gain,
-    sem_down,
+    in_prompt,
+    sem_quad,
 ):
-    n_col, total_rows, part = hidden.shape
+    n_col, received_rows, part = received.shape
+    total_rows = row_scale.shape[0]
     width = n_col * part
-    n_prompts = down_raw.shape[0]
-    rank2 = down_raw.shape[1] // n_col
+    n_prompts = lengths.shape[1]
+    rank2 = (received_rows - total_rows - GAIN_ROWS) // n_col
     rank = rank2 // 2
-    blocks = total_rows // BLOCK
-
-    gain_copy = pltpu.make_async_copy(
-        gathered.at[:, pl.ds(gathered.shape[1] - GAIN_ROWS, GAIN_ROWS)], gain, sem_gain.at[0]
-    )
-    gain_copy.start()
-    hidden_copies = []
-    for i in range(blocks):
-        rows = pl.ds(i * BLOCK, BLOCK)
-        hidden_copies.append(
-            pltpu.make_async_copy(gathered.at[:, rows], hidden.at[:, rows], sem_hidden.at[i])
-        )
-        hidden_copies[i].start()
+    gain_row = received_rows - GAIN_ROWS
+
+    quads = n_col // 4
+    quad_copies = []
+    for q in range(quads):
+        four = pl.ds(q * 4, 4)
+        quad_copies.append(
+            pltpu.make_async_copy(gathered.at[four], received.at[four], sem_quad.at[q])
+        )
+        quad_copies[q].start()
     prompt_slots = [slots[adapters[0, p]] for p in range(n_prompts)]
-    down_copies = []
-    for p in range(n_prompts):
-        down_copies.append(
-            pltpu.make_async_copy(
-                gathered.at[prompt_slots[p], pl.ds(total_rows, n_col * rank2)],
-                down_raw.at[p],
-                sem_down.at[p],
-            )
-        )
-        down_copies[p].start()
 
     up_wide[...] = jnp.zeros_like(up_wide)
     for p in range(n_prompts):
         first = p * rank2
         up_wide[first : first + rank, 0:HEAD_DIM] = up[prompt_slots[p], 0]
         up_wide[first + rank : first + rank2, HEAD_DIM:] = up[prompt_slots[p], 1]
-
     end_0 = lengths[0, 0]
     end_1 = end_0 + lengths[0, 1]
     end_2 = end_1 + lengths[0, 2]
-    place_wide = lax.broadcasted_iota(jnp.int32, (total_rows, HEAD_DIM), 0)
-    lane_sign = jnp.where(
-        lax.broadcasted_iota(jnp.int32, (1, HEAD_DIM), 1) < HEAD_DIM // 2, -1.0, 1.0
-    )
+    place = lax.broadcasted_iota(jnp.int32, (total_rows, HEAD_DIM), 0)
+    lane = lax.broadcasted_iota(jnp.int32, (total_rows, HEAD_DIM), 1)
+    lane_sign = jnp.where(lane[0:1] < HEAD_DIM // 2, -1.0, 1.0)
     start_cos = jnp.ones((total_rows, HEAD_DIM), jnp.float32)
     start_sin = jnp.zeros((total_rows, HEAD_DIM), jnp.float32)
     for end in (end_0, end_1, end_2):
-        after = place_wide >= end
+        after = place >= end
         start_cos = jnp.where(after, cosine[pl.ds(end, 1), :], start_cos)
         start_sin = jnp.where(after, sine_part[pl.ds(end, 1), :], start_sin)
     cos_all[...] = cosine[...] * start_cos + sine_part[...] * start_sin
     sin_all[...] = (sine_part[...] * start_cos - cosine[...] * start_sin) * lane_sign
+    segment = (
+        (place >= end_0).astype(jnp.int32)
+        + (place >= end_1).astype(jnp.int32)
+        + (place >= end_2).astype(jnp.int32)
+    )
+    chosen = (lane >= segment * rank2) & (lane < segment * rank2 + rank2)
+    in_prompt[...] = jnp.where(chosen, 1.0, 0.0)
+    bias_wide = bias[...].astype(jnp.float32)
+    offset[:, HEAD_DIM : 2 * HEAD_DIM] = jnp.broadcast_to(bias_wide[1:2], (total_rows, HEAD_DIM))
 
     def by_x(one, two):
         low_half = lax.broadcasted_iota(jnp.int32, one.shape, 1) < part // 2
@@ -126,59 +115,45 @@
             jnp.where(low_half, one_turned, two).astype(jnp.bfloat16),
         )
 
-    for p in range(n_prompts):
-        down_copies[p].wait()
-        rows = slice(p * rank2, (p + 1) * rank2)
-        for quad in range(n_col // 4):
-            lanes = slice(quad * part, (quad + 1) * part)
-            for pair in range(2):
-                c = quad * 4 + pair
-                one = down_raw[p, c * rank2 : (c + 1) * rank2, :].astype(jnp.float32)
-                two = down_raw[p, (c + 2) * rank2 : (c + 3) * rank2, :].astype(jnp.float32)
-                even, odd = by_x(one, two)
-                down_x[2 * pair, rows, lanes] = even
-                down_x[2 * pair + 1, rows, lanes] = odd
-
-    gain_copy.wait()
-    for i in range(blocks):
-        hidden_copies[i].wait()
-        rows = slice(i * BLOCK, (i + 1) * BLOCK)
-        squares = jnp.zeros((BLOCK, part), jnp.float32)
-        for quad in range(n_col // 4):
-            lanes = slice(quad * part, (quad + 1) * part)
-            for pair in range(2):
-                c = quad * 4 + pair
-                one = hidden[c, rows, :].astype(jnp.float32)
-                two = hidden[c + 2, rows, :].astype(jnp.float32)
-                squares = squares + one * one + two * two
-                even, odd = by_x(
-                    one * gain[c, 0:1, :].astype(jnp.float32),
-                    two * gain[c + 2, 0:1, :].astype(jnp.float32),
-                )
+    for q in range(quads):
+        quad_copies[q].wait()
+        lanes = slice(q * part, (q + 1) * part)
+        for pair in range(2):
+            c = q * 4 + pair
+            gain_one = received[c, gain_row : gain_row + 1, :].astype(jnp.float32)
+            gain_two = received[c + 2, gain_row : gain_row + 1, :].astype(jnp.float32)
+            for i in range(total_rows // BLOCK):
+                rows = slice(i * BLOCK, (i + 1) * BLOCK)
+                one = received[c, rows, :].astype(jnp.float32)
+                two = received[c + 2, rows, :].astype(jnp.float32)
+                squares = one * one + two * two
+                row_scale[rows, :] = squares if c == 0 else row_scale[rows, :] + squares
+                even, odd = by_x(one * gain_one, two * gain_two)
                 gained_x[2 * pair, rows, lanes] = even
                 gained_x[2 * pair + 1, rows, lanes] = odd
-        power = jnp.sum(squares, axis=1, keepdims=True) * (1.0 / width)
-        row_scale[rows, :] = jnp.broadcast_to(lax.rsqrt(power + norm_eps), (BLOCK, HEAD_DIM))
-
+    for p in range(n_prompts):
+        ranks = slice(p * rank2, (p + 1) * rank2)
+        for q in range(quads):
+            lanes = slice(q * part, (q + 1) * part)
+            for pair in range(2):
+                first = total_rows + (q * 4 + pair) * rank2
+                second = first + 2 * rank2
+                one = received[prompt_slots[p], first : first + rank2, :]
+                two = received[prompt_slots[p], second : second + rank2, :]
+                even, odd = by_x(one.astype(jnp.float32), two.astype(jnp.float32))
+                down_x[2 * pair, ranks, lanes] = even
+                down_x[2 * pair + 1, ranks, lanes] = odd
+    power = jnp.sum(row_scale[...], axis=1, keepdims=True) * (1.0 / width)
+    row_scale[...] = jnp.broadcast_to(lax.rsqrt(power + norm_eps), (total_rows, HEAD_DIM))
     unscaled = jnp.zeros((total_rows, n_prompts * rank2), jnp.float32)
     for x in range(X_SIZE):
         unscaled = unscaled + lax.dot_general(
             gained_x[x], down_x[x], (((1,), (1,)), ((), ())), preferred_element_type=jnp.float32
         )
     lowrank = (unscaled * row_scale[...]).astype(jnp.bfloat16)
-    place = lax.broadcasted_iota(jnp.int32, (total_rows, n_prompts * rank2), 0)
-    segment = (
-        (place >= end_0).astype(jnp.int32)
-        + (place >= end_1).astype(jnp.int32)
-        + (place >= end_2).astype(jnp.int32)
-    )
-    lane = lax.broadcasted_iota(jnp.int32, (total_rows, n_prompts * rank2), 1)
-    in_prompt = (lane >= segment * rank2) & (lane < segment * rank2 + rank2)
-    picked = jnp.where(in_prompt, lowrank.astype(jnp.float32), 0.0).astype(jnp.bfloat16)
+    picked = (lowrank.astype(jnp.float32) * in_prompt[...]).astype(jnp.bfloat16)
     update = jnp.dot(picked, up_wide[...], preferred_element_type=jnp.float32)
-    bias_wide = bias[...].astype(jnp.float32)
     offset[:, 0:HEAD_DIM] = bias_wide[0:1] + adapter_scale * update[:, 0:HEAD_DIM]
-    offset[:, HEAD_DIM : 2 * HEAD_DIM] = jnp.broadcast_to(bias_wide[1:2], (total_rows, HEAD_DIM))
     offset[:, 2 * HEAD_DIM :] = bias_wide[2:3] + adapter_scale * update[:, HEAD_DIM:]
 
 
@@ -327,23 +302,27 @@
         n_prompts = prompt_length_list.shape[1]
         out_rows = total_rows // n_col
         payload_rows = total_rows + n_col * rank2 + GAIN_ROWS
-        payload = pl.pallas_call(
-            payload_kernel,
-            out_shape=jax.ShapeDtypeStruct((payload_rows, part), jnp.bfloat16),
-            name="payload",
-        )(incoming_hidden, input_norm_weight, adapter_down_weight.reshape(rank2, width))
+        payload, weight_copies = pl.pallas_call(
+            outgoing_kernel,
+            out_shape=(
+                jax.ShapeDtypeStruct((payload_rows, part), jnp.bfloat16),
+                jax.ShapeDtypeStruct((n_z, row_part, 4 * head_cols), jnp.bfloat16),
+            ),
+            name="outgoing",
+        )(
+            incoming_hidden,
+            input_norm_weight,
+            adapter_down_weight.reshape(rank2, width),
+            query_key_value_weight,
+            output_weight.T,
+        )
         gathered = lax.all_gather(payload, "col", axis=0, tiled=False)
-        weight_copies = pl.pallas_call(
-            weight_copies_kernel,
-            out_shape=jax.ShapeDtypeStruct((n_z, row_part, 4 * head_cols), jnp.bfloat16),
-            name="weight_copies",
-        )(query_key_value_weight, output_weight.T)
         over_z = lax.all_to_all(weight_copies, "row", 0, 0, tiled=False, axis_index_groups=z_groups)
         own_qkv = over_z[:, :, : 3 * head_cols]
         own_out = over_z[:, :, 3 * head_cols :]
         pieces, out_pieces = [over_z] * X_SIZE, [over_z] * X_SIZE
-        for k in (1, 3, 2):
-            if k == 1:
+        for k in (2, 1, 3):
+            if k == 2:
                 pieces[k] = out_pieces[k] = lax.ppermute(over_z, "row", x_shift(k))
             else:
                 pieces[k] = lax.ppermute(own_qkv, "row", x_shift(k))
@@ -367,14 +346,11 @@
             in_specs=[scalar] * 3 + [pl.BlockSpec(memory_space=HBM)] + [whole] * 4,
             out_specs=(whole,) * 5,
             scratch_shapes=[
-                pltpu.VMEM((n_col, total_rows, part), jnp.bfloat16),
-                pltpu.VMEM((n_col, GAIN_ROWS, part), jnp.bfloat16),
-                pltpu.VMEM((n_prompts, n_col * rank2, part), jnp.bfloat16),
+                pltpu.VMEM((n_col, payload_rows, part), jnp.bfloat16),
                 pltpu.VMEM((X_SIZE, n_prompts * rank2, width // X_SIZE), jnp.bfloat16),
                 pltpu.VMEM((n_prompts * rank2, 2 * head_cols), jnp.bfloat16),
-                pltpu.SemaphoreType.DMA((total_rows // BLOCK,)),
-                pltpu.SemaphoreType.DMA((1,)),
-                pltpu.SemaphoreType.DMA((n_prompts,)),
+                pltpu.VMEM((total_rows, n_prompts * rank2), jnp.float32),
+                pltpu.SemaphoreType.DMA((n_col // 4,)),
             ],
             compiler_params=pltpu.CompilerParams(vmem_limit_bytes=32 * 1024 * 1024),
             name="norm_and_adapters",

time: 119 us -> 116 us (0.975)
  Pallas kernels: 11.8 us -> 9.98 us
  blocking collectives: 67 us -> 65.4 us
  waiting for transfers between devices: 7.44 us -> 8.88 us
    ppermute x1, starting transfers between devices: 3.11 us -> 4.64 us  [body(): pieces[k] = out_pieces[k] = lax.ppermute(over_z, 'row', x_shift(k))]
    ppermute x2, starting transfers between devices: 6.82 us -> 5.28 us  [body(): pieces[k] = lax.ppermute(own_qkv, 'row', x_shift(k))]
    all_gather x1, waiting for transfers between devices: 7.41 us -> 8.85 us  [body(): gathered = lax.all_gather(payload, 'col', axis=0, tiled=False)]
    pallas_call x2 -> x1, Pallas kernels: 3.51 us -> 2.07 us  [body(): pl.pallas_call(outgoing_kernel, out_shape=(jax.ShapeDtypeStruct((payload_...]
    all_to_all x1, blocking collectives: 34.6 us -> 33.2 us  [body(): lax.all_to_all(pair_sum, 'col', 0, 0, tiled=False, axis_index_groups=y_gr...]
  transfers between devices with their start and end apart: 6 -> 6, of which waited for: 1 -> 1; matrix products, arithmetic and copies ran while one was open for 0% -> 0% of each run, Pallas kernels for 8% -> 6%
where the time goes in v4:
time: 116 us
  blocking collectives  65.4 us (56%)
  starting transfers between devices  15.9 us (14%)
  between operations  14.2 us (12%)
  Pallas kernels  9.98 us (9%)
  waiting for transfers between devices  8.88 us (8%)
  other arithmetic  1.21 us (1%)
    all_to_all x1, blocking collectives, body(): lax.all_to_all(pair_sum, 'col', 0, 0, tiled=False, axis_index_groups=y_gr...  33.2 us
    all_to_all x1, blocking collectives, body(): lax.all_to_all(weight_copies, 'row', 0, 0, tiled=False, axis_index_groups...  26.9 us
    all_gather x1, waiting for transfers between devices, body(): gathered = lax.all_gather(payload, 'col', axis=0, tiled=False)  8.85 us
    ppermute x2, starting transfers between devices, body(): out_pieces[k] = lax.ppermute(own_out, 'row', x_shift(k))  5.9 us
    all_to_all x1, blocking collectives, body(): lax.all_to_all(partial, 'col', 0, 0, tiled=False, axis_index_groups=pair_...  5.31 us
    ppermute x2, starting transfers between devices, body(): pieces[k] = lax.ppermute(own_qkv, 'row', x_shift(k))  5.28 us
    ppermute x1, starting transfers between devices, body(): pieces[k] = out_pieces[k] = lax.ppermute(over_z, 'row', x_shift(k))  4.64 us
    pallas_call x1, Pallas kernels, body(): pl.pallas_call(norm_kernel, out_shape=(jax.ShapeDtypeStruct((X_SIZE, tota...  3.88 us
  transfers between devices with their start and end apart: 6, of which 1 were waited for; matrix products, arithmetic and copies ran while one was open for 0% of the time, Pallas kernels for 6%

profile of v4, /device:TPU:1, one launch (start us, length us, event | category | flops | bytes accessed | tf_op | source)
XLA Modules:
  0.0 115.7 jit_solution(4496859317240976029)
XLA Ops:
  7.2 0.0 copy-start
  7.2 0.0 copy-start.1
  7.2 0.0 all-gather.3.cloned.1.call-start
  7.3 2.1 %outgoing.1 = (bf16[1040,128]{1,0:T(8,128)(2,1)}, bf16[8,64,512]{2,1,0:T(8,128)(2,1)}) custom-call(bf16[512,128]{1,0:T(8,128)(2,1)} %hidden.1, bf16[1,128]{1,0:T(2,128)(2,1)} %gain.1, bf16[32,2048]{1,0:T(8,128)(2,1)} %bitcast.7, bf16[3,64,128]{2,1,0:T(8,128)(2,1)} %qkv.1, bf16[64,128]{1,0:T(8,128)(2,1)} %bitcast.8), custom_call_target="tpu_custom_call" | custom-call | tf_op jit(solution)/shard_map/outgoing/pallas_call | solution.py:305
  9.4 0.0 all-gather.3.cloned.1.call-update
  9.4 26.9 %all_to_all.15.piece_0 = bf16[8,64,512]{2,1,0:T(8,128)(2,1)S(1)} all-to-all(bf16[8,64,512]{2,1,0:T(8,128)(2,1)} %get-tuple-element.11), channel_id=1, replica_groups={{0,64,128,192,256,320,384,448},{16,80,144,208,272,336,400,464},{32,96,1..., dimensions={0} | all-to-all | bytes 1048576 | tf_op jit(solution)/shard_map/all_to_all | solution.py:320
  36.3 4.6 %collective-permute-start.1 = (bf16[8,64,512]{2,1,0:T(8,128)(2,1)S(1)}, bf16[8,64,512]{2,1,0:T(8,128)(2,1)S(1)}, u32[]{:S(2)}, u32[]{:S(2)}) collective-permute-start(bf16[8,64,512]{2,1,0:T(8,128)(2,1)S(1)} %all_to_all.15.piece_0), channel_id=1, source_target_pairs={{0,32},{16,48},{32,0},{48,16},{64,96},{80,112},{96,64},{112,80},{1... | collective-permute-start | bytes 1572872 | tf_op jit(solution)/shard_map/ppermute | solution.py:326
  41.0 2.8 %collective-permute-start.4 = (bf16[8,64,384]{2,1,0:T(8,128)(2,1)S(1)}, bf16[8,64,384]{2,1,0:T(8,128)(2,1)S(1)}, u32[]{:S(2)}, u32[]{:S(2)}) collective-permute-start(bf16[8,64,384]{2,1,0:T(8,128)(2,1)S(1)} %slice.17), channel_id=1, source_target_pairs={{0,48},{16,0},{32,16},{48,32},{64,112},{80,64},{96,80},{112,96},{1... | collective-permute-start | bytes 1179656 | tf_op jit(solution)/shard_map/ppermute | solution.py:328
  43.7 2.5 %collective-permute-start.3 = (bf16[8,64,384]{2,1,0:T(8,128)(2,1)S(1)}, bf16[8,64,384]{2,1,0:T(8,128)(2,1)S(1)}, u32[]{:S(2)}, u32[]{:S(2)}) collective-permute-start(bf16[8,64,384]{2,1,0:T(8,128)(2,1)S(1)} %slice.17), channel_id=1, source_target_pairs={{0,16},{16,32},{32,48},{48,0},{64,80},{80,96},{96,112},{112,64},{1... | collective-permute-start | bytes 1179656 | tf_op jit(solution)/shard_map/ppermute | solution.py:328
  46.3 4.0 %collective-permute-start.2 = (bf16[8,64,128]{2,1,0:T(8,128)(2,1)S(1)}, bf16[8,64,128]{2,1,0:T(8,128)(2,1)S(1)}, u32[]{:S(2)}, u32[]{:S(2)}) collective-permute-start(bf16[8,64,128]{2,1,0:T(8,128)(2,1)S(1)} %slice.16), channel_id=1, source_target_pairs={{0,48},{16,0},{32,16},{48,32},{64,112},{80,64},{96,80},{112,96},{1... | collective-permute-start | bytes 393224 | tf_op jit(solution)/shard_map/ppermute | solution.py:329
  50.3 1.9 %collective-permute-start = (bf16[8,64,128]{2,1,0:T(8,128)(2,1)S(1)}, bf16[8,64,128]{2,1,0:T(8,128)(2,1)S(1)}, u32[]{:S(2)}, u32[]{:S(2)}) collective-permute-start(bf16[8,64,128]{2,1,0:T(8,128)(2,1)S(1)} %slice.16), channel_id=1, source_target_pairs={{0,16},{16,32},{32,48},{48,0},{64,80},{80,96},{96,112},{112,64},{1... | collective-permute-start | bytes 393224 | tf_op jit(solution)/shard_map/ppermute | solution.py:329
  52.2 8.8 %all-gather.3.cloned.1.call-done = bf16[16640,128]{1,0:T(8,128)(2,1)} async-done(((bf16[1040,128]{1,0:T(8,128)(2,1)}), bf16[16640,128]{1,0:T(8,128)(2,1)}) %all-gather.3.cloned.1.call-update) | async-done | bytes 4259856 | tf_op jit(solution)/shard_map/all_gather | solution.py:319
  61.1 0.0 copy-start.7
  61.1 3.9 %norm_and_adapters.1 = (bf16[4,512,512]{2,1,0:T(8,128)(2,1)S(1)}, f32[512,128]{1,0:T(8,128)S(1)}, f32[512,384]{1,0:T(8,128)S(1)}, f32[512,128]{1,0:T(8,128)S(1)}, f32[512,128]{1,0:T(8,128)S(1)}) custom-call(s32[16]{0:T(128)S(1)} %copy-done.5, s32[1,4]{1,0:T(1,128)S(1)} %copy-done.6, s32[1,4]{1,0:T(1,128)S(1)} %copy-done.3, bf16[16,1040,128]{2,1,0:T(8,128)(2,1)} %bitcast.6, ...), custom_call_target="tpu_custom_call" | custom-call | tf_op jit(solution)/shard_map/norm_and_adapters/pallas_call | solution.py:337
  65.0 0.0 collective-permute-done.4.piece_3
  65.0 0.0 collective-permute-done.3.piece_1
  65.0 0.0 collective-permute-done.1.piece_2
  65.0 3.2 %attention_block.1 = (bf16[512,128]{1,0:T(8,128)(2,1)S(1)}, bf16[32,2,16,128]{3,2,1,0:T(8,128)(2,1)}) custom-call(s32[1,4]{1,0:T(1,128)S(1)} %copy-done.3, s32[1,32]{1,0:T(1,128)S(1)} %copy-done.7, s32[1]{0:T(128)} %bitcast.x_place, bf16[8,64,512]{2,1,0:T(8,128)(2,1)S(1)} %all_to_all.15.piece_0, bf16[8,64,384]{2,1,0:T(8,128)(2,1)S(1)} %collective-permute-done.3.piece_1, ...), custom_call_target="tpu_custom_call" | custom-call | tf_op jit(solution)/shard_map/attention_block/pallas_call | solution.py:367
  68.2 0.0 collective-permute-done.2.piece_3
  68.2 0.9 output_projection.1
  69.1 5.3 %all_to_all.16 = bf16[2,8,32,2048]{3,2,1,0:T(8,128)(2,1)S(1)} all-to-all(bf16[2,8,32,2048]{3,2,1,0:T(8,128)(2,1)S(1)} %output_projection.1), channel_id=1, replica_groups={{0,1},{2,3},{4,5},{6,7},{8,9},{10,11},{12,13},{14,15},{16,17},{18,19},{..., dimensions={0} | all-to-all | bytes 4194304 | tf_op jit(solution)/shard_map/all_to_all | solution.py:404
  74.4 0.4 fusion
  74.8 33.2 %all_to_all.17 = bf16[8,32,2048]{2,1,0:T(8,128)(2,1)S(1)} all-to-all(bf16[8,32,2048]{2,1,0:T(8,128)(2,1)S(1)} %fusion), channel_id=1, replica_groups={{0,2,4,6,8,10,12,14},{1,3,5,7,9,11,13,15},{16,18,20,22,24,26,28,30},{17..., dimensions={0} | all-to-all | bytes 2097152 | tf_op jit(solution)/shard_map/all_to_all | solution.py:406
  108.0 0.8 reduce_sum.12
  (16 shorter events, 0.1 us)
Async XLA Ops:
  7.2 53.9 %copy-start = (f32[512,128]{1,0:T(8,128)S(1)}, f32[512,128]{1,0:T(8,128)}, u32[]{:S(2)}) copy-start(f32[512,128]{1,0:T(8,128)} %constant.19.clone.sine_part) | copy-start | bytes 786436
  7.2 53.9 %copy-start.1 = (f32[512,128]{1,0:T(8,128)S(1)}, f32[512,128]{1,0:T(8,128)}, u32[]{:S(2)}) copy-start(f32[512,128]{1,0:T(8,128)} %constant.18.clone.cosine) | copy-start | bytes 786436
  7.2 53.9 %copy-start.3 = (s32[1,4]{1,0:T(1,128)S(1)}, s32[1,4]{1,0:T(1,128)}, u32[]{:S(2)}) copy-start(s32[1,4]{1,0:T(1,128)} %lengths.3) | copy-start | bytes 52
  7.2 53.9 %copy-start.6 = (s32[1,4]{1,0:T(1,128)S(1)}, s32[1,4]{1,0:T(1,128)}, u32[]{:S(2)}) copy-start(s32[1,4]{1,0:T(1,128)} %adapters.1) | copy-start | bytes 52
  7.2 53.9 %copy-start.5 = (s32[16]{0:T(128)S(1)}, s32[16]{0:T(128)}, u32[]{:S(2)}) copy-start(s32[16]{0:T(128)} %slots.1) | copy-start | bytes 196
  7.2 53.9 %copy-start.2 = (bf16[16,2,16,128]{3,2,1,0:T(8,128)(2,1)S(1)}, bf16[16,2,16,128]{3,2,1,0:T(8,128)(2,1)}, u32[]{:S(2)}) copy-start(bf16[16,2,16,128]{3,2,1,0:T(8,128)(2,1)} %up.1) | copy-start | bytes 393220
  7.2 53.9 %copy-start.4 = (bf16[3,128]{1,0:T(4,128)(2,1)S(1)}, bf16[3,128]{1,0:T(4,128)(2,1)}, u32[]{:S(2)}) copy-start(bf16[3,128]{1,0:T(4,128)(2,1)} %bias.1) | copy-start | bytes 2308
  7.2 53.8 %all-gather.3.cloned.1.call-start = ((), (), s32[]{:S(2)}) async-start(), calls=%async_computation.3 | async-start | bytes 4526080 | tf_op jit(solution)/shard_map/all_gather | solution.py:319
  36.3 28.8 %collective-permute-start.1 = (bf16[8,64,512]{2,1,0:T(8,128)(2,1)S(1)}, bf16[8,64,512]{2,1,0:T(8,128)(2,1)S(1)}, u32[]{:S(2)}, u32[]{:S(2)}) collective-permute-start(bf16[8,64,512]{2,1,0:T(8,128)(2,1)S(1)} %all_to_all.15.piece_0), channel_id=1, source_target_pairs={{0,32},{16,48},{32,0},{48,16},{64,96},{80,112},{96,64},{112,80},{1... | collective-permute-start | bytes 1572872 | tf_op jit(solution)/shard_map/ppermute | solution.py:326
  41.0 24.0 %collective-permute-start.4 = (bf16[8,64,384]{2,1,0:T(8,128)(2,1)S(1)}, bf16[8,64,384]{2,1,0:T(8,128)(2,1)S(1)}, u32[]{:S(2)}, u32[]{:S(2)}) collective-permute-start(bf16[8,64,384]{2,1,0:T(8,128)(2,1)S(1)} %slice.17), channel_id=1, source_target_pairs={{0,48},{16,0},{32,16},{48,32},{64,112},{80,64},{96,80},{112,96},{1... | collective-permute-start | bytes 1179656 | tf_op jit(solution)/shard_map/ppermute | solution.py:328
  43.7 21.3 %collective-permute-start.3 = (bf16[8,64,384]{2,1,0:T(8,128)(2,1)S(1)}, bf16[8,64,384]{2,1,0:T(8,128)(2,1)S(1)}, u32[]{:S(2)}, u32[]{:S(2)}) collective-permute-start(bf16[8,64,384]{2,1,0:T(8,128)(2,1)S(1)} %slice.17), channel_id=1, source_target_pairs={{0,16},{16,32},{32,48},{48,0},{64,80},{80,96},{96,112},{112,64},{1... | collective-permute-start | bytes 1179656 | tf_op jit(solution)/shard_map/ppermute | solution.py:328
  46.3 21.9 %collective-permute-start.2 = (bf16[8,64,128]{2,1,0:T(8,128)(2,1)S(1)}, bf16[8,64,128]{2,1,0:T(8,128)(2,1)S(1)}, u32[]{:S(2)}, u32[]{:S(2)}) collective-permute-start(bf16[8,64,128]{2,1,0:T(8,128)(2,1)S(1)} %slice.16), channel_id=1, source_target_pairs={{0,48},{16,0},{32,16},{48,32},{64,112},{80,64},{96,80},{112,96},{1... | collective-permute-start | bytes 393224 | tf_op jit(solution)/shard_map/ppermute | solution.py:329
  50.3 17.9 %collective-permute-start = (bf16[8,64,128]{2,1,0:T(8,128)(2,1)S(1)}, bf16[8,64,128]{2,1,0:T(8,128)(2,1)S(1)}, u32[]{:S(2)}, u32[]{:S(2)}) collective-permute-start(bf16[8,64,128]{2,1,0:T(8,128)(2,1)S(1)} %slice.16), channel_id=1, source_target_pairs={{0,16},{16,32},{32,48},{48,0},{64,80},{80,96},{96,112},{112,64},{1... | collective-permute-start | bytes 393224 | tf_op jit(solution)/shard_map/ppermute | solution.py:329
  61.1 3.9 %copy-start.7 = (s32[1,32]{1,0:T(1,128)S(1)}, s32[1,32]{1,0:T(1,128)}, u32[]{:S(2)}) copy-start(s32[1,32]{1,0:T(1,128)} %pages.1) | copy-start | bytes 388
Sparse Core Ops, SparseCore 0:
  10.2 50.8 all-gather.2

commit v5 on v4

--- a/solution.py
+++ b/solution.py
@@ -12,6 +12,8 @@
 X_SIZE = 4
 LONGEST = 256
 BLOCK = 128
+QUERY_ROWS = 256
+LOG2_E = 1.4426950408889634
 
 rope_base = 1000000.0
 norm_eps = 1e-06
@@ -177,7 +179,7 @@
 ):
     total_rows = gained_x.shape[1]
     inner = gained_x.shape[2]
-    blocks = total_rows // BLOCK
+    blocks = total_rows // QUERY_ROWS
     me = x_place[0]
     unscaled = jnp.zeros(offset.shape, jnp.float32)
     for k, piece in enumerate((piece_0, piece_1, piece_2, piece_3)):
@@ -207,16 +209,16 @@
     end_0 = lengths[0, 0]
     end_1 = end_0 + lengths[0, 1]
     end_2 = end_1 + lengths[0, 2]
-    factor = HEAD_DIM ** (-0.5)
-    reach = LONGEST // BLOCK
+    factor = HEAD_DIM ** (-0.5) * LOG2_E
+    reach = LONGEST // QUERY_ROWS
     for i in range(blocks):
-        low = max(0, i - reach) * BLOCK
-        high = (i + 1) * BLOCK
-        query = queries[i * BLOCK : high, :]
+        low = max(0, i - reach) * QUERY_ROWS
+        high = (i + 1) * QUERY_ROWS
+        query = queries[i * QUERY_ROWS : high, :]
         scores = lax.dot_general(
             query, keys[low:high, :], (((1,), (1,)), ((), ())), preferred_element_type=jnp.float32
         )
-        query_place = i * BLOCK + lax.broadcasted_iota(jnp.int32, scores.shape, 0)
+        query_place = i * QUERY_ROWS + lax.broadcasted_iota(jnp.int32, scores.shape, 0)
         key_place = low + lax.broadcasted_iota(jnp.int32, scores.shape, 1)
         start = jnp.where(
             query_place >= end_2,
@@ -224,13 +226,14 @@
             jnp.where(query_place >= end_1, end_1, jnp.where(query_place >= end_0, end_0, 0)),
         )
         allowed = (key_place <= query_place) & (key_place >= start)
-        scores = jnp.where(allowed, scores * factor, -1e30)
+        scores = jnp.where(allowed, scores, -1e30)
         highest = jnp.max(scores, axis=1, keepdims=True)
-        exps = jnp.exp(scores - highest)
-        probs = (exps * (1.0 / jnp.sum(exps, axis=1, keepdims=True))).astype(jnp.bfloat16)
-        attended[i * BLOCK : high, :] = jnp.dot(
-            probs, values[low:high, :], preferred_element_type=jnp.float32
-        ).astype(jnp.bfloat16)
+        exps = jnp.exp2((scores - highest) * factor)
+        total = jnp.sum(exps, axis=1, keepdims=True)
+        mixed = jnp.dot(
+            exps.astype(jnp.bfloat16), values[low:high, :], preferred_element_type=jnp.float32
+        )
+        attended[i * QUERY_ROWS : high, :] = (mixed * (1.0 / total)).astype(jnp.bfloat16)
 
 
 def output_kernel(

time: 116 us -> 116 us (level)
  no operation moved by 1% of the time
where the time goes in v5:
time: 116 us; the launch traced here: 115 us
  blocking collectives  65.4 us (56%)
  starting transfers between devices  15.9 us (14%)
  between operations  14.2 us (12%)
  Pallas kernels  9.64 us (8%)
  waiting for transfers between devices  8.88 us (8%)
  other arithmetic  1.21 us (1%)
    all_to_all x1, blocking collectives, body(): lax.all_to_all(pair_sum, 'col', 0, 0, tiled=False, axis_index_groups=y_gr...  33.2 us
    all_to_all x1, blocking collectives, body(): lax.all_to_all(weight_copies, 'row', 0, 0, tiled=False, axis_index_groups...  26.9 us
    all_gather x1, waiting for transfers between devices, body(): gathered = lax.all_gather(payload, 'col', axis=0, tiled=False)  8.85 us
    ppermute x2, starting transfers between devices, body(): out_pieces[k] = lax.ppermute(own_out, 'row', x_shift(k))  5.9 us
    all_to_all x1, blocking collectives, body(): lax.all_to_all(partial, 'col', 0, 0, tiled=False, axis_index_groups=pair_...  5.3 us
    ppermute x2, starting transfers between devices, body(): pieces[k] = lax.ppermute(own_qkv, 'row', x_shift(k))  5.28 us
    ppermute x1, starting transfers between devices, body(): pieces[k] = out_pieces[k] = lax.ppermute(over_z, 'row', x_shift(k))  4.64 us
    pallas_call x1, Pallas kernels, body(): pl.pallas_call(norm_kernel, out_shape=(jax.ShapeDtypeStruct((X_SIZE, tota...  3.88 us
  transfers between devices with their start and end apart: 6, of which 1 were waited for; matrix products, arithmetic and copies ran while one was open for 0% of the time, Pallas kernels for 6%

profile of v5, /device:TPU:1, one launch (start us, length us, event | category | flops | bytes accessed | tf_op | source)
XLA Modules:
  0.0 115.3 jit_solution(12552768741763008898)
XLA Ops:
  7.2 0.0 copy-start
  7.2 0.0 copy-start.1
  7.2 0.0 all-gather.3.cloned.1.call-start
  7.3 2.1 %outgoing.1 = (bf16[1040,128]{1,0:T(8,128)(2,1)}, bf16[8,64,512]{2,1,0:T(8,128)(2,1)}) custom-call(bf16[512,128]{1,0:T(8,128)(2,1)} %hidden.1, bf16[1,128]{1,0:T(2,128)(2,1)} %gain.1, bf16[32,2048]{1,0:T(8,128)(2,1)} %bitcast.7, bf16[3,64,128]{2,1,0:T(8,128)(2,1)} %qkv.1, bf16[64,128]{1,0:T(8,128)(2,1)} %bitcast.8), custom_call_target="tpu_custom_call" | custom-call | tf_op jit(solution)/shard_map/outgoing/pallas_call | solution.py:308
  9.4 0.0 all-gather.3.cloned.1.call-update
  9.4 26.9 %all_to_all.15.piece_0 = bf16[8,64,512]{2,1,0:T(8,128)(2,1)S(1)} all-to-all(bf16[8,64,512]{2,1,0:T(8,128)(2,1)} %get-tuple-element.11), channel_id=1, replica_groups={{0,64,128,192,256,320,384,448},{16,80,144,208,272,336,400,464},{32,96,1..., dimensions={0} | all-to-all | bytes 1048576 | tf_op jit(solution)/shard_map/all_to_all | solution.py:323
  36.3 4.6 %collective-permute-start.1 = (bf16[8,64,512]{2,1,0:T(8,128)(2,1)S(1)}, bf16[8,64,512]{2,1,0:T(8,128)(2,1)S(1)}, u32[]{:S(2)}, u32[]{:S(2)}) collective-permute-start(bf16[8,64,512]{2,1,0:T(8,128)(2,1)S(1)} %all_to_all.15.piece_0), channel_id=1, source_target_pairs={{0,32},{16,48},{32,0},{48,16},{64,96},{80,112},{96,64},{112,80},{1... | collective-permute-start | bytes 1572872 | tf_op jit(solution)/shard_map/ppermute | solution.py:329
  41.0 2.8 %collective-permute-start.4 = (bf16[8,64,384]{2,1,0:T(8,128)(2,1)S(1)}, bf16[8,64,384]{2,1,0:T(8,128)(2,1)S(1)}, u32[]{:S(2)}, u32[]{:S(2)}) collective-permute-start(bf16[8,64,384]{2,1,0:T(8,128)(2,1)S(1)} %slice.17), channel_id=1, source_target_pairs={{0,48},{16,0},{32,16},{48,32},{64,112},{80,64},{96,80},{112,96},{1... | collective-permute-start | bytes 1179656 | tf_op jit(solution)/shard_map/ppermute | solution.py:331
  43.7 2.5 %collective-permute-start.3 = (bf16[8,64,384]{2,1,0:T(8,128)(2,1)S(1)}, bf16[8,64,384]{2,1,0:T(8,128)(2,1)S(1)}, u32[]{:S(2)}, u32[]{:S(2)}) collective-permute-start(bf16[8,64,384]{2,1,0:T(8,128)(2,1)S(1)} %slice.17), channel_id=1, source_target_pairs={{0,16},{16,32},{32,48},{48,0},{64,80},{80,96},{96,112},{112,64},{1... | collective-permute-start | bytes 1179656 | tf_op jit(solution)/shard_map/ppermute | solution.py:331
  46.3 4.0 %collective-permute-start.2 = (bf16[8,64,128]{2,1,0:T(8,128)(2,1)S(1)}, bf16[8,64,128]{2,1,0:T(8,128)(2,1)S(1)}, u32[]{:S(2)}, u32[]{:S(2)}) collective-permute-start(bf16[8,64,128]{2,1,0:T(8,128)(2,1)S(1)} %slice.16), channel_id=1, source_target_pairs={{0,48},{16,0},{32,16},{48,32},{64,112},{80,64},{96,80},{112,96},{1... | collective-permute-start | bytes 393224 | tf_op jit(solution)/shard_map/ppermute | solution.py:332
  50.3 1.9 %collective-permute-start = (bf16[8,64,128]{2,1,0:T(8,128)(2,1)S(1)}, bf16[8,64,128]{2,1,0:T(8,128)(2,1)S(1)}, u32[]{:S(2)}, u32[]{:S(2)}) collective-permute-start(bf16[8,64,128]{2,1,0:T(8,128)(2,1)S(1)} %slice.16), channel_id=1, source_target_pairs={{0,16},{16,32},{32,48},{48,0},{64,80},{80,96},{96,112},{112,64},{1... | collective-permute-start | bytes 393224 | tf_op jit(solution)/shard_map/ppermute | solution.py:332
  52.2 8.8 %all-gather.3.cloned.1.call-done = bf16[16640,128]{1,0:T(8,128)(2,1)} async-done(((bf16[1040,128]{1,0:T(8,128)(2,1)}), bf16[16640,128]{1,0:T(8,128)(2,1)}) %all-gather.3.cloned.1.call-update) | async-done | bytes 4259856 | tf_op jit(solution)/shard_map/all_gather | solution.py:322
  61.1 0.0 copy-start.7
  61.1 3.9 %norm_and_adapters.1 = (bf16[4,512,512]{2,1,0:T(8,128)(2,1)S(1)}, f32[512,128]{1,0:T(8,128)S(1)}, f32[512,384]{1,0:T(8,128)S(1)}, f32[512,128]{1,0:T(8,128)S(1)}, f32[512,128]{1,0:T(8,128)S(1)}) custom-call(s32[16]{0:T(128)S(1)} %copy-done.5, s32[1,4]{1,0:T(1,128)S(1)} %copy-done.6, s32[1,4]{1,0:T(1,128)S(1)} %copy-done.3, bf16[16,1040,128]{2,1,0:T(8,128)(2,1)} %bitcast.6, ...), custom_call_target="tpu_custom_call" | custom-call | tf_op jit(solution)/shard_map/norm_and_adapters/pallas_call | solution.py:340
  65.0 0.0 collective-permute-done.4.piece_3
  65.0 0.0 collective-permute-done.3.piece_1
  65.0 0.0 collective-permute-done.1.piece_2
  65.0 2.8 %attention_block.1 = (bf16[512,128]{1,0:T(8,128)(2,1)S(1)}, bf16[32,2,16,128]{3,2,1,0:T(8,128)(2,1)}) custom-call(s32[1,4]{1,0:T(1,128)S(1)} %copy-done.3, s32[1,32]{1,0:T(1,128)S(1)} %copy-done.7, s32[1]{0:T(128)} %bitcast.x_place, bf16[8,64,512]{2,1,0:T(8,128)(2,1)S(1)} %all_to_all.15.piece_0, bf16[8,64,384]{2,1,0:T(8,128)(2,1)S(1)} %collective-permute-done.3.piece_1, ...), custom_call_target="tpu_custom_call" | custom-call | tf_op jit(solution)/shard_map/attention_block/pallas_call | solution.py:370
  67.9 0.0 collective-permute-done.2.piece_3
  67.9 0.9 output_projection.1
  68.7 5.3 %all_to_all.16 = bf16[2,8,32,2048]{3,2,1,0:T(8,128)(2,1)S(1)} all-to-all(bf16[2,8,32,2048]{3,2,1,0:T(8,128)(2,1)S(1)} %output_projection.1), channel_id=1, replica_groups={{0,1},{2,3},{4,5},{6,7},{8,9},{10,11},{12,13},{14,15},{16,17},{18,19},{..., dimensions={0} | all-to-all | bytes 4194304 | tf_op jit(solution)/shard_map/all_to_all | solution.py:407
  74.0 0.4 fusion
  74.4 33.2 %all_to_all.17 = bf16[8,32,2048]{2,1,0:T(8,128)(2,1)S(1)} all-to-all(bf16[8,32,2048]{2,1,0:T(8,128)(2,1)S(1)} %fusion), channel_id=1, replica_groups={{0,2,4,6,8,10,12,14},{1,3,5,7,9,11,13,15},{16,18,20,22,24,26,28,30},{17..., dimensions={0} | all-to-all | bytes 2097152 | tf_op jit(solution)/shard_map/all_to_all | solution.py:409
  107.7 0.8 reduce_sum.12
  (16 shorter events, 0.1 us)
Async XLA Ops:
  7.2 53.9 %copy-start = (f32[512,128]{1,0:T(8,128)S(1)}, f32[512,128]{1,0:T(8,128)}, u32[]{:S(2)}) copy-start(f32[512,128]{1,0:T(8,128)} %constant.19.clone.sine_part) | copy-start | bytes 786436
  7.2 53.9 %copy-start.1 = (f32[512,128]{1,0:T(8,128)S(1)}, f32[512,128]{1,0:T(8,128)}, u32[]{:S(2)}) copy-start(f32[512,128]{1,0:T(8,128)} %constant.18.clone.cosine) | copy-start | bytes 786436
  7.2 53.9 %copy-start.3 = (s32[1,4]{1,0:T(1,128)S(1)}, s32[1,4]{1,0:T(1,128)}, u32[]{:S(2)}) copy-start(s32[1,4]{1,0:T(1,128)} %lengths.3) | copy-start | bytes 52
  7.2 53.9 %copy-start.6 = (s32[1,4]{1,0:T(1,128)S(1)}, s32[1,4]{1,0:T(1,128)}, u32[]{:S(2)}) copy-start(s32[1,4]{1,0:T(1,128)} %adapters.1) | copy-start | bytes 52
  7.2 53.9 %copy-start.5 = (s32[16]{0:T(128)S(1)}, s32[16]{0:T(128)}, u32[]{:S(2)}) copy-start(s32[16]{0:T(128)} %slots.1) | copy-start | bytes 196
  7.2 53.9 %copy-start.2 = (bf16[16,2,16,128]{3,2,1,0:T(8,128)(2,1)S(1)}, bf16[16,2,16,128]{3,2,1,0:T(8,128)(2,1)}, u32[]{:S(2)}) copy-start(bf16[16,2,16,128]{3,2,1,0:T(8,128)(2,1)} %up.1) | copy-start | bytes 393220
  7.2 53.9 %copy-start.4 = (bf16[3,128]{1,0:T(4,128)(2,1)S(1)}, bf16[3,128]{1,0:T(4,128)(2,1)}, u32[]{:S(2)}) copy-start(bf16[3,128]{1,0:T(4,128)(2,1)} %bias.1) | copy-start | bytes 2308
  7.2 53.8 %all-gather.3.cloned.1.call-start = ((), (), s32[]{:S(2)}) async-start(), calls=%async_computation.3 | async-start | bytes 4526080 | tf_op jit(solution)/shard_map/all_gather | solution.py:322
  36.3 28.8 %collective-permute-start.1 = (bf16[8,64,512]{2,1,0:T(8,128)(2,1)S(1)}, bf16[8,64,512]{2,1,0:T(8,128)(2,1)S(1)}, u32[]{:S(2)}, u32[]{:S(2)}) collective-permute-start(bf16[8,64,512]{2,1,0:T(8,128)(2,1)S(1)} %all_to_all.15.piece_0), channel_id=1, source_target_pairs={{0,32},{16,48},{32,0},{48,16},{64,96},{80,112},{96,64},{112,80},{1... | collective-permute-start | bytes 1572872 | tf_op jit(solution)/shard_map/ppermute | solution.py:329
  41.0 24.0 %collective-permute-start.4 = (bf16[8,64,384]{2,1,0:T(8,128)(2,1)S(1)}, bf16[8,64,384]{2,1,0:T(8,128)(2,1)S(1)}, u32[]{:S(2)}, u32[]{:S(2)}) collective-permute-start(bf16[8,64,384]{2,1,0:T(8,128)(2,1)S(1)} %slice.17), channel_id=1, source_target_pairs={{0,48},{16,0},{32,16},{48,32},{64,112},{80,64},{96,80},{112,96},{1... | collective-permute-start | bytes 1179656 | tf_op jit(solution)/shard_map/ppermute | solution.py:331
  43.7 21.3 %collective-permute-start.3 = (bf16[8,64,384]{2,1,0:T(8,128)(2,1)S(1)}, bf16[8,64,384]{2,1,0:T(8,128)(2,1)S(1)}, u32[]{:S(2)}, u32[]{:S(2)}) collective-permute-start(bf16[8,64,384]{2,1,0:T(8,128)(2,1)S(1)} %slice.17), channel_id=1, source_target_pairs={{0,16},{16,32},{32,48},{48,0},{64,80},{80,96},{96,112},{112,64},{1... | collective-permute-start | bytes 1179656 | tf_op jit(solution)/shard_map/ppermute | solution.py:331
  46.3 21.6 %collective-permute-start.2 = (bf16[8,64,128]{2,1,0:T(8,128)(2,1)S(1)}, bf16[8,64,128]{2,1,0:T(8,128)(2,1)S(1)}, u32[]{:S(2)}, u32[]{:S(2)}) collective-permute-start(bf16[8,64,128]{2,1,0:T(8,128)(2,1)S(1)} %slice.16), channel_id=1, source_target_pairs={{0,48},{16,0},{32,16},{48,32},{64,112},{80,64},{96,80},{112,96},{1... | collective-permute-start | bytes 393224 | tf_op jit(solution)/shard_map/ppermute | solution.py:332
  50.3 17.6 %collective-permute-start = (bf16[8,64,128]{2,1,0:T(8,128)(2,1)S(1)}, bf16[8,64,128]{2,1,0:T(8,128)(2,1)S(1)}, u32[]{:S(2)}, u32[]{:S(2)}) collective-permute-start(bf16[8,64,128]{2,1,0:T(8,128)(2,1)S(1)} %slice.16), channel_id=1, source_target_pairs={{0,16},{16,32},{32,48},{48,0},{64,80},{80,96},{96,112},{112,64},{1... | collective-permute-start | bytes 393224 | tf_op jit(solution)/shard_map/ppermute | solution.py:332
  61.1 3.9 %copy-start.7 = (s32[1,32]{1,0:T(1,128)S(1)}, s32[1,32]{1,0:T(1,128)}, u32[]{:S(2)}) copy-start(s32[1,32]{1,0:T(1,128)} %pages.1) | copy-start | bytes 388
Sparse Core Ops, SparseCore 0:
  10.2 50.8 all-gather.2

commit v6 on v5

--- a/solution.py
+++ b/solution.py
@@ -237,7 +237,7 @@
 
 
 def output_kernel(
-    x_place, piece_0, piece_1, piece_2, piece_3, attended, out, out_weights, sem
+    x_place, core, piece_0, piece_1, piece_2, piece_3, attended, keep, send, out_weights, sem
 ):
     me = x_place[0]
     copies = []
@@ -248,14 +248,26 @@
         copies[k].start()
     for k in range(X_SIZE):
         copies[k].wait()
-    width = out.shape[3]
+    width = keep.shape[2]
     weight_out = out_weights[...].reshape(width, HEAD_DIM)
     partial = lax.dot_general(
         attended[...], weight_out, (((1,), (1,)), ((), ())), preferred_element_type=jnp.float32
     ).astype(jnp.bfloat16)
-    out_rows = out.shape[2]
-    for b in range(2 * out.shape[1]):
-        out[b % 2, b // 2] = partial[b * out_rows : (b + 1) * out_rows, :]
+    out_rows = keep.shape[1]
+
+    def store(even, odd):
+        for y in range(keep.shape[0]):
+            first = 2 * y * out_rows
+            even[y] = partial[first : first + out_rows, :]
+            odd[y] = partial[first + out_rows : first + 2 * out_rows, :]
+
+    @pl.when(core[0] == 0)
+    def _():
+        store(keep, send)
+
+    @pl.when(core[0] == 1)
+    def _():
+        store(send, keep)
 
 
 def rotary_tables(rows):
@@ -274,7 +286,6 @@
 def make_body(n_row, n_col):
     n_z = n_row // X_SIZE
     z_groups = [[z * X_SIZE + x for z in range(n_z)] for x in range(X_SIZE)]
-    pair_groups = [[i, i + 1] for i in range(0, n_col, 2)]
     y_groups = [list(range(core, n_col, 2)) for core in range(2)]
 
     def x_shift(step):
@@ -392,20 +403,22 @@
             cos_all,
             sin_all,
         )
-        partial = pl.pallas_call(
+        core = lax.rem(lax.axis_index("col"), 2).astype(jnp.int32).reshape(1)
+        half_shape = jax.ShapeDtypeStruct((n_col // 2, out_rows, width), jnp.bfloat16)
+        keep, send = pl.pallas_call(
             output_kernel,
-            out_shape=jax.ShapeDtypeStruct((2, n_col // 2, out_rows, width), jnp.bfloat16),
-            in_specs=[scalar] + [raw] * X_SIZE + [whole],
-            out_specs=whole,
+            out_shape=(half_shape, half_shape),
+            in_specs=[scalar] * 2 + [raw] * X_SIZE + [whole],
+            out_specs=(whole, whole),
             scratch_shapes=[
                 pltpu.VMEM((n_z, X_SIZE, row_part, head_cols), jnp.bfloat16),
                 pltpu.SemaphoreType.DMA((X_SIZE,)),
             ],
             compiler_params=pltpu.CompilerParams(vmem_limit_bytes=32 * 1024 * 1024),
             name="output_projection",
-        )(x_place, *out_pieces, attended)
-        pair = lax.all_to_all(partial, "col", 0, 0, tiled=False, axis_index_groups=pair_groups)
-        pair_sum = (pair[0].astype(jnp.float32) + pair[1].astype(jnp.float32)).astype(jnp.bfloat16)
+        )(x_place, core, *out_pieces, attended)
+        received = lax.ppermute(send, "col", [(i, i ^ 1) for i in range(n_col)])
+        pair_sum = (keep.astype(jnp.float32) + received.astype(jnp.float32)).astype(jnp.bfloat16)
         terms = lax.all_to_all(pair_sum, "col", 0, 0, tiled=False, axis_index_groups=y_groups)
         summed = jnp.sum(terms.astype(jnp.float32), axis=0).astype(jnp.bfloat16)
         return (summed, cache)

time: 116 us -> 115 us (level)
  blocking collectives: 65.4 us -> 60 us
  waiting for transfers between devices: 8.88 us -> 11.2 us
  starting transfers between devices: 15.9 us -> 18 us
    all_to_all x1 -> x0, blocking collectives: 5.3 us -> none  [body(): lax.all_to_all(partial, 'col', 0, 0, tiled=False, axis_index_groups=pair_...]
    ppermute x0 -> x1, waiting for transfers between devices: none -> 2.38 us  [body(): received = lax.ppermute(send, 'col', [(i, i ^ 1) for i in range(n_col)])]
    ppermute x0 -> x1, starting transfers between devices: none -> 2.17 us  [body(): received = lax.ppermute(send, 'col', [(i, i ^ 1) for i in range(n_col)])]
  transfers between devices with their start and end apart: 6 -> 7, of which waited for: 1 -> 2; matrix products, arithmetic and copies ran while one was open for 0% -> 0% of each run, Pallas kernels for 6% -> 6%
where the time goes in v6:
time: 115 us
  blocking collectives  60 us (52%)
  starting transfers between devices  18 us (16%)
  between operations  14.2 us (12%)
  waiting for transfers between devices  11.2 us (10%)
  Pallas kernels  9.84 us (9%)
  other arithmetic  1.2 us (1%)
    all_to_all x1, blocking collectives, body(): lax.all_to_all(pair_sum, 'col', 0, 0, tiled=False, axis_index_groups=y_gr...  33.1 us
    all_to_all x1, blocking collectives, body(): lax.all_to_all(weight_copies, 'row', 0, 0, tiled=False, axis_index_groups...  26.9 us
    all_gather x1, waiting for transfers between devices, body(): gathered = lax.all_gather(payload, 'col', axis=0, tiled=False)  8.84 us
    ppermute x2, starting transfers between devices, body(): out_pieces[k] = lax.ppermute(own_out, 'row', x_shift(k))  5.9 us
    ppermute x2, starting transfers between devices, body(): pieces[k] = lax.ppermute(own_qkv, 'row', x_shift(k))  5.28 us
    ppermute x1, starting transfers between devices, body(): pieces[k] = out_pieces[k] = lax.ppermute(over_z, 'row', x_shift(k))  4.64 us
    pallas_call x1, Pallas kernels, body(): pl.pallas_call(norm_kernel, out_shape=(jax.ShapeDtypeStruct((X_SIZE, tota...  3.88 us
    pallas_call x1, Pallas kernels, body(): pl.pallas_call(block_kernel, out_shape=(jax.ShapeDtypeStruct((total_rows,...  2.84 us
  transfers between devices with their start and end apart: 7, of which 2 were waited for; matrix products, arithmetic and copies ran while one was open for 0% of the time, Pallas kernels for 6%

profile of v6, /device:TPU:1, one launch (start us, length us, event | category | flops | bytes accessed | tf_op | source)
XLA Modules:
  0.0 114.7 jit_solution(17283984356763123479)
XLA Ops:
  7.2 0.0 copy-start
  7.2 0.0 copy-start.1
  7.2 0.0 all-gather.3.cloned.1.call-start
  7.3 2.1 %outgoing.1 = (bf16[1040,128]{1,0:T(8,128)(2,1)}, bf16[8,64,512]{2,1,0:T(8,128)(2,1)}) custom-call(bf16[512,128]{1,0:T(8,128)(2,1)} %hidden.1, bf16[1,128]{1,0:T(2,128)(2,1)} %gain.1, bf16[32,2048]{1,0:T(8,128)(2,1)} %bitcast.6, bf16[3,64,128]{2,1,0:T(8,128)(2,1)} %qkv.1, bf16[64,128]{1,0:T(8,128)(2,1)} %bitcast.7), custom_call_target="tpu_custom_call" | custom-call | tf_op jit(solution)/shard_map/outgoing/pallas_call | solution.py:319
  9.4 0.0 all-gather.3.cloned.1.call-update
  9.4 26.9 %all_to_all.10.piece_0 = bf16[8,64,512]{2,1,0:T(8,128)(2,1)S(1)} all-to-all(bf16[8,64,512]{2,1,0:T(8,128)(2,1)} %get-tuple-element.13), channel_id=1, replica_groups={{0,64,128,192,256,320,384,448},{16,80,144,208,272,336,400,464},{32,96,1..., dimensions={0} | all-to-all | bytes 1048576 | tf_op jit(solution)/shard_map/all_to_all | solution.py:334
  36.3 4.6 %collective-permute-start.1 = (bf16[8,64,512]{2,1,0:T(8,128)(2,1)S(1)}, bf16[8,64,512]{2,1,0:T(8,128)(2,1)S(1)}, u32[]{:S(2)}, u32[]{:S(2)}) collective-permute-start(bf16[8,64,512]{2,1,0:T(8,128)(2,1)S(1)} %all_to_all.10.piece_0), channel_id=1, source_target_pairs={{0,32},{16,48},{32,0},{48,16},{64,96},{80,112},{96,64},{112,80},{1... | collective-permute-start | bytes 1572872 | tf_op jit(solution)/shard_map/ppermute | solution.py:340
  41.0 2.8 %collective-permute-start.4 = (bf16[8,64,384]{2,1,0:T(8,128)(2,1)S(1)}, bf16[8,64,384]{2,1,0:T(8,128)(2,1)S(1)}, u32[]{:S(2)}, u32[]{:S(2)}) collective-permute-start(bf16[8,64,384]{2,1,0:T(8,128)(2,1)S(1)} %slice.9), channel_id=1, source_target_pairs={{0,48},{16,0},{32,16},{48,32},{64,112},{80,64},{96,80},{112,96},{1... | collective-permute-start | bytes 1179656 | tf_op jit(solution)/shard_map/ppermute | solution.py:342
  43.7 2.5 %collective-permute-start.3 = (bf16[8,64,384]{2,1,0:T(8,128)(2,1)S(1)}, bf16[8,64,384]{2,1,0:T(8,128)(2,1)S(1)}, u32[]{:S(2)}, u32[]{:S(2)}) collective-permute-start(bf16[8,64,384]{2,1,0:T(8,128)(2,1)S(1)} %slice.9), channel_id=1, source_target_pairs={{0,16},{16,32},{32,48},{48,0},{64,80},{80,96},{96,112},{112,64},{1... | collective-permute-start | bytes 1179656 | tf_op jit(solution)/shard_map/ppermute | solution.py:342
  46.3 4.0 %collective-permute-start.2 = (bf16[8,64,128]{2,1,0:T(8,128)(2,1)S(1)}, bf16[8,64,128]{2,1,0:T(8,128)(2,1)S(1)}, u32[]{:S(2)}, u32[]{:S(2)}) collective-permute-start(bf16[8,64,128]{2,1,0:T(8,128)(2,1)S(1)} %slice.8), channel_id=1, source_target_pairs={{0,48},{16,0},{32,16},{48,32},{64,112},{80,64},{96,80},{112,96},{1... | collective-permute-start | bytes 393224 | tf_op jit(solution)/shard_map/ppermute | solution.py:343
  50.3 1.9 %collective-permute-start = (bf16[8,64,128]{2,1,0:T(8,128)(2,1)S(1)}, bf16[8,64,128]{2,1,0:T(8,128)(2,1)S(1)}, u32[]{:S(2)}, u32[]{:S(2)}) collective-permute-start(bf16[8,64,128]{2,1,0:T(8,128)(2,1)S(1)} %slice.8), channel_id=1, source_target_pairs={{0,16},{16,32},{32,48},{48,0},{64,80},{80,96},{96,112},{112,64},{1... | collective-permute-start | bytes 393224 | tf_op jit(solution)/shard_map/ppermute | solution.py:343
  52.2 8.8 %all-gather.3.cloned.1.call-done = bf16[16640,128]{1,0:T(8,128)(2,1)} async-done(((bf16[1040,128]{1,0:T(8,128)(2,1)}), bf16[16640,128]{1,0:T(8,128)(2,1)}) %all-gather.3.cloned.1.call-update) | async-done | bytes 4259856 | tf_op jit(solution)/shard_map/all_gather | solution.py:333
  61.1 0.0 copy-start.7
  61.1 3.9 %norm_and_adapters.1 = (bf16[4,512,512]{2,1,0:T(8,128)(2,1)S(1)}, f32[512,128]{1,0:T(8,128)S(1)}, f32[512,384]{1,0:T(8,128)S(1)}, f32[512,128]{1,0:T(8,128)S(1)}, f32[512,128]{1,0:T(8,128)S(1)}) custom-call(s32[16]{0:T(128)S(1)} %copy-done.5, s32[1,4]{1,0:T(1,128)S(1)} %copy-done.6, s32[1,4]{1,0:T(1,128)S(1)} %copy-done.3, bf16[16,1040,128]{2,1,0:T(8,128)(2,1)} %bitcast.5, ...), custom_call_target="tpu_custom_call" | custom-call | tf_op jit(solution)/shard_map/norm_and_adapters/pallas_call | solution.py:351
  65.0 0.0 collective-permute-done.4.piece_3
  65.0 0.0 collective-permute-done.3.piece_1
  65.0 0.0 collective-permute-done.1.piece_2
  65.0 2.8 %attention_block.1 = (bf16[512,128]{1,0:T(8,128)(2,1)S(1)}, bf16[32,2,16,128]{3,2,1,0:T(8,128)(2,1)}) custom-call(s32[1,4]{1,0:T(1,128)S(1)} %copy-done.3, s32[1,32]{1,0:T(1,128)S(1)} %copy-done.7, s32[1]{0:T(128)} %bitcast.x_place, bf16[8,64,512]{2,1,0:T(8,128)(2,1)S(1)} %all_to_all.10.piece_0, bf16[8,64,384]{2,1,0:T(8,128)(2,1)S(1)} %collective-permute-done.3.piece_1, ...), custom_call_target="tpu_custom_call" | custom-call | tf_op jit(solution)/shard_map/attention_block/pallas_call | solution.py:381
  67.9 1.0 output_projection.1
  68.9 2.2 %collective-permute-start.5 = (bf16[8,32,2048]{2,1,0:T(8,128)(2,1)S(1)}, bf16[8,32,2048]{2,1,0:T(8,128)(2,1)S(1)}, u32[]{:S(2)}, u32[]{:S(2)}) collective-permute-start(bf16[8,32,2048]{2,1,0:T(8,128)(2,1)S(1)} %get-tuple-element.22), channel_id=1, source_target_pairs={{0,1},{1,0},{2,3},{3,2},{4,5},{5,4},{6,7},{7,6},{8,9},{9,8},{10,11... | collective-permute-start | bytes 3145736 | tf_op jit(solution)/shard_map/ppermute | solution.py:420
  71.1 2.4 %collective-permute-done.5 = bf16[8,32,2048]{2,1,0:T(8,128)(2,1)S(1)} collective-permute-done((bf16[8,32,2048]{2,1,0:T(8,128)(2,1)S(1)}, bf16[8,32,2048]{2,1,0:T(8,128)(2,1)S(1)}, u32[]{:S(2)}, u32[]{:S(2)}) %collective-permute-start.5) | collective-permute-done | bytes 1048608 | tf_op jit(solution)/shard_map/ppermute | solution.py:420
  73.5 0.4 add_convert_fusion
  73.9 33.1 %all_to_all.11 = bf16[8,32,2048]{2,1,0:T(8,128)(2,1)S(1)} all-to-all(bf16[8,32,2048]{2,1,0:T(8,128)(2,1)S(1)} %add_convert_fusion), channel_id=1, replica_groups={{0,2,4,6,8,10,12,14},{1,3,5,7,9,11,13,15},{16,18,20,22,24,26,28,30},{17..., dimensions={0} | all-to-all | bytes 2097152 | tf_op jit(solution)/shard_map/all_to_all | solution.py:422
  107.0 0.8 reduce_sum.12
  (17 shorter events, 0.1 us)
Async XLA Ops:
  7.2 53.9 %copy-start = (f32[512,128]{1,0:T(8,128)S(1)}, f32[512,128]{1,0:T(8,128)}, u32[]{:S(2)}) copy-start(f32[512,128]{1,0:T(8,128)} %constant.26.clone.sine_part) | copy-start | bytes 786436
  7.2 53.9 %copy-start.1 = (f32[512,128]{1,0:T(8,128)S(1)}, f32[512,128]{1,0:T(8,128)}, u32[]{:S(2)}) copy-start(f32[512,128]{1,0:T(8,128)} %constant.25.clone.cosine) | copy-start | bytes 786436
  7.2 53.9 %copy-start.3 = (s32[1,4]{1,0:T(1,128)S(1)}, s32[1,4]{1,0:T(1,128)}, u32[]{:S(2)}) copy-start(s32[1,4]{1,0:T(1,128)} %lengths.3) | copy-start | bytes 52
  7.2 53.9 %copy-start.6 = (s32[1,4]{1,0:T(1,128)S(1)}, s32[1,4]{1,0:T(1,128)}, u32[]{:S(2)}) copy-start(s32[1,4]{1,0:T(1,128)} %adapters.1) | copy-start | bytes 52
  7.2 53.9 %copy-start.5 = (s32[16]{0:T(128)S(1)}, s32[16]{0:T(128)}, u32[]{:S(2)}) copy-start(s32[16]{0:T(128)} %slots.1) | copy-start | bytes 196
  7.2 53.9 %copy-start.2 = (bf16[16,2,16,128]{3,2,1,0:T(8,128)(2,1)S(1)}, bf16[16,2,16,128]{3,2,1,0:T(8,128)(2,1)}, u32[]{:S(2)}) copy-start(bf16[16,2,16,128]{3,2,1,0:T(8,128)(2,1)} %up.1) | copy-start | bytes 393220
  7.2 53.9 %copy-start.4 = (bf16[3,128]{1,0:T(4,128)(2,1)S(1)}, bf16[3,128]{1,0:T(4,128)(2,1)}, u32[]{:S(2)}) copy-start(bf16[3,128]{1,0:T(4,128)(2,1)} %bias.1) | copy-start | bytes 2308
  7.2 53.8 %all-gather.3.cloned.1.call-start = ((), (), s32[]{:S(2)}) async-start(), calls=%async_computation.2 | async-start | bytes 4526080 | tf_op jit(solution)/shard_map/all_gather | solution.py:333
  36.3 28.8 %collective-permute-start.1 = (bf16[8,64,512]{2,1,0:T(8,128)(2,1)S(1)}, bf16[8,64,512]{2,1,0:T(8,128)(2,1)S(1)}, u32[]{:S(2)}, u32[]{:S(2)}) collective-permute-start(bf16[8,64,512]{2,1,0:T(8,128)(2,1)S(1)} %all_to_all.10.piece_0), channel_id=1, source_target_pairs={{0,32},{16,48},{32,0},{48,16},{64,96},{80,112},{96,64},{112,80},{1... | collective-permute-start | bytes 1572872 | tf_op jit(solution)/shard_map/ppermute | solution.py:340
  41.0 24.0 %collective-permute-start.4 = (bf16[8,64,384]{2,1,0:T(8,128)(2,1)S(1)}, bf16[8,64,384]{2,1,0:T(8,128)(2,1)S(1)}, u32[]{:S(2)}, u32[]{:S(2)}) collective-permute-start(bf16[8,64,384]{2,1,0:T(8,128)(2,1)S(1)} %slice.9), channel_id=1, source_target_pairs={{0,48},{16,0},{32,16},{48,32},{64,112},{80,64},{96,80},{112,96},{1... | collective-permute-start | bytes 1179656 | tf_op jit(solution)/shard_map/ppermute | solution.py:342
  43.7 21.3 %collective-permute-start.3 = (bf16[8,64,384]{2,1,0:T(8,128)(2,1)S(1)}, bf16[8,64,384]{2,1,0:T(8,128)(2,1)S(1)}, u32[]{:S(2)}, u32[]{:S(2)}) collective-permute-start(bf16[8,64,384]{2,1,0:T(8,128)(2,1)S(1)} %slice.9), channel_id=1, source_target_pairs={{0,16},{16,32},{32,48},{48,0},{64,80},{80,96},{96,112},{112,64},{1... | collective-permute-start | bytes 1179656 | tf_op jit(solution)/shard_map/ppermute | solution.py:342
  46.3 21.6 %collective-permute-start.2 = (bf16[8,64,128]{2,1,0:T(8,128)(2,1)S(1)}, bf16[8,64,128]{2,1,0:T(8,128)(2,1)S(1)}, u32[]{:S(2)}, u32[]{:S(2)}) collective-permute-start(bf16[8,64,128]{2,1,0:T(8,128)(2,1)S(1)} %slice.8), channel_id=1, source_target_pairs={{0,48},{16,0},{32,16},{48,32},{64,112},{80,64},{96,80},{112,96},{1... | collective-permute-start | bytes 393224 | tf_op jit(solution)/shard_map/ppermute | solution.py:343
  50.3 17.6 %collective-permute-start = (bf16[8,64,128]{2,1,0:T(8,128)(2,1)S(1)}, bf16[8,64,128]{2,1,0:T(8,128)(2,1)S(1)}, u32[]{:S(2)}, u32[]{:S(2)}) collective-permute-start(bf16[8,64,128]{2,1,0:T(8,128)(2,1)S(1)} %slice.8), channel_id=1, source_target_pairs={{0,16},{16,32},{32,48},{48,0},{64,80},{80,96},{96,112},{112,64},{1... | collective-permute-start | bytes 393224 | tf_op jit(solution)/shard_map/ppermute | solution.py:343
  61.1 3.9 %copy-start.7 = (s32[1,32]{1,0:T(1,128)S(1)}, s32[1,32]{1,0:T(1,128)}, u32[]{:S(2)}) copy-start(s32[1,32]{1,0:T(1,128)} %pages.1) | copy-start | bytes 388
  68.9 4.6 %collective-permute-start.5 = (bf16[8,32,2048]{2,1,0:T(8,128)(2,1)S(1)}, bf16[8,32,2048]{2,1,0:T(8,128)(2,1)S(1)}, u32[]{:S(2)}, u32[]{:S(2)}) collective-permute-start(bf16[8,32,2048]{2,1,0:T(8,128)(2,1)S(1)} %get-tuple-element.22), channel_id=1, source_target_pairs={{0,1},{1,0},{2,3},{3,2},{4,5},{5,4},{6,7},{7,6},{8,9},{9,8},{10,11... | collective-permute-start | bytes 3145736 | tf_op jit(solution)/shard_map/ppermute | solution.py:420
Sparse Core Ops, SparseCore 0:
  10.2 50.8 all-gather.2

commit v7 on v5

--- a/solution.py
+++ b/solution.py
@@ -237,7 +237,7 @@
 
 
 def output_kernel(
-    x_place, piece_0, piece_1, piece_2, piece_3, attended, out, out_weights, sem
+    x_place, which, piece_0, piece_1, piece_2, piece_3, attended, out, out_weights, sem
 ):
     me = x_place[0]
     copies = []
@@ -248,14 +248,20 @@
         copies[k].start()
     for k in range(X_SIZE):
         copies[k].wait()
-    width = out.shape[3]
+    width = out.shape[2]
     weight_out = out_weights[...].reshape(width, HEAD_DIM)
+    out_rows = out.shape[1]
+    mine = jnp.concatenate(
+        [
+            attended[pl.ds(pl.multiple_of((2 * y + which[0]) * out_rows, out_rows), out_rows), :]
+            for y in range(out.shape[0])
+        ],
+        axis=0,
+    )
     partial = lax.dot_general(
-        attended[...], weight_out, (((1,), (1,)), ((), ())), preferred_element_type=jnp.float32
-    ).astype(jnp.bfloat16)
-    out_rows = out.shape[2]
-    for b in range(2 * out.shape[1]):
-        out[b % 2, b // 2] = partial[b * out_rows : (b + 1) * out_rows, :]
+        mine, weight_out, (((1,), (1,)), ((), ())), preferred_element_type=jnp.float32
+    )
+    out[...] = partial.astype(jnp.bfloat16).reshape(out.shape)
 
 
 def rotary_tables(rows):
@@ -274,7 +280,6 @@
 def make_body(n_row, n_col):
     n_z = n_row // X_SIZE
     z_groups = [[z * X_SIZE + x for z in range(n_z)] for x in range(X_SIZE)]
-    pair_groups = [[i, i + 1] for i in range(0, n_col, 2)]
     y_groups = [list(range(core, n_col, 2)) for core in range(2)]
 
     def x_shift(step):
@@ -392,10 +397,12 @@
             cos_all,
             sin_all,
         )
-        partial = pl.pallas_call(
+        core = lax.rem(lax.axis_index("col"), 2).astype(jnp.int32).reshape(1)
+        half_shape = jax.ShapeDtypeStruct((n_col // 2, out_rows, width), jnp.bfloat16)
+        project = pl.pallas_call(
             output_kernel,
-            out_shape=jax.ShapeDtypeStruct((2, n_col // 2, out_rows, width), jnp.bfloat16),
-            in_specs=[scalar] + [raw] * X_SIZE + [whole],
+            out_shape=half_shape,
+            in_specs=[scalar] * 2 + [raw] * X_SIZE + [whole],
             out_specs=whole,
             scratch_shapes=[
                 pltpu.VMEM((n_z, X_SIZE, row_part, head_cols), jnp.bfloat16),
@@ -403,9 +410,11 @@
             ],
             compiler_params=pltpu.CompilerParams(vmem_limit_bytes=32 * 1024 * 1024),
             name="output_projection",
-        )(x_place, *out_pieces, attended)
-        pair = lax.all_to_all(partial, "col", 0, 0, tiled=False, axis_index_groups=pair_groups)
-        pair_sum = (pair[0].astype(jnp.float32) + pair[1].astype(jnp.float32)).astype(jnp.bfloat16)
+        )
+        send = project(x_place, 1 - core, *out_pieces, attended)
+        keep = project(x_place, core, *out_pieces, attended)
+        received = lax.ppermute(send, "col", [(i, i ^ 1) for i in range(n_col)])
+        pair_sum = (keep.astype(jnp.float32) + received.astype(jnp.float32)).astype(jnp.bfloat16)
         terms = lax.all_to_all(pair_sum, "col", 0, 0, tiled=False, axis_index_groups=y_groups)
         summed = jnp.sum(terms.astype(jnp.float32), axis=0).astype(jnp.bfloat16)
         return (summed, cache)

time: 116 us -> 115 us (level)
  blocking collectives: 65.4 us -> 60 us
  starting transfers between devices: 15.9 us -> 18 us
  waiting for transfers between devices: 8.88 us -> 10.7 us
    all_to_all x1 -> x0, blocking collectives: 5.3 us -> none  [body(): lax.all_to_all(partial, 'col', 0, 0, tiled=False, axis_index_groups=pair_...]
    ppermute x0 -> x1, starting transfers between devices: none -> 2.16 us  [body(): received = lax.ppermute(send, 'col', [(i, i ^ 1) for i in range(n_col)])]
    ppermute x0 -> x1, waiting for transfers between devices: none -> 1.79 us  [body(): received = lax.ppermute(send, 'col', [(i, i ^ 1) for i in range(n_col)])]
  transfers between devices with their start and end apart: 6 -> 7, of which waited for: 1 -> 2; matrix products, arithmetic and copies ran while one was open for 0% -> 0% of each run, Pallas kernels for 6% -> 6%
where the time goes in v7:
time: 115 us; the launch traced here: 114 us
  blocking collectives  60 us (52%)
  starting transfers between devices  18 us (16%)
  between operations  14.3 us (12%)
  waiting for transfers between devices  10.7 us (9%)
  Pallas kernels  9.96 us (9%)
  other arithmetic  1.22 us (1%)
    all_to_all x1, blocking collectives, body(): lax.all_to_all(pair_sum, 'col', 0, 0, tiled=False, axis_index_groups=y_gr...  33.1 us
    all_to_all x1, blocking collectives, body(): lax.all_to_all(weight_copies, 'row', 0, 0, tiled=False, axis_index_groups...  26.9 us
    all_gather x1, waiting for transfers between devices, body(): gathered = lax.all_gather(payload, 'col', axis=0, tiled=False)  8.84 us
    ppermute x2, starting transfers between devices, body(): out_pieces[k] = lax.ppermute(own_out, 'row', x_shift(k))  5.9 us
    ppermute x2, starting transfers between devices, body(): pieces[k] = lax.ppermute(own_qkv, 'row', x_shift(k))  5.28 us
    ppermute x1, starting transfers between devices, body(): pieces[k] = out_pieces[k] = lax.ppermute(over_z, 'row', x_shift(k))  4.64 us
    pallas_call x1, Pallas kernels, body(): pl.pallas_call(norm_kernel, out_shape=(jax.ShapeDtypeStruct((X_SIZE, tota...  3.88 us
    pallas_call x1, Pallas kernels, body(): pl.pallas_call(block_kernel, out_shape=(jax.ShapeDtypeStruct((total_rows,...  2.83 us
  transfers between devices with their start and end apart: 7, of which 2 were waited for; matrix products, arithmetic and copies ran while one was open for 0% of the time, Pallas kernels for 6%

profile of v7, /device:TPU:1, one launch (start us, length us, event | category | flops | bytes accessed | tf_op | source)
XLA Modules:
  0.0 114.2 jit_solution(12471103218611822397)
XLA Ops:
  7.2 0.0 copy-start
  7.2 0.0 copy-start.1
  7.2 0.0 all-gather.3.cloned.1.call-start
  7.3 2.1 %outgoing.1 = (bf16[1040,128]{1,0:T(8,128)(2,1)}, bf16[8,64,512]{2,1,0:T(8,128)(2,1)}) custom-call(bf16[512,128]{1,0:T(8,128)(2,1)} %hidden.1, bf16[1,128]{1,0:T(2,128)(2,1)} %gain.1, bf16[32,2048]{1,0:T(8,128)(2,1)} %bitcast.6, bf16[3,64,128]{2,1,0:T(8,128)(2,1)} %qkv.1, bf16[64,128]{1,0:T(8,128)(2,1)} %bitcast.7), custom_call_target="tpu_custom_call" | custom-call | tf_op jit(solution)/shard_map/outgoing/pallas_call | solution.py:313
  9.4 0.0 all-gather.3.cloned.1.call-update
  9.4 26.9 %all_to_all.10.piece_0 = bf16[8,64,512]{2,1,0:T(8,128)(2,1)S(1)} all-to-all(bf16[8,64,512]{2,1,0:T(8,128)(2,1)} %get-tuple-element.11), channel_id=1, replica_groups={{0,64,128,192,256,320,384,448},{16,80,144,208,272,336,400,464},{32,96,1..., dimensions={0} | all-to-all | bytes 1048576 | tf_op jit(solution)/shard_map/all_to_all | solution.py:328
  36.3 4.6 %collective-permute-start.1 = (bf16[8,64,512]{2,1,0:T(8,128)(2,1)S(1)}, bf16[8,64,512]{2,1,0:T(8,128)(2,1)S(1)}, u32[]{:S(2)}, u32[]{:S(2)}) collective-permute-start(bf16[8,64,512]{2,1,0:T(8,128)(2,1)S(1)} %all_to_all.10.piece_0), channel_id=1, source_target_pairs={{0,32},{16,48},{32,0},{48,16},{64,96},{80,112},{96,64},{112,80},{1... | collective-permute-start | bytes 1572872 | tf_op jit(solution)/shard_map/ppermute | solution.py:334
  41.0 2.8 %collective-permute-start.4 = (bf16[8,64,384]{2,1,0:T(8,128)(2,1)S(1)}, bf16[8,64,384]{2,1,0:T(8,128)(2,1)S(1)}, u32[]{:S(2)}, u32[]{:S(2)}) collective-permute-start(bf16[8,64,384]{2,1,0:T(8,128)(2,1)S(1)} %slice.9), channel_id=1, source_target_pairs={{0,48},{16,0},{32,16},{48,32},{64,112},{80,64},{96,80},{112,96},{1... | collective-permute-start | bytes 1179656 | tf_op jit(solution)/shard_map/ppermute | solution.py:336
  43.7 2.5 %collective-permute-start.3 = (bf16[8,64,384]{2,1,0:T(8,128)(2,1)S(1)}, bf16[8,64,384]{2,1,0:T(8,128)(2,1)S(1)}, u32[]{:S(2)}, u32[]{:S(2)}) collective-permute-start(bf16[8,64,384]{2,1,0:T(8,128)(2,1)S(1)} %slice.9), channel_id=1, source_target_pairs={{0,16},{16,32},{32,48},{48,0},{64,80},{80,96},{96,112},{112,64},{1... | collective-permute-start | bytes 1179656 | tf_op jit(solution)/shard_map/ppermute | solution.py:336
  46.3 4.0 %collective-permute-start.2 = (bf16[8,64,128]{2,1,0:T(8,128)(2,1)S(1)}, bf16[8,64,128]{2,1,0:T(8,128)(2,1)S(1)}, u32[]{:S(2)}, u32[]{:S(2)}) collective-permute-start(bf16[8,64,128]{2,1,0:T(8,128)(2,1)S(1)} %slice.8), channel_id=1, source_target_pairs={{0,48},{16,0},{32,16},{48,32},{64,112},{80,64},{96,80},{112,96},{1... | collective-permute-start | bytes 393224 | tf_op jit(solution)/shard_map/ppermute | solution.py:337
  50.3 1.9 %collective-permute-start = (bf16[8,64,128]{2,1,0:T(8,128)(2,1)S(1)}, bf16[8,64,128]{2,1,0:T(8,128)(2,1)S(1)}, u32[]{:S(2)}, u32[]{:S(2)}) collective-permute-start(bf16[8,64,128]{2,1,0:T(8,128)(2,1)S(1)} %slice.8), channel_id=1, source_target_pairs={{0,16},{16,32},{32,48},{48,0},{64,80},{80,96},{96,112},{112,64},{1... | collective-permute-start | bytes 393224 | tf_op jit(solution)/shard_map/ppermute | solution.py:337
  52.2 8.8 %all-gather.3.cloned.1.call-done = bf16[16640,128]{1,0:T(8,128)(2,1)} async-done(((bf16[1040,128]{1,0:T(8,128)(2,1)}), bf16[16640,128]{1,0:T(8,128)(2,1)}) %all-gather.3.cloned.1.call-update) | async-done | bytes 4259856 | tf_op jit(solution)/shard_map/all_gather | solution.py:327
  61.1 0.0 copy-start.7
  61.1 3.9 %norm_and_adapters.1 = (bf16[4,512,512]{2,1,0:T(8,128)(2,1)S(1)}, f32[512,128]{1,0:T(8,128)S(1)}, f32[512,384]{1,0:T(8,128)S(1)}, f32[512,128]{1,0:T(8,128)S(1)}, f32[512,128]{1,0:T(8,128)S(1)}) custom-call(s32[16]{0:T(128)S(1)} %copy-done.5, s32[1,4]{1,0:T(1,128)S(1)} %copy-done.6, s32[1,4]{1,0:T(1,128)S(1)} %copy-done.3, bf16[16,1040,128]{2,1,0:T(8,128)(2,1)} %bitcast.5, ...), custom_call_target="tpu_custom_call" | custom-call | tf_op jit(solution)/shard_map/norm_and_adapters/pallas_call | solution.py:345
  65.0 0.0 collective-permute-done.4.piece_3
  65.0 0.0 collective-permute-done.1.piece_2
  65.0 2.8 %attention_block.1 = (bf16[512,128]{1,0:T(8,128)(2,1)S(1)}, bf16[32,2,16,128]{3,2,1,0:T(8,128)(2,1)}) custom-call(s32[1,4]{1,0:T(1,128)S(1)} %copy-done.3, s32[1,32]{1,0:T(1,128)S(1)} %copy-done.7, s32[1]{0:T(128)} %bitcast.x_place, bf16[8,64,512]{2,1,0:T(8,128)(2,1)S(1)} %all_to_all.10.piece_0, bf16[8,64,384]{2,1,0:T(8,128)(2,1)S(1)} %collective-permute-done.3.piece_1, ...), custom_call_target="tpu_custom_call" | custom-call | tf_op jit(solution)/shard_map/attention_block/pallas_call | solution.py:375
  67.9 0.6 output_projection.3
  68.5 2.2 %collective-permute-start.5 = (bf16[8,32,2048]{2,1,0:T(8,128)(2,1)S(1)}, bf16[8,32,2048]{2,1,0:T(8,128)(2,1)S(1)}, u32[]{:S(2)}, u32[]{:S(2)}) collective-permute-start(bf16[8,32,2048]{2,1,0:T(8,128)(2,1)S(1)} %output_projection.3), channel_id=1, source_target_pairs={{0,1},{1,0},{2,3},{3,2},{4,5},{5,4},{6,7},{7,6},{8,9},{9,8},{10,11... | collective-permute-start | bytes 3145736 | tf_op jit(solution)/shard_map/ppermute | solution.py:416
  70.6 0.6 output_projection.2
  71.2 1.8 %collective-permute-done.5 = bf16[8,32,2048]{2,1,0:T(8,128)(2,1)S(1)} collective-permute-done((bf16[8,32,2048]{2,1,0:T(8,128)(2,1)S(1)}, bf16[8,32,2048]{2,1,0:T(8,128)(2,1)S(1)}, u32[]{:S(2)}, u32[]{:S(2)}) %collective-permute-start.5) | collective-permute-done | bytes 1048608 | tf_op jit(solution)/shard_map/ppermute | solution.py:416
  73.0 0.4 add_convert_fusion
  73.4 33.1 %all_to_all.11 = bf16[8,32,2048]{2,1,0:T(8,128)(2,1)S(1)} all-to-all(bf16[8,32,2048]{2,1,0:T(8,128)(2,1)S(1)} %add_convert_fusion), channel_id=1, replica_groups={{0,2,4,6,8,10,12,14},{1,3,5,7,9,11,13,15},{16,18,20,22,24,26,28,30},{17..., dimensions={0} | all-to-all | bytes 2097152 | tf_op jit(solution)/shard_map/all_to_all | solution.py:418
  106.5 0.8 reduce_sum.12
  (18 shorter events, 0.1 us)
Async XLA Ops:
  7.2 53.9 %copy-start = (f32[512,128]{1,0:T(8,128)S(1)}, f32[512,128]{1,0:T(8,128)}, u32[]{:S(2)}) copy-start(f32[512,128]{1,0:T(8,128)} %constant.28.clone.sine_part) | copy-start | bytes 786436
  7.2 53.9 %copy-start.1 = (f32[512,128]{1,0:T(8,128)S(1)}, f32[512,128]{1,0:T(8,128)}, u32[]{:S(2)}) copy-start(f32[512,128]{1,0:T(8,128)} %constant.27.clone.cosine) | copy-start | bytes 786436
  7.2 53.9 %copy-start.3 = (s32[1,4]{1,0:T(1,128)S(1)}, s32[1,4]{1,0:T(1,128)}, u32[]{:S(2)}) copy-start(s32[1,4]{1,0:T(1,128)} %lengths.3) | copy-start | bytes 52
  7.2 53.9 %copy-start.6 = (s32[1,4]{1,0:T(1,128)S(1)}, s32[1,4]{1,0:T(1,128)}, u32[]{:S(2)}) copy-start(s32[1,4]{1,0:T(1,128)} %adapters.1) | copy-start | bytes 52
  7.2 53.9 %copy-start.5 = (s32[16]{0:T(128)S(1)}, s32[16]{0:T(128)}, u32[]{:S(2)}) copy-start(s32[16]{0:T(128)} %slots.1) | copy-start | bytes 196
  7.2 53.9 %copy-start.2 = (bf16[16,2,16,128]{3,2,1,0:T(8,128)(2,1)S(1)}, bf16[16,2,16,128]{3,2,1,0:T(8,128)(2,1)}, u32[]{:S(2)}) copy-start(bf16[16,2,16,128]{3,2,1,0:T(8,128)(2,1)} %up.1) | copy-start | bytes 393220
  7.2 53.9 %copy-start.4 = (bf16[3,128]{1,0:T(4,128)(2,1)S(1)}, bf16[3,128]{1,0:T(4,128)(2,1)}, u32[]{:S(2)}) copy-start(bf16[3,128]{1,0:T(4,128)(2,1)} %bias.1) | copy-start | bytes 2308
  7.2 53.8 %all-gather.3.cloned.1.call-start = ((), (), s32[]{:S(2)}) async-start(), calls=%async_computation.2 | async-start | bytes 4526080 | tf_op jit(solution)/shard_map/all_gather | solution.py:327
  36.3 28.8 %collective-permute-start.1 = (bf16[8,64,512]{2,1,0:T(8,128)(2,1)S(1)}, bf16[8,64,512]{2,1,0:T(8,128)(2,1)S(1)}, u32[]{:S(2)}, u32[]{:S(2)}) collective-permute-start(bf16[8,64,512]{2,1,0:T(8,128)(2,1)S(1)} %all_to_all.10.piece_0), channel_id=1, source_target_pairs={{0,32},{16,48},{32,0},{48,16},{64,96},{80,112},{96,64},{112,80},{1... | collective-permute-start | bytes 1572872 | tf_op jit(solution)/shard_map/ppermute | solution.py:334
  41.0 24.0 %collective-permute-start.4 = (bf16[8,64,384]{2,1,0:T(8,128)(2,1)S(1)}, bf16[8,64,384]{2,1,0:T(8,128)(2,1)S(1)}, u32[]{:S(2)}, u32[]{:S(2)}) collective-permute-start(bf16[8,64,384]{2,1,0:T(8,128)(2,1)S(1)} %slice.9), channel_id=1, source_target_pairs={{0,48},{16,0},{32,16},{48,32},{64,112},{80,64},{96,80},{112,96},{1... | collective-permute-start | bytes 1179656 | tf_op jit(solution)/shard_map/ppermute | solution.py:336
  43.7 21.3 %collective-permute-start.3 = (bf16[8,64,384]{2,1,0:T(8,128)(2,1)S(1)}, bf16[8,64,384]{2,1,0:T(8,128)(2,1)S(1)}, u32[]{:S(2)}, u32[]{:S(2)}) collective-permute-start(bf16[8,64,384]{2,1,0:T(8,128)(2,1)S(1)} %slice.9), channel_id=1, source_target_pairs={{0,16},{16,32},{32,48},{48,0},{64,80},{80,96},{96,112},{112,64},{1... | collective-permute-start | bytes 1179656 | tf_op jit(solution)/shard_map/ppermute | solution.py:336
  46.3 21.6 %collective-permute-start.2 = (bf16[8,64,128]{2,1,0:T(8,128)(2,1)S(1)}, bf16[8,64,128]{2,1,0:T(8,128)(2,1)S(1)}, u32[]{:S(2)}, u32[]{:S(2)}) collective-permute-start(bf16[8,64,128]{2,1,0:T(8,128)(2,1)S(1)} %slice.8), channel_id=1, source_target_pairs={{0,48},{16,0},{32,16},{48,32},{64,112},{80,64},{96,80},{112,96},{1... | collective-permute-start | bytes 393224 | tf_op jit(solution)/shard_map/ppermute | solution.py:337
  50.3 17.6 %collective-permute-start = (bf16[8,64,128]{2,1,0:T(8,128)(2,1)S(1)}, bf16[8,64,128]{2,1,0:T(8,128)(2,1)S(1)}, u32[]{:S(2)}, u32[]{:S(2)}) collective-permute-start(bf16[8,64,128]{2,1,0:T(8,128)(2,1)S(1)} %slice.8), channel_id=1, source_target_pairs={{0,16},{16,32},{32,48},{48,0},{64,80},{80,96},{96,112},{112,64},{1... | collective-permute-start | bytes 393224 | tf_op jit(solution)/shard_map/ppermute | solution.py:337
  61.1 3.9 %copy-start.7 = (s32[1,32]{1,0:T(1,128)S(1)}, s32[1,32]{1,0:T(1,128)}, u32[]{:S(2)}) copy-start(s32[1,32]{1,0:T(1,128)} %pages.1) | copy-start | bytes 388
  68.5 4.6 %collective-permute-start.5 = (bf16[8,32,2048]{2,1,0:T(8,128)(2,1)S(1)}, bf16[8,32,2048]{2,1,0:T(8,128)(2,1)S(1)}, u32[]{:S(2)}, u32[]{:S(2)}) collective-permute-start(bf16[8,32,2048]{2,1,0:T(8,128)(2,1)S(1)} %output_projection.3), channel_id=1, source_target_pairs={{0,1},{1,0},{2,3},{3,2},{4,5},{5,4},{6,7},{7,6},{8,9},{9,8},{10,11... | collective-permute-start | bytes 3145736 | tf_op jit(solution)/shard_map/ppermute | solution.py:416
Sparse Core Ops, SparseCore 0:
  10.2 50.8 all-gather.2
